TPU v7x, 32 devices: a whole 2x2x4 slice. The times are simulated.
32 devices in a mesh: dp: 8 (over z, core), row: 2 (over x), col: 2 (over y).
Axes of the slice: x: 2, y: 2, z: 4, core: 2. Of those that a mesh axis runs over, the one named last changes fastest.
Arguments:
- tokens: float32 [24, 112, 28, 512], P('dp', 'row', 'col'), may hold values from -6 to 6
- position_index: int32 [49, 49], replicated, may hold values from 0 to 168, as said below
- first_gain: float32 [512], P('dp'), may hold values from 0.5 to 1.5
- first_shift: float32 [512], P('dp'), may hold values from -3 to 3
- joint_weight: float32 [512, 1536], P('dp'), may hold values from -0.25 to 0.25
- query_bias: float32 [512], P('dp'), may hold values from -3 to 3
- value_bias: float32 [512], P('dp'), may hold values from -3 to 3
- position_table: float32 [16, 169], P('dp'), may hold values from -4 to 4
- output_weight: float32 [512, 512], P('dp'), may hold values from -1 to 1
- output_bias: float32 [512], P('dp'), may hold values from -3 to 3
- second_gain: float32 [512], P('dp'), may hold values from 0.5 to 1.5
- second_shift: float32 [512], P('dp'), may hold values from -3 to 3
- expand_weight: float32 [512, 2048], P('dp'), may hold values from -0.25 to 0.25
- expand_bias: float32 [2048], P('dp'), may hold values from -3 to 3
- shrink_weight: float32 [2048, 512], P('dp'), may hold values from -0.25 to 0.25
- shrink_bias: float32 [512], P('dp'), may hold values from -3 to 3
- cotangent: float32 [24, 112, 28, 512], P('dp', 'row', 'col'), may hold values from -6 to 6
Outputs:
- result: float32 [24, 112, 28, 512], P('dp', 'row', 'col')
- grad_tokens: float32 [24, 112, 28, 512], P('dp', 'row', 'col')
- grad_first_gain: float32 [512], P('dp')
- grad_first_shift: float32 [512], P('dp')
- grad_joint_weight: float32 [512, 1536], P('dp')
- grad_query_bias: float32 [512], P('dp')
- grad_value_bias: float32 [512], P('dp')
- grad_position_table: float32 [16, 169], P('dp')
- grad_output_weight: float32 [512, 512], P('dp')
- grad_output_bias: float32 [512], P('dp')
- grad_second_gain: float32 [512], P('dp')
- grad_second_shift: float32 [512], P('dp')
- grad_expand_weight: float32 [512, 2048], P('dp')
- grad_expand_bias: float32 [2048], P('dp')
- grad_shrink_weight: float32 [2048, 512], P('dp')
- grad_shrink_bias: float32 [512], P('dp')
Inputs may be any that keep to these rules, and one draw needn't show every extreme that they name: position_index[q, k] names the row of position_table for the offset between places q and k of a window; two pairs share a row exactly when their offsets are equal, and every row is named.
All inputs are finite; a program needn't handle non-finite values.
Results may differ from a plain program's by a relative error of at most 0.019.
Values may be sent and summed in bfloat16 or wider, within the bound.
No kernel may reach another device: no remote copies, remote signals or barrier semaphores. Data moves between devices by JAX's collectives and lax.ppermute only.
A program may use at most 256 MiB of HBM per device.

v0:
```python
import functools

import jax
import jax.numpy as jnp
from jax import lax
from jax.experimental import pallas as pl
from jax.experimental.pallas import tpu as pltpu
from jax.sharding import PartitionSpec as P


WIN = 7
SHIFT = 3
PAD = 8
WT = WIN * PAD
QL = 64
EPSILON = 1e-05
ROOT_HALF = 0.7071067811865476
NORMAL_PEAK = 0.3989422804014327
FAR_BELOW = -1000000000.0
BF = jnp.bfloat16
F32 = jnp.float32
BANDS = 4
LINES = 16
VMEM_LIMIT = 60 * 1024 * 1024


def nn(a, b):
    return lax.dot_general(a, b, (((1,), (0,)), ((), ())), preferred_element_type=F32)


def nt(a, b):
    return lax.dot_general(a, b, (((1,), (1,)), ((), ())), preferred_element_type=F32)


def tn(a, b):
    return lax.dot_general(a, b, (((0,), (0,)), ((), ())), preferred_element_type=F32)


def norm_parts(values):
    center = values - jnp.mean(values, axis=-1, keepdims=True)
    inverse = lax.rsqrt(jnp.mean(center * center, axis=-1, keepdims=True) + EPSILON)
    return center * inverse, inverse


def norm_back(upper, normed, inverse, scaling):
    scaled = upper * scaling
    return inverse * (
        scaled
        - jnp.mean(scaled, axis=-1, keepdims=True)
        - normed * jnp.mean(scaled * normed, axis=-1, keepdims=True)
    )


def row_of(band, col):
    return ((2 * band + col // WIN) * WIN + col % WIN) * PAD


def extract(half, tile_ref, row_ref, col_ref, out_ref):
    _, breadth, height, features = tile_ref.shape
    zero = jnp.zeros((1, features), F32)
    for band in range(BANDS):
        for col in range(breadth):
            at = row_of(band, col)
            out_ref[at + WIN : at + PAD, :] = zero
    for place in range(height // (BANDS * WIN)):

        @pl.when(half == place)
        def _():
            for col in range(breadth):
                local = col < breadth - SHIFT
                for band in range(BANDS):
                    at = row_of(band, col)
                    start = (place * BANDS + band) * WIN + SHIFT
                    count = min(WIN, height - start)
                    rows = slice(start, start + count)
                    out_ref[at : at + count, :] = (
                        tile_ref[0, col + SHIFT, rows, :]
                        if local
                        else col_ref[0, col + SHIFT - breadth, rows, :]
                    )
                    for j in range(WIN - count):
                        out_ref[at + count + j : at + count + j + 1, :] = row_ref[
                            0, j, col : col + 1, :
                        ]


def deposit(half, src_ref, tile_ref, row_ref, col_ref):
    _, breadth, height, _ = tile_ref.shape
    for place in range(height // (BANDS * WIN)):

        @pl.when(half == place)
        def _():
            for col in range(breadth):
                local = col < breadth - SHIFT
                for band in range(BANDS):
                    at = row_of(band, col)
                    start = (place * BANDS + band) * WIN + SHIFT
                    count = min(WIN, height - start)
                    rows = slice(start, start + count)
                    if local:
                        tile_ref[0, col + SHIFT, rows, :] = src_ref[at : at + count, :]
                    else:
                        col_ref[0, col + SHIFT - breadth, rows, :] = src_ref[at : at + count, :]
                    for j in range(WIN - count):
                        row_ref[0, j, col : col + 1, :] = src_ref[
                            at + count + j : at + count + j + 1, :
                        ]


def spread(rows, head_size, lanes):
    heads = lanes // head_size
    rows = jnp.concatenate([rows, jnp.zeros((QL - WT, lanes), rows.dtype)], axis=0)
    lane = lax.broadcasted_iota(jnp.int32, (QL, lanes), 1) // head_size
    zero = jnp.zeros_like(rows)
    return jnp.concatenate([jnp.where(lane == h, rows, zero) for h in range(heads)], axis=0)


def collapse(wide, head_size, lanes):
    heads = lanes // head_size
    lane = lax.broadcasted_iota(jnp.int32, (WT, lanes), 1) // head_size
    out = wide[0:WT]
    for h in range(1, heads):
        out = jnp.where(lane == h, wide[h * QL : h * QL + WT], out)
    return out


def per_query(scores_low, feats, head_size):
    features = feats.shape[1]
    quad = 128 // head_size
    parts = []
    for g in range(features // 128):
        block = scores_low[:, g * quad * QL : (g + 1) * quad * QL]
        wide = tn(block, feats[:, g * 128 : (g + 1) * 128])
        parts.append(collapse(wide, head_size, 128))
    return jnp.concatenate(parts, axis=1)


def attend_kernel(
    head_size,
    tile_ref,
    row_ref,
    col_ref,
    weight_ref,
    vec_ref,
    bias_ref,
    xp_ref,
    hid_ref,
    qkv_ref,
    prob_ref,
    att_ref,
    mid_ref,
    wide_ref,
):
    half = pl.program_id(1)
    features = tile_ref.shape[-1]
    extract(half, tile_ref, row_ref, col_ref, xp_ref)
    normed, _ = norm_parts(xp_ref[...])
    hidden = (normed * vec_ref[0:1, :] + vec_ref[1:2, :]).astype(BF)
    hid_ref[...] = hidden
    scale = head_size ** (-0.5)
    for part in range(3):
        got = nn(hidden, weight_ref[:, part * features : (part + 1) * features])
        if part == 0:
            got = got + vec_ref[2:3, :]
        if part == 2:
            got = got + vec_ref[3:4, :]
        qkv_ref[:, :, part * features : (part + 1) * features] = got.reshape(
            2 * BANDS, WT, features
        ).astype(BF)

    group = 256
    span = group // head_size * QL
    for w in range(2 * BANDS):
        kind = w % 2
        edge = jnp.where(half == 0, 0, 1) if w // 2 == BANDS - 1 else 0
        for g in range(features // group):
            q = qkv_ref[w, :, g * group : (g + 1) * group]
            k = qkv_ref[w, :, features + g * group : features + (g + 1) * group]
            raw = nt(k, spread(q, head_size, group))
            score = raw * scale + bias_ref[edge, kind, :, g * span : (g + 1) * span]
            highest = jnp.max(score, axis=0, keepdims=True)
            grown = jnp.exp(score - highest)
            total = jnp.sum(grown, axis=0, keepdims=True)
            probs = (grown * (1.0 / total)).astype(BF)
            prob_ref[w, :, g * span : (g + 1) * span] = probs
            v = qkv_ref[w, :, 2 * features + g * group : 2 * features + (g + 1) * group]
            wide_ref[w * WT : (w + 1) * WT, g * group : (g + 1) * group] = per_query(
                probs, v, head_size
            )
    attended = wide_ref[...].astype(BF)
    att_ref[...] = attended
    branch = nn(attended, weight_ref[:, 3 * features :]) + vec_ref[4:5, :]
    mid_ref[...] = xp_ref[...] + branch


def mlp_kernel(
    tile_ref,
    row_ref,
    col_ref,
    mid_ref,
    att_ref,
    weight_ref,
    packed_ref,
    vec_ref,
    ebias_ref,
    res_ref,
    resrow_ref,
    rescol_ref,
    gmid_ref,
    gatt_ref,
    pack_ref,
    cot_ref,
    we_ref,
    ws_ref,
    ge_ref,
    gs_ref,
    go_ref,
    out_ref,
    sums_ref,
    esum_ref,
):
    half = pl.program_id(1)
    step = pl.program_id(0) * pl.num_programs(1) + half
    steps = pl.num_programs(0) * pl.num_programs(1)
    features = tile_ref.shape[-1]
    hidden_units = we_ref.shape[1]
    shards = pack_ref.shape[0]
    deep = features // shards
    blocks = hidden_units // features

    @pl.when(step == 0)
    def _():
        for d in range(shards):
            we_ref[d * deep : (d + 1) * deep, :] = packed_ref[d, 0:deep, :]
            for j in range(blocks):
                at = d * deep * blocks + j * deep
                ws_ref[at : at + deep, :] = packed_ref[
                    d, deep : 2 * deep, j * features : (j + 1) * features
                ]
        ge_ref[...] = jnp.zeros_like(ge_ref)
        gs_ref[...] = jnp.zeros_like(gs_ref)
        go_ref[...] = jnp.zeros_like(go_ref)
        sums_ref[...] = jnp.zeros_like(sums_ref)
        esum_ref[...] = jnp.zeros_like(esum_ref)

    extract(half, tile_ref, row_ref, col_ref, cot_ref)
    mid = mid_ref[...]
    normed, inverse = norm_parts(mid)
    hidden = (normed * vec_ref[5:6, :] + vec_ref[6:7, :]).astype(BF)
    hidden_t = hidden.T
    low = cot_ref[...].astype(BF)
    low_t = low.T
    out = mid + vec_ref[7:8, :]
    ghid = None
    chunk = features
    for c in range(hidden_units // chunk):
        cols = slice(c * chunk, (c + 1) * chunk)
        before = nn(hidden, we_ref[:, cols]) + ebias_ref[0:1, cols]
        phi = 0.5 * (1.0 + lax.erf(before * ROOT_HALF))
        slope = phi + before * (NORMAL_PEAK * jnp.exp(-0.5 * before * before))
        active = (before * phi).astype(BF)
        out = out + nn(active, ws_ref[cols, :])
        gbefore = nt(low, ws_ref[cols, :]) * slope
        esum_ref[0:1, cols] += jnp.sum(gbefore, axis=0, keepdims=True)
        gbefore = gbefore.astype(BF)
        back = nt(gbefore, we_ref[:, cols])
        ghid = back if ghid is None else ghid + back
        gs_ref[:, cols] += nn(low_t, active)
        ge_ref[:, cols] += nn(hidden_t, gbefore)
    out_ref[...] = out
    deposit(half, out_ref, res_ref, resrow_ref, rescol_ref)
    cot = cot_ref[...]
    gmid = cot + norm_back(ghid, normed, inverse, vec_ref[5:6, :])
    gmid_ref[...] = gmid
    gbranch = gmid.astype(BF)
    go_ref[...] += nn(att_ref[...].T, gbranch)
    gatt = nt(gbranch, weight_ref[:, 3 * features :])
    gatt_ref[...] = gatt.reshape(2 * BANDS, WT, features).astype(BF)
    sums_ref[0:1, :] += jnp.sum(gmid, axis=0, keepdims=True)
    sums_ref[1:2, :] += jnp.sum(ghid * normed, axis=0, keepdims=True)
    sums_ref[2:3, :] += jnp.sum(ghid, axis=0, keepdims=True)
    sums_ref[3:4, :] += jnp.sum(cot, axis=0, keepdims=True)

    @pl.when(step == steps - 1)
    def _():
        even = hidden_units // shards
        base = 2 * deep + LINES
        pack_ref[:, 2 * deep : base, :] = jnp.zeros((shards, LINES, hidden_units), BF)
        for d in range(shards):
            pack_ref[d, 2 * deep : base, 0:deep] = sums_ref[:, d * deep : (d + 1) * deep].astype(BF)
            pack_ref[d, 2 * deep : base, features : features + even] = esum_ref[
                :, d * even : (d + 1) * even
            ].astype(BF)
            pack_ref[d, 0:deep, :] = ge_ref[d * deep : (d + 1) * deep, :].astype(BF)
            for j in range(blocks):
                at = d * deep * blocks + j * deep
                if deep * 2 % 128 == 0 and j % 2 == 0:
                    both = gs_ref[:, at : at + 2 * deep].T
                    pack_ref[d, deep : 2 * deep, j * features : (j + 1) * features] = both[
                        :deep
                    ].astype(BF)
                    pack_ref[d, deep : 2 * deep, (j + 1) * features : (j + 2) * features] = both[
                        deep:
                    ].astype(BF)
                elif deep * 2 % 128 != 0:
                    pack_ref[d, deep : 2 * deep, j * features : (j + 1) * features] = (
                        gs_ref[:, at : at + deep].T.astype(BF)
                    )
                thin = deep // blocks
                pack_ref[d, base : base + thin, j * features : (j + 1) * features] = go_ref[
                    d * deep + j * thin : d * deep + (j + 1) * thin, :
                ].astype(BF)


def back_kernel(
    head_size,
    hid_ref,
    qkv_ref,
    prob_ref,
    gatt_ref,
    weight_ref,
    vec_ref,
    gact_ref,
    pack_ref,
    acc_ref,
    wide_ref,
    sums_ref,
    table_ref,
):
    half = pl.program_id(1)
    step = pl.program_id(0) * pl.num_programs(1) + half
    steps = pl.num_programs(0) * pl.num_programs(1)
    features = hid_ref.shape[-1]
    scale = head_size ** (-0.5)

    @pl.when(step == 0)
    def _():
        acc_ref[...] = jnp.zeros_like(acc_ref)
        sums_ref[...] = jnp.zeros_like(sums_ref)
        table_ref[...] = jnp.zeros_like(table_ref)

    group = 256
    span = group // head_size * QL
    for w in range(2 * BANDS):
        rows = slice(w * WT, (w + 1) * WT)
        for g in range(features // group):
            feats = slice(g * group, (g + 1) * group)
            lanes = slice(g * span, (g + 1) * span)
            q = qkv_ref[w, :, g * group : (g + 1) * group]
            k = qkv_ref[w, :, features + g * group : features + (g + 1) * group]
            v = qkv_ref[w, :, 2 * features + g * group : 2 * features + (g + 1) * group]
            up = spread(gatt_ref[w, :, feats], head_size, group)
            low = prob_ref[w, :, lanes]
            probs = low.astype(F32)
            gprobs = nt(v, up)
            mean = jnp.sum(probs * gprobs, axis=0, keepdims=True)
            gscore = probs * (gprobs - mean)
            table_ref[0:WT, lanes] += gscore
            graw = (gscore * scale).astype(BF)
            wide_ref[rows, g * group : (g + 1) * group] = per_query(graw, k, head_size)
            wide_ref[rows, features + g * group : features + (g + 1) * group] = nn(
                graw, spread(q, head_size, group)
            )
            wide_ref[rows, 2 * features + g * group : 2 * features + (g + 1) * group] = nn(low, up)
    gjoint = wide_ref[...]
    sums_ref[...] += jnp.sum(gjoint, axis=0, keepdims=True)
    gjoint = gjoint.astype(BF)
    gact_ref[...] = gjoint
    acc_ref[...] += nn(hid_ref[...].T, gjoint)

    @pl.when(step == steps - 1)
    def _():
        shards = pack_ref.shape[0]
        deep = features // shards
        lanes = table_ref.shape[1] // shards
        total = sums_ref[0:1, :]
        by_acc = jnp.zeros((features, 128), F32)
        by_sum = jnp.zeros((features, 128), F32)
        for c in range(3 * features // 128):
            cols = slice(c * 128, (c + 1) * 128)
            weight = weight_ref[:, cols].astype(F32)
            by_acc = by_acc + weight * acc_ref[:, cols]
            by_sum = by_sum + weight * total[:, cols]
        by_acc = jnp.sum(by_acc.T, axis=0, keepdims=True)
        gshift = jnp.sum(by_sum.T, axis=0, keepdims=True)
        ggain = (by_acc - vec_ref[1:2, :] * gshift) / vec_ref[0:1, :]
        lines = jnp.concatenate(
            [
                ggain,
                gshift,
                total[:, :features],
                total[:, 2 * features :],
                jnp.zeros((LINES - 4, features), F32),
            ],
            axis=0,
        )
        for d in range(shards):
            pack_ref[d, 0:deep, :] = acc_ref[d * deep : (d + 1) * deep, :].astype(BF)
            pack_ref[d, deep : deep + LINES, 4 * lanes + deep :] = jnp.zeros(
                (LINES, 3 * features - 4 * lanes - deep), BF
            )
            for j in range(4):
                pack_ref[d, deep : deep + LINES, j * lanes : (j + 1) * lanes] = table_ref[
                    j * LINES : (j + 1) * LINES, d * lanes : (d + 1) * lanes
                ].astype(BF)
            pack_ref[d, deep : deep + LINES, 4 * lanes : 4 * lanes + deep] = lines[
                :, d * deep : (d + 1) * deep
            ].astype(BF)


def close_kernel(
    gact_ref, xp_ref, gmid_ref, weight_ref, vec_ref, gtok_ref, grow_ref, gcol_ref, out_ref
):
    features = xp_ref.shape[-1]
    ghid = nt(gact_ref[...], weight_ref[:, : 3 * features])
    normed, inverse = norm_parts(xp_ref[...])
    out_ref[...] = gmid_ref[...] + norm_back(ghid, normed, inverse, vec_ref[0:1, :])
    deposit(pl.program_id(1), out_ref, gtok_ref, grow_ref, gcol_ref)


def patch_kernel(tile_ref, col_ref, row_ref, out_ref, flank_ref, top_ref, sems):
    images, breadth, _, _ = tile_ref.shape
    fetch = pltpu.make_async_copy(out_ref.at[:, SHIFT:, 0:PAD], top_ref, sems.at[0])
    fetch.start()
    flank_ref[...] = col_ref[...].astype(F32)
    for i in range(images):
        for c in range(SHIFT):
            for j in range(SHIFT):
                flank_ref[i, c, j : j + 1, :] = row_ref[i, j, c : c + 1, :]
    side = pltpu.make_async_copy(flank_ref, out_ref.at[:, 0:SHIFT], sems.at[1])
    side.start()
    fetch.wait()
    for i in range(images):
        for c in range(breadth - SHIFT):
            for j in range(SHIFT):
                top_ref[i, c, j : j + 1, :] = row_ref[i, j, c + SHIFT : c + SHIFT + 1, :]
    back = pltpu.make_async_copy(top_ref, out_ref.at[:, SHIFT:, 0:PAD], sems.at[2])
    back.start()
    side.wait()
    back.wait()


def shifted(block, axis, distance):
    count = lax.axis_size(axis)
    return lax.ppermute(block, axis, [((i - distance) % count, i) for i in range(count)])


def slanted(block, distance):
    rows, cols = lax.axis_size("row"), lax.axis_size("col")
    route = [
        (((r - distance) % rows) * cols + (c - distance) % cols, r * cols + c)
        for r in range(rows)
        for c in range(cols)
    ]
    return lax.ppermute(block, ("row", "col"), route)


def roll_in(values):
    cols = shifted(values[:, :SHIFT].astype(BF), "col", -1)
    top = values[:, :, :SHIFT].astype(BF).transpose(0, 2, 1, 3)
    rows = shifted(top[:, :, SHIFT:], "row", -1)
    corner = slanted(top[:, :, :SHIFT], -1)
    return jnp.concatenate([rows, corner], axis=2).astype(F32), cols.astype(F32)


def roll_out(tile, rows, cols):
    images, breadth, height, features = tile.shape
    rows = rows.astype(BF)
    flank = shifted(cols.astype(BF), "col", 1)
    top = shifted(rows[:, :, : breadth - SHIFT], "row", 1)
    corner = slanted(rows[:, :, breadth - SHIFT :], 1)
    top = jnp.concatenate([corner, top], axis=2).astype(F32)
    vmem = pl.BlockSpec(memory_space=pltpu.VMEM)
    return pl.pallas_call(
        patch_kernel,
        in_specs=[pl.BlockSpec(memory_space=pl.ANY), vmem, vmem],
        out_specs=pl.BlockSpec(memory_space=pl.ANY),
        out_shape=jax.ShapeDtypeStruct(tile.shape, F32),
        scratch_shapes=[
            pltpu.VMEM((images, SHIFT, height, features), F32),
            pltpu.VMEM((images, breadth - SHIFT, PAD, features), F32),
            pltpu.SemaphoreType.DMA((3,)),
        ],
        input_output_aliases={0: 0},
        compiler_params=pltpu.CompilerParams(vmem_limit_bytes=24 * 1024 * 1024),
        cost_estimate=pl.CostEstimate(flops=0, bytes_accessed=4_000_000, transcendentals=0),
        name="patch",
    )(tile, flank, top)


def over_tiles(block):
    def added(part, axis):
        total = part.astype(F32)
        for step in range(1, lax.axis_size(axis)):
            total = total + shifted(part, axis, step).astype(F32)
        return total

    cut = block.shape[-1] // 2
    first = added(added(block[:, :cut], "row").astype(BF), "col")
    second = added(added(block[:, cut:], "col").astype(BF), "row")
    return jnp.concatenate([first, second], axis=1)


def region_band(places, count):
    return jnp.where(places < count - WIN, 0, jnp.where(places < count - SHIFT, 1, 2)).astype(
        jnp.int32
    )


def whole(shape):
    return pl.BlockSpec(shape, lambda i, j: (0,) * len(shape), pipeline_mode=pl.Buffered(1))


def body(
    tokens,
    position_index,
    first_gain,
    first_shift,
    joint_weight,
    query_bias,
    value_bias,
    position_table,
    output_weight,
    output_bias,
    second_gain,
    second_shift,
    expand_weight,
    expand_bias,
    shrink_weight,
    shrink_bias,
    cotangent,
):
    images, height, breadth, features = tokens.shape
    shards = lax.axis_size("dp")
    deep = joint_weight.shape[0]
    table_heads, table_rows = position_table.shape
    heads = table_heads * shards
    head_size = features // heads
    hidden_units = expand_weight.shape[1]
    blocks = hidden_units // features
    halves = height // (WIN * BANDS)
    grid = (images, halves)
    step_rows = 2 * BANDS * WT
    total_rows = images * halves * step_rows
    windows = images * halves * 2 * BANDS
    wide = heads * QL

    small = [
        first_gain,
        first_shift,
        query_bias,
        value_bias,
        output_bias,
        second_gain,
        second_shift,
        shrink_bias,
        expand_bias,
        position_table.reshape(-1),
    ]
    small = jnp.concatenate([s.astype(BF) for s in small])
    small = jnp.pad(small, (0, -small.shape[0] % 128))[None]
    small = lax.all_gather(small, "dp", axis=0, tiled=True)
    vec = small[:, : 8 * deep].reshape(shards, 8, deep).transpose(1, 0, 2).reshape(8, features)
    vec = vec.astype(F32)
    at = 8 * deep
    ebias = small[:, at : at + blocks * deep].reshape(1, hidden_units).astype(F32)
    at += blocks * deep
    table = small[:, at : at + table_heads * table_rows].reshape(heads, table_rows)
    weight_one = lax.all_gather(
        jnp.concatenate([joint_weight, output_weight], axis=1).astype(BF), "dp", axis=0, tiled=True
    )
    thick = jnp.concatenate(
        [shrink_weight[j * deep : (j + 1) * deep] for j in range(blocks)], axis=1
    )
    weight_two = lax.all_gather(
        jnp.concatenate([expand_weight, thick], axis=0).astype(BF)[None], "dp", axis=0, tiled=True
    )

    tokens, cotangent = tokens.transpose(0, 2, 1, 3), cotangent.transpose(0, 2, 1, 3)
    tok_row, tok_col = roll_in(tokens)
    cot_row, cot_col = roll_in(cotangent)

    paired = position_index.reshape(WIN, WIN, WIN, WIN)
    paired = paired.transpose(1, 0, 3, 2)
    paired = jnp.pad(paired, ((0, 0), (0, 1), (0, 0), (0, 1)), constant_values=-1)
    paired = jnp.pad(
        paired.reshape(WT, WT).T, ((0, 0), (0, QL - WT)), constant_values=-1
    ).reshape(-1)
    onehot = paired[None, :] == jnp.arange(table_rows, dtype=jnp.int32)[:, None]
    position = jnp.dot(table, onehot.astype(BF), preferred_element_type=F32)
    position = position.reshape(heads, WT, QL).transpose(1, 0, 2)
    grid_rows = height * lax.axis_size("row")
    grid_cols = breadth * lax.axis_size("col")
    row_places = jnp.stack([jnp.arange(WIN), jnp.arange(WIN) + height - WIN]).astype(jnp.int32)
    row_places = row_places + lax.axis_index("row") * height
    col_places = jnp.arange(2 * WIN, dtype=jnp.int32).reshape(2, WIN)
    col_places = col_places + lax.axis_index("col") * breadth
    row_label = jnp.pad(region_band(row_places, grid_rows), ((0, 0), (0, 1)))
    col_label = region_band(col_places, grid_cols)
    label = 3 * row_label[:, None, None, :] + col_label[None, :, :, None]
    label = label.reshape(2, 2, WT)
    label_q = jnp.pad(label, ((0, 0), (0, 0), (0, QL - WT)))
    masking = jnp.where(label[:, :, :, None] == label_q[:, :, None, :], 0.0, -100.0)
    absent = (jnp.arange(WT) % PAD == WIN)[:, None]
    masking = jnp.where(absent, FAR_BELOW, masking).astype(F32)
    bias = (position[None, None] + masking[:, :, :, None, :]).reshape(2, 2, WT, wide)

    tile_spec = pl.BlockSpec((1, breadth, height, features), lambda i, j: (i, 0, 0, 0))
    row_spec = pl.BlockSpec((1, SHIFT, breadth, features), lambda i, j: (i, 0, 0, 0))
    col_spec = pl.BlockSpec((1, SHIFT, height, features), lambda i, j: (i, 0, 0, 0))
    flat_spec = pl.BlockSpec((step_rows, features), lambda i, j: (i * halves + j, 0))

    joint_spec = pl.BlockSpec((step_rows, 3 * features), lambda i, j: (i * halves + j, 0))

    def window_spec(last):
        return pl.BlockSpec((2 * BANDS, WT, last), lambda i, j: (i * halves + j, 0, 0))

    params = pltpu.CompilerParams(
        dimension_semantics=("arbitrary", "arbitrary"), vmem_limit_bytes=VMEM_LIMIT
    )
    shape = jax.ShapeDtypeStruct
    dense = 2 * total_rows * features * features

    xp, hidden_one, qkv, probs, attended, middle = pl.pallas_call(
        functools.partial(attend_kernel, head_size),
        grid=grid,
        in_specs=[
            tile_spec,
            row_spec,
            col_spec,
            whole((features, 4 * features)),
            whole((8, features)),
            whole((2, 2, WT, wide)),
        ],
        out_specs=[
            flat_spec,
            flat_spec,
            window_spec(3 * features),
            window_spec(wide),
            flat_spec,
            flat_spec,
        ],
        out_shape=[
            shape((total_rows, features), F32),
            shape((total_rows, features), BF),
            shape((windows, WT, 3 * features), BF),
            shape((windows, WT, wide), BF),
            shape((total_rows, features), BF),
            shape((total_rows, features), F32),
        ],
        scratch_shapes=[pltpu.VMEM((step_rows, features), F32)],
        compiler_params=params,
        cost_estimate=pl.CostEstimate(
            flops=6 * dense, bytes_accessed=40_000_000, transcendentals=windows * WT * wide
        ),
        name="attend",
    )(tokens, tok_row, tok_col, weight_one, vec, bias)

    packed_rows = 2 * deep + deep // blocks + LINES
    result, res_row, res_col, gmid, gatt, pack_two = pl.pallas_call(
        mlp_kernel,
        grid=grid,
        in_specs=[
            tile_spec,
            row_spec,
            col_spec,
            flat_spec,
            flat_spec,
            whole((features, 4 * features)),
            whole((shards, 2 * deep, hidden_units)),
            whole((8, features)),
            whole((1, hidden_units)),
        ],
        out_specs=[
            tile_spec,
            row_spec,
            col_spec,
            flat_spec,
            window_spec(features),
            whole((shards, packed_rows, hidden_units)),
        ],
        out_shape=[
            shape(tokens.shape, F32),
            shape((images, SHIFT, breadth, features), F32),
            shape((images, SHIFT, height, features), F32),
            shape((total_rows, features), F32),
            shape((windows, WT, features), BF),
            shape((shards, packed_rows, hidden_units), BF),
        ],
        scratch_shapes=[
            pltpu.VMEM((step_rows, features), F32),
            pltpu.VMEM((features, hidden_units), BF),
            pltpu.VMEM((hidden_units, features), BF),
            pltpu.VMEM((features, hidden_units), F32),
            pltpu.VMEM((features, hidden_units), F32),
            pltpu.VMEM((features, features), F32),
            pltpu.VMEM((step_rows, features), F32),
            pltpu.VMEM((LINES, features), F32),
            pltpu.VMEM((LINES, hidden_units), F32),
        ],
        compiler_params=params,
        cost_estimate=pl.CostEstimate(
            flops=26 * dense,
            bytes_accessed=50_000_000,
            transcendentals=total_rows * hidden_units,
        ),
        name="mlp",
    )(
        cotangent,
        cot_row,
        cot_col,
        middle,
        attended,
        weight_one,
        weight_two,
        vec,
        ebias,
    )

    pack_two = lax.psum_scatter(pack_two, "dp", scatter_dimension=0, tiled=True)[0]
    final = roll_out(result, res_row, res_col)

    gact, pack_one = pl.pallas_call(
        functools.partial(back_kernel, head_size),
        grid=grid,
        in_specs=[
            flat_spec,
            window_spec(3 * features),
            window_spec(wide),
            window_spec(features),
            whole((features, 4 * features)),
            whole((8, features)),
        ],
        out_specs=[joint_spec, whole((shards, deep + LINES, 3 * features))],
        out_shape=[
            shape((total_rows, 3 * features), BF),
            shape((shards, deep + LINES, 3 * features), BF),
        ],
        scratch_shapes=[
            pltpu.VMEM((features, 3 * features), F32),
            pltpu.VMEM((step_rows, 3 * features), F32),
            pltpu.VMEM((1, 3 * features), F32),
            pltpu.VMEM((4 * LINES, wide), F32),
        ],
        compiler_params=params,
        cost_estimate=pl.CostEstimate(
            flops=18 * dense, bytes_accessed=50_000_000, transcendentals=0
        ),
        name="back",
    )(hidden_one, qkv, probs, gatt, weight_one, vec)

    pack_one = lax.psum_scatter(pack_one, "dp", scatter_dimension=0, tiled=True)[0]

    gtok, gtok_row, gtok_col = pl.pallas_call(
        close_kernel,
        grid=grid,
        in_specs=[
            joint_spec,
            flat_spec,
            flat_spec,
            whole((features, 4 * features)),
            whole((8, features)),
        ],
        out_specs=[tile_spec, row_spec, col_spec],
        out_shape=[
            shape(tokens.shape, F32),
            shape((images, SHIFT, breadth, features), F32),
            shape((images, SHIFT, height, features), F32),
        ],
        scratch_shapes=[pltpu.VMEM((step_rows, features), F32)],
        compiler_params=params,
        cost_estimate=pl.CostEstimate(
            flops=6 * dense, bytes_accessed=30_000_000, transcendentals=0
        ),
        name="close",
    )(gact, xp, gmid, weight_one, vec)
    grad_tokens = roll_out(gtok, gtok_row, gtok_col)

    pack_two = over_tiles(pack_two)
    pack_one = over_tiles(pack_one)
    grad_expand = pack_two[:deep]
    grad_shrink = jnp.concatenate(
        [pack_two[deep : 2 * deep, j * features : (j + 1) * features] for j in range(blocks)],
        axis=0,
    )
    base = 2 * deep + LINES
    grad_output = jnp.concatenate(
        [pack_two[base:, j * features : (j + 1) * features] for j in range(blocks)], axis=0
    )
    lines_two = pack_two[2 * deep : base, :deep]
    grad_expand_bias = pack_two[2 * deep, features : features + blocks * deep]
    grad_joint = pack_one[:deep]
    lanes = table_heads * QL
    lines_one = pack_one[deep:, 4 * lanes : 4 * lanes + deep]
    gtable = jnp.concatenate(
        [pack_one[deep:, j * lanes : (j + 1) * lanes] for j in range(4)], axis=0
    )[:WT]
    gtable = gtable.reshape(WT, table_heads, QL).transpose(1, 0, 2).reshape(table_heads, WT * QL)
    grad_position = lax.dot_general(
        gtable,
        onehot.astype(F32),
        (((1,), (1,)), ((), ())),
        precision=lax.Precision.HIGHEST,
        preferred_element_type=F32,
    )
    final, grad_tokens = final.transpose(0, 2, 1, 3), grad_tokens.transpose(0, 2, 1, 3)
    return (
        final,
        grad_tokens,
        lines_one[0],
        lines_one[1],
        grad_joint,
        lines_one[2],
        lines_one[3],
        grad_position,
        grad_output,
        lines_two[0],
        lines_two[1],
        lines_two[2],
        grad_expand,
        grad_expand_bias,
        grad_shrink,
        lines_two[3],
    )


def solution(mesh):
    tile = P("dp", "row", "col", None)
    flat = P("dp")
    wide = P("dp", None)

    return jax.shard_map(
        body,
        mesh=mesh,
        in_specs=(
            tile,
            P(),
            flat,
            flat,
            wide,
            flat,
            flat,
            wide,
            wide,
            flat,
            flat,
            flat,
            wide,
            flat,
            wide,
            flat,
            tile,
        ),
        out_specs=(
            tile,
            tile,
            flat,
            flat,
            wide,
            flat,
            flat,
            wide,
            wide,
            flat,
            flat,
            flat,
            wide,
            flat,
            wide,
            flat,
        ),
        check_vma=False,
    )
```

profile of v0, /device:TPU:0, one launch (start us, length us, event | category | flops | bytes accessed | tf_op | source)
XLA Modules:
  0.0 338.2 jit_solution(635541779197915598)
XLA Ops:
  7.2 0.9 convert.37
  8.1 1.0 convert.36
  10.0 1.1 convert.39
  11.1 1.1 convert_bitcast_fusion
  12.2 0.8 pad_maximum_fusion.1
  13.1 2.7 bitcast_convert_fusion
  16.5 3.9 %collective-permute-start.4 = (bf16[3,3,3,512]{3,1,2,0:T(4,128)(2,1)}, bf16[3,3,3,512]{3,1,2,0:T(4,128)(2,1)S(1)}, u32[]{:S(2)}, u32[]{:S(2)}) collective-permute-start(bf16[3,3,3,512]{3,1,2,0:T(4,128)(2,1)} %slice.212), channel_id=1, source_target_pairs={{3,0},{2,1},{1,2},{0,3},{7,4},{6,5},{5,6},{4,7},{11,8},{10,9},{9,1... | collective-permute-start | bytes 82952 | tf_op jit(solution)/shard_map/ppermute | solution.py:455
  22.1 2.7 bitcast_convert_fusion.1
  25.5 2.9 collective-permute-start.1
  30.4 14.5 %all-gather.1 = bf16[8,1,1152]{2,1,0:T(2,128)(2,1)S(1)} all-gather(bf16[1,1,1152]{2,1,0:T(2,128)(2,1)S(1)} %reshape.175), channel_id=2, replica_groups=mesh['dp'=8,'row'=2,'col'=2] {'dp'}, dimensions={0}, use_global_device_ids=true | all-gather | bytes 20736 | tf_op jit(solution)/shard_map/all_gather | solution.py:562
  45.8 1.6 fusion.6
  48.3 1.0 broadcast_add_fusion.bias_ref
  52.3 4.3 %collective-permute-done = bf16[3,3,11,512]{3,1,2,0:T(4,128)(2,1)S(1)} collective-permute-done((bf16[3,3,11,512]{3,1,2,0:T(4,128)(2,1)S(1)}, bf16[3,3,11,512]{3,1,2,0:T(4,128)(2,1)S(1)}, u32[]{:S(2)}, u32[]{:S(2)}) %collective-permute-start) | collective-permute-done | bytes 101408 | tf_op jit(solution)/shard_map/ppermute | solution.py:445
  57.5 2.1 convert_element_type.157.col_ref
  59.7 2.2 convert_element_type.155.col_ref
  61.8 43.9 %attend.1 = (f32[2688,512]{1,0:T(8,128)}, bf16[2688,512]{1,0:T(8,128)(2,1)}, bf16[48,56,1536]{2,1,0:T(8,128)(2,1)}, bf16[48,56,1024]{2,1,0:T(8,128)(2,1)}, bf16[...) custom-call(f32[3,14,56,512]{3,2,1,0:T(8,128)} %bitcast.59, f32[3,3,14,512]{3,2,1,0:T(8,128)} %copy.67.row_ref, ...), custom_call_target="tpu_custom_call" | custom-call | flops 8455716864 | bytes 40000000 | tf_op jit(solution)/shard_map/attend/pallas_call | solution.py:624
  105.8 57.8 %mlp.1 = (f32[3,14,56,512]{3,2,1,0:T(8,128)}, f32[3,3,14,512]{3,2,1,0:T(8,128)}, f32[3,3,56,512]{3,2,1,0:T(8,128)}, f32[2688,512]{1,0:T(8,128)}, bf16[48,56,512]...) custom-call(f32[3,14,56,512]{3,2,1,0:T(8,128)} %bitcast.60, f32[3,3,14,512]{3,2,1,0:T(8,128)} %copy.68.row_ref, ...), custom_call_target="tpu_custom_call" | custom-call | flops 36641439744 | bytes 50000000 | tf_op jit(solution)/shard_map/mlp/pallas_call | solution.py:660
  163.6 48.0 %back.1 = (bf16[2688,1536]{1,0:T(8,128)(2,1)}, bf16[8,80,1536]{2,1,0:T(8,128)(2,1)}) custom-call(bf16[2688,512]{1,0:T(8,128)(2,1)} %get-tuple-element.38.hid_ref, bf16[48,56,1536]{2,1,0:T(8,128)(2,1)} %get-tuple-element.39.qkv_ref, bf16[48,56,1024]{2,1,0:T(8,128)(2,1)} %get-tuple-element.40.prob_ref, bf16[48,56,512]{2,1,0:T(8,128)(2,1)} %get-tuple-element.41.gatt_ref, ...), custom_call_target="tpu_custom_call" | custom-call | flops 25367150592 | bytes 50000000 | tf_op jit(solution)/shard_map/back/pallas_call | solution.py:723
  212.2 35.6 %reduce-scatter.3.cloned.1.call-done = bf16[1,80,1536]{2,1,0:T(8,128)(2,1)} async-done(((bf16[8,80,1536]{2,1,0:T(8,128)(2,1)}), bf16[1,80,1536]{2,1,0:T(8,128)(2,1)}) %reduce-scatter.3.cloned.1.call-update) | async-done | bytes 245776 | tf_op jit(solution)/shard_map/reduce_scatter | solution.py:752
  247.8 1.0 fusion.17
  248.8 1.4 collective-permute-start.14
  250.1 1.8 collective-permute-start.12
  251.9 15.2 %close.1 = (f32[3,14,56,512]{3,2,1,0:T(8,128)}, f32[3,3,14,512]{3,2,1,0:T(8,128)}, f32[3,3,56,512]{3,2,1,0:T(8,128)}) custom-call(bf16[2688,1536]{1,0:T(8,128)(2,1)} %get-tuple-element.42.gact_ref, f32[2688,512]{1,0:T(8,128)} %get-tuple-element.43.xp_ref, f32[2688,512]{1,0:T(8,128)} %get-tuple-element.44.gmid_ref, ...), custom_call_target="tpu_custom_call" | custom-call | flops 8455716864 | bytes 30000000 | tf_op jit(solution)/shard_map/close/pallas_call | solution.py:754
  267.1 1.3 convert_element_type.178
  268.6 2.1 collective-permute-start.6
  270.9 1.0 convert_element_type.179
  271.9 3.0 collective-permute-start.10
  275.0 2.3 collective-permute-done.10
  277.3 1.2 collective-permute-start.8
  278.5 1.6 collective-permute-done.11
  280.5 1.9 collective-permute-done.8
  282.5 1.5 collective-permute-done.9.col_ref
  283.9 2.1 patch.3
  286.1 5.7 %collective-permute-done.6.col_ref = bf16[3,3,56,512]{3,2,1,0:T(8,128)(2,1)S(1)} collective-permute-done((bf16[3,3,56,512]{3,2,1,0:T(8,128)(2,1)S(1)}, bf16[3,3,56,512]{3,2,1,0:T(8,128)(2,1)S(1)}, u32[]{:S(2)}, u32[]{:S(2)}) %collective-permute-start.6) | collective-permute-done | bytes 516128 | tf_op jit(solution)/shard_map/ppermute | solution.py:445
  291.7 2.1 patch.2
  293.9 0.9 collective-permute-start.15
  295.0 13.1 %reduce-scatter.5.cloned.1.call-done = bf16[1,160,2048]{2,1,0:T(8,128)(2,1)} async-done(((bf16[8,160,2048]{2,1,0:T(8,128)(2,1)}), bf16[1,160,2048]{2,1,0:T(8,128)(2,1)}) %reduce-scatter.5.cloned.1.call-update) | async-done | bytes 655376 | tf_op jit(solution)/shard_map/reduce_scatter | solution.py:720
  308.1 1.1 fusion.13
  309.2 1.5 collective-permute-start.16
  310.7 1.5 collective-permute-start.18
  312.2 1.8 fusion.3
  314.0 2.8 collective-permute-done.16
  316.8 1.2 collective-permute-done.18
  318.0 1.3 add_convert_fusion.1
  319.4 1.5 collective-permute-start.17
  322.7 3.8 %collective-permute-done.17 = bf16[160,1024]{1,0:T(8,128)(2,1)S(1)} collective-permute-done((bf16[160,1024]{1,0:T(8,128)(2,1)S(1)}, bf16[160,1024]{1,0:T(8,128)(2,1)S(1)}, u32[]{:S(2)}, u32[]{:S(2)}) %collective-permute-start.17) | collective-permute-done | bytes 327712 | tf_op jit(solution)/shard_map/ppermute | solution.py:445
  327.7 1.5 collective-permute-done.19
  329.3 0.8 pad_maximum_fusion
  (144 shorter events, 17.8 us)
Async XLA Ops:
  7.2 54.6 %all-gather.5.cloned.1.call-start = ((), (), s32[]{:S(2)}) async-start(), calls=%async_computation.2 | async-start | bytes 2359296 | tf_op jit(solution)/shard_map/all_gather | solution.py:569
  9.9 95.9 %all-gather.7.cloned.1.call-start = ((), (), s32[]{:S(2)}) async-start(), calls=%async_computation.3 | async-start | bytes 4718592 | tf_op jit(solution)/shard_map/all_gather | solution.py:575
  13.0 234.7 %reduce-scatter.3.cloned.1.call-start = ((), (), s32[]{:S(2)}) async-start(), calls=%async_computation.4 | async-start | bytes 2211840 | tf_op jit(solution)/shard_map/reduce_scatter | solution.py:752
  16.5 34.3 %collective-permute-start.4 = (bf16[3,3,3,512]{3,1,2,0:T(4,128)(2,1)}, bf16[3,3,3,512]{3,1,2,0:T(4,128)(2,1)S(1)}, u32[]{:S(2)}, u32[]{:S(2)}) collective-permute-start(bf16[3,3,3,512]{3,1,2,0:T(4,128)(2,1)} %slice.212), channel_id=1, source_target_pairs={{3,0},{2,1},{1,2},{0,3},{7,4},{6,5},{5,6},{4,7},{11,8},{10,9},{9,1... | collective-permute-start | bytes 82952 | tf_op jit(solution)/shard_map/ppermute | solution.py:455
  20.5 30.9 %collective-permute-start.3 = (bf16[3,3,11,512]{3,1,2,0:T(4,128)(2,1)S(1)}, bf16[3,3,11,512]{3,1,2,0:T(4,128)(2,1)S(1)}, u32[]{:S(2)}, u32[]{:S(2)}) collective-permute-start(bf16[3,3,11,512]{3,1,2,0:T(4,128)(2,1)S(1)} %slice.211), channel_id=1, source_target_pairs={{2,0},{0,2},{3,1},{1,3},{6,4},{4,6},{7,5},{5,7},{10,8},{8,10},{11,... | collective-permute-start | bytes 304136 | tf_op jit(solution)/shard_map/ppermute | solution.py:445
  21.9 7.8 %copy-start.6 = (f32[64]{0:T(128)S(1)}, f32[64]{0:T(128)}, u32[]{:S(2)}) copy-start(f32[64]{0:T(128)} %param.19) | copy-start | bytes 772
  21.9 7.8 %copy-start.7 = (f32[64]{0:T(128)S(1)}, f32[64]{0:T(128)}, u32[]{:S(2)}) copy-start(f32[64]{0:T(128)} %param.20) | copy-start | bytes 772
  21.9 7.8 %copy-start.8 = (f32[64]{0:T(128)S(1)}, f32[64]{0:T(128)}, u32[]{:S(2)}) copy-start(f32[64]{0:T(128)} %param.22) | copy-start | bytes 772
  21.9 7.9 %copy-start.9 = (f32[64]{0:T(128)S(1)}, f32[64]{0:T(128)}, u32[]{:S(2)}) copy-start(f32[64]{0:T(128)} %param.23) | copy-start | bytes 772
  21.9 7.9 %copy-start.10 = (f32[64]{0:T(128)S(1)}, f32[64]{0:T(128)}, u32[]{:S(2)}) copy-start(f32[64]{0:T(128)} %param.26) | copy-start | bytes 772
  21.9 7.9 %copy-start.11 = (f32[64]{0:T(128)S(1)}, f32[64]{0:T(128)}, u32[]{:S(2)}) copy-start(f32[64]{0:T(128)} %param.27) | copy-start | bytes 772
  21.9 7.9 %copy-start.12 = (f32[64]{0:T(128)S(1)}, f32[64]{0:T(128)}, u32[]{:S(2)}) copy-start(f32[64]{0:T(128)} %param.28) | copy-start | bytes 772
  21.9 7.9 %copy-start.5 = (f32[256]{0:T(256)S(1)}, f32[256]{0:T(256)}, u32[]{:S(2)}) copy-start(f32[256]{0:T(256)} %param.30) | copy-start | bytes 3076
  21.9 7.9 %copy-start.13 = (f32[64]{0:T(128)S(1)}, f32[64]{0:T(128)}, u32[]{:S(2)}) copy-start(f32[64]{0:T(128)} %param.32) | copy-start | bytes 772
  21.9 7.9 %copy-start.4 = (f32[2,169]{1,0:T(2,128)S(1)}, f32[2,169]{1,0:T(2,128)}, u32[]{:S(2)}) copy-start(f32[2,169]{1,0:T(2,128)} %param.24) | copy-start | bytes 4060
  22.0 23.0 %copy-start.3 = (s32[49,49]{1,0:T(8,128)S(1)}, s32[49,49]{1,0:T(8,128)}, u32[]{:S(2)}) copy-start(s32[49,49]{1,0:T(8,128)} %param.18) | copy-start | bytes 28816
  22.0 35.6 %collective-permute-start.5 = (bf16[3,3,56,512]{3,2,1,0:T(8,128)(2,1)}, bf16[3,3,56,512]{3,2,1,0:T(8,128)(2,1)}, u32[]{:S(2)}, u32[]{:S(2)}) collective-permute-start(bf16[3,3,56,512]{3,2,1,0:T(8,128)(2,1)} %slice.213), channel_id=1, source_target_pairs={{1,0},{0,1},{3,2},{2,3},{5,4},{4,5},{7,6},{6,7},{9,8},{8,9},{11,10... | collective-permute-start | bytes 1548296 | tf_op jit(solution)/shard_map/ppermute | solution.py:445
  25.5 26.8 %collective-permute-start.1 = (bf16[3,3,3,512]{3,1,2,0:T(4,128)(2,1)}, bf16[3,3,3,512]{3,1,2,0:T(4,128)(2,1)S(1)}, u32[]{:S(2)}, u32[]{:S(2)}) collective-permute-start(bf16[3,3,3,512]{3,1,2,0:T(4,128)(2,1)} %slice.208), channel_id=1, source_target_pairs={{3,0},{2,1},{1,2},{0,3},{7,4},{6,5},{5,6},{4,7},{11,8},{10,9},{9,1... | collective-permute-start | bytes 82952 | tf_op jit(solution)/shard_map/ppermute | solution.py:455
  29.2 30.5 %collective-permute-start.2 = (bf16[3,3,56,512]{3,2,1,0:T(8,128)(2,1)}, bf16[3,3,56,512]{3,2,1,0:T(8,128)(2,1)}, u32[]{:S(2)}, u32[]{:S(2)}) collective-permute-start(bf16[3,3,56,512]{3,2,1,0:T(8,128)(2,1)} %slice.209), channel_id=1, source_target_pairs={{1,0},{0,1},{3,2},{2,3},{5,4},{4,5},{7,6},{6,7},{9,8},{8,9},{11,10... | collective-permute-start | bytes 1548296 | tf_op jit(solution)/shard_map/ppermute | solution.py:445
  50.8 5.8 %collective-permute-start = (bf16[3,3,11,512]{3,1,2,0:T(4,128)(2,1)S(1)}, bf16[3,3,11,512]{3,1,2,0:T(4,128)(2,1)S(1)}, u32[]{:S(2)}, u32[]{:S(2)}) collective-permute-start(bf16[3,3,11,512]{3,1,2,0:T(4,128)(2,1)S(1)} %slice.207), channel_id=1, source_target_pairs={{2,0},{0,2},{3,1},{1,3},{6,4},{4,6},{7,5},{5,7},{10,8},{8,10},{11,... | collective-permute-start | bytes 304136 | tf_op jit(solution)/shard_map/ppermute | solution.py:445
  211.6 96.5 %reduce-scatter.5.cloned.1.call-start = ((), (), s32[]{:S(2)}) async-start(), calls=%async_computation.5 | async-start | bytes 5898240 | tf_op jit(solution)/shard_map/reduce_scatter | solution.py:720
  248.8 23.2 %collective-permute-start.14 = (bf16[80,768]{1,0:T(8,128)(2,1)S(1)}, bf16[80,768]{1,0:T(8,128)(2,1)S(1)}, u32[]{:S(2)}, u32[]{:S(2)}) collective-permute-start(bf16[80,768]{1,0:T(8,128)(2,1)S(1)} %get-tuple-element.80), channel_id=1, source_target_pairs={{1,0},{0,1},{3,2},{2,3},{5,4},{4,5},{7,6},{6,7},{9,8},{8,9},{11,10... | collective-permute-start | bytes 368648 | tf_op jit(solution)/shard_map/ppermute | solution.py:445
  250.1 24.8 %collective-permute-start.12 = (bf16[80,768]{1,0:T(8,128)(2,1)S(1)}, bf16[80,768]{1,0:T(8,128)(2,1)S(1)}, u32[]{:S(2)}, u32[]{:S(2)}) collective-permute-start(bf16[80,768]{1,0:T(8,128)(2,1)S(1)} %get-tuple-element.81), channel_id=1, source_target_pairs={{2,0},{0,2},{3,1},{1,3},{6,4},{4,6},{7,5},{5,7},{10,8},{8,10},{11,... | collective-permute-start | bytes 368648 | tf_op jit(solution)/shard_map/ppermute | solution.py:445
  251.9 16.7 %copy-start = (f32[3,3,56,512]{3,2,1,0:T(8,128)S(1)}, f32[3,3,56,512]{3,2,1,0:T(8,128)}, u32[]{:S(2)}) copy-start(f32[3,3,56,512]{3,2,1,0:T(8,128)} %get-tuple-element.36) | copy-start | bytes 3096580
  251.9 18.9 %copy-start.2 = (f32[3,3,14,512]{3,2,1,0:T(8,128)S(1)}, f32[3,3,14,512]{3,2,1,0:T(8,128)}, u32[]{:S(2)}) copy-start(f32[3,3,14,512]{3,2,1,0:T(8,128)} %get-tuple-element.37) | copy-start | bytes 774148
  267.1 7.8 %copy-start.1 = (bf16[1,80,1536]{2,1,0:T(8,128)(2,1)S(1)}, bf16[1,80,1536]{2,1,0:T(8,128)(2,1)}, u32[]{:S(2)}) copy-start(bf16[1,80,1536]{2,1,0:T(8,128)(2,1)} %reduce-scatter.3.cloned.1.call-done) | copy-start | bytes 737284
  268.5 15.5 %collective-permute-start.9 = (bf16[3,3,56,512]{3,2,1,0:T(8,128)(2,1)S(1)}, bf16[3,3,56,512]{3,2,1,0:T(8,128)(2,1)S(1)}, u32[]{:S(2)}, u32[]{:S(2)}) collective-permute-start(bf16[3,3,56,512]{3,2,1,0:T(8,128)(2,1)S(1)} %convert_element_type.178), channel_id=1, source_target_pairs={{1,0},{0,1},{3,2},{2,3},{5,4},{4,5},{7,6},{6,7},{9,8},{8,9},{11,10... | collective-permute-start | bytes 1548296 | tf_op jit(solution)/shard_map/ppermute | solution.py:445
  268.6 23.1 %collective-permute-start.6 = (bf16[3,3,56,512]{3,2,1,0:T(8,128)(2,1)S(1)}, bf16[3,3,56,512]{3,2,1,0:T(8,128)(2,1)S(1)}, u32[]{:S(2)}, u32[]{:S(2)}) collective-permute-start(bf16[3,3,56,512]{3,2,1,0:T(8,128)(2,1)S(1)} %convert_element_type.175), channel_id=1, source_target_pairs={{1,0},{0,1},{3,2},{2,3},{5,4},{4,5},{7,6},{6,7},{9,8},{8,9},{11,10... | collective-permute-start | bytes 1548296 | tf_op jit(solution)/shard_map/ppermute | solution.py:445
  270.8 9.7 %collective-permute-start.7 = (bf16[3,3,3,512]{3,2,1,0:T(4,128)(2,1)S(1)}, bf16[3,3,3,512]{3,2,1,0:T(4,128)(2,1)S(1)}, u32[]{:S(2)}, u32[]{:S(2)}) collective-permute-start(bf16[3,3,3,512]{3,2,1,0:T(4,128)(2,1)S(1)} %slice.221), channel_id=1, source_target_pairs={{3,0},{2,1},{1,2},{0,3},{7,4},{6,5},{5,6},{4,7},{11,8},{10,9},{9,1... | collective-permute-start | bytes 82952 | tf_op jit(solution)/shard_map/ppermute | solution.py:455
  271.9 5.3 %collective-permute-start.10 = (bf16[3,3,3,512]{3,2,1,0:T(4,128)(2,1)S(1)}, bf16[3,3,3,512]{3,2,1,0:T(4,128)(2,1)S(1)}, u32[]{:S(2)}, u32[]{:S(2)}) collective-permute-start(bf16[3,3,3,512]{3,2,1,0:T(4,128)(2,1)S(1)} %slice.223), channel_id=1, source_target_pairs={{3,0},{2,1},{1,2},{0,3},{7,4},{6,5},{5,6},{4,7},{11,8},{10,9},{9,1... | collective-permute-start | bytes 82952 | tf_op jit(solution)/shard_map/ppermute | solution.py:455
  274.9 5.1 %collective-permute-start.11 = (bf16[3,3,11,512]{3,2,1,0:T(8,128)(2,1)S(1)}, bf16[3,3,11,512]{3,2,1,0:T(8,128)(2,1)S(1)}, u32[]{:S(2)}, u32[]{:S(2)}) collective-permute-start(bf16[3,3,11,512]{3,2,1,0:T(8,128)(2,1)S(1)} %bitcast.69), channel_id=1, source_target_pairs={{2,0},{0,2},{3,1},{1,3},{6,4},{4,6},{7,5},{5,7},{10,8},{8,10},{11,... | collective-permute-start | bytes 304136 | tf_op jit(solution)/shard_map/ppermute | solution.py:445
  277.3 5.1 %collective-permute-start.8 = (bf16[3,3,11,512]{3,2,1,0:T(8,128)(2,1)S(1)}, bf16[3,3,11,512]{3,2,1,0:T(8,128)(2,1)S(1)}, u32[]{:S(2)}, u32[]{:S(2)}) collective-permute-start(bf16[3,3,11,512]{3,2,1,0:T(8,128)(2,1)S(1)} %bitcast.68), channel_id=1, source_target_pairs={{2,0},{0,2},{3,1},{1,3},{6,4},{4,6},{7,5},{5,7},{10,8},{8,10},{11,... | collective-permute-start | bytes 304136 | tf_op jit(solution)/shard_map/ppermute | solution.py:445
  280.1 14.7 %collective-permute-start.13 = (bf16[80,768]{1,0:T(8,128)(2,1)S(1)}, bf16[80,768]{1,0:T(8,128)(2,1)S(1)}, u32[]{:S(2)}, u32[]{:S(2)}) collective-permute-start(bf16[80,768]{1,0:T(8,128)(2,1)S(1)} %get-tuple-element.79), channel_id=1, source_target_pairs={{1,0},{0,1},{3,2},{2,3},{5,4},{4,5},{7,6},{6,7},{9,8},{8,9},{11,10... | collective-permute-start | bytes 368648 | tf_op jit(solution)/shard_map/ppermute | solution.py:445
  293.9 20.1 %collective-permute-start.15 = (bf16[80,768]{1,0:T(8,128)(2,1)S(1)}, bf16[80,768]{1,0:T(8,128)(2,1)S(1)}, u32[]{:S(2)}, u32[]{:S(2)}) collective-permute-start(bf16[80,768]{1,0:T(8,128)(2,1)S(1)} %get-tuple-element.78), channel_id=1, source_target_pairs={{2,0},{0,2},{3,1},{1,3},{6,4},{4,6},{7,5},{5,7},{10,8},{8,10},{11,... | collective-permute-start | bytes 368648 | tf_op jit(solution)/shard_map/ppermute | solution.py:445
  309.2 7.6 %collective-permute-start.16 = (bf16[160,1024]{1,0:T(8,128)(2,1)S(1)}, bf16[160,1024]{1,0:T(8,128)(2,1)S(1)}, u32[]{:S(2)}, u32[]{:S(2)}) collective-permute-start(bf16[160,1024]{1,0:T(8,128)(2,1)S(1)} %get-tuple-element.62), channel_id=1, source_target_pairs={{2,0},{0,2},{3,1},{1,3},{6,4},{4,6},{7,5},{5,7},{10,8},{8,10},{11,... | collective-permute-start | bytes 983048 | tf_op jit(solution)/shard_map/ppermute | solution.py:445
  310.7 7.3 %collective-permute-start.18 = (bf16[160,1024]{1,0:T(8,128)(2,1)S(1)}, bf16[160,1024]{1,0:T(8,128)(2,1)S(1)}, u32[]{:S(2)}, u32[]{:S(2)}) collective-permute-start(bf16[160,1024]{1,0:T(8,128)(2,1)S(1)} %get-tuple-element.63), channel_id=1, source_target_pairs={{1,0},{0,1},{3,2},{2,3},{5,4},{4,5},{7,6},{6,7},{9,8},{8,9},{11,10... | collective-permute-start | bytes 983048 | tf_op jit(solution)/shard_map/ppermute | solution.py:445
  319.4 7.1 %collective-permute-start.17 = (bf16[160,1024]{1,0:T(8,128)(2,1)S(1)}, bf16[160,1024]{1,0:T(8,128)(2,1)S(1)}, u32[]{:S(2)}, u32[]{:S(2)}) collective-permute-start(bf16[160,1024]{1,0:T(8,128)(2,1)S(1)} %get-tuple-element.60), channel_id=1, source_target_pairs={{1,0},{0,1},{3,2},{2,3},{5,4},{4,5},{7,6},{6,7},{9,8},{8,9},{11,10... | collective-permute-start | bytes 983048 | tf_op jit(solution)/shard_map/ppermute | solution.py:445
  322.2 7.1 %collective-permute-start.19 = (bf16[160,1024]{1,0:T(8,128)(2,1)S(1)}, bf16[160,1024]{1,0:T(8,128)(2,1)S(1)}, u32[]{:S(2)}, u32[]{:S(2)}) collective-permute-start(bf16[160,1024]{1,0:T(8,128)(2,1)S(1)} %get-tuple-element.61), channel_id=1, source_target_pairs={{2,0},{0,2},{3,1},{1,3},{6,4},{4,6},{7,5},{5,7},{10,8},{8,10},{11,... | collective-permute-start | bytes 983048 | tf_op jit(solution)/shard_map/ppermute | solution.py:445
Sparse Core Ops, SparseCore 0:
  10.0 32.1 all-gather.4
  44.4 46.2 all-gather.6
  211.7 36.0 reduce-scatter.2
  249.9 58.0 reduce-scatter.4
where the time goes:
time: 340 us; the launch traced here: 338 us
  Pallas kernels  169 us (50%)
  waiting for transfers between devices  75.8 us (22%)
  starting transfers between devices  24.7 us (7%)
  other arithmetic  24 us (7%)
  blocking collectives  14.5 us (4%)
  between operations  14.4 us (4%)
  local copies, waits for them, and re-layouts  12.3 us (4%)
  matrix products  3.4 us (1%)
    pallas_call x1, Pallas kernels, body(): pl.pallas_call(mlp_kernel, grid=grid, in_specs=[tile_spec, row_spec, col_...  57.8 us
    pallas_call x1, Pallas kernels, body(): pl.pallas_call(functools.partial(back_kernel, head_size), grid=grid, in_s...  48 us
    pallas_call x1, Pallas kernels, body(): pl.pallas_call(functools.partial(attend_kernel, head_size), grid=grid, in...  43.9 us
    reduce_scatter x1, waiting for transfers between devices, body(): lax.psum_scatter(pack_one, 'dp', scatter_dimension=0, tiled=True)[0]  35.6 us
    ppermute x16, waiting for transfers between devices, shifted(): lax.ppermute(block, axis, [((i - distance) % count, i) for i in range(cou...  24.3 us
    pallas_call x1, Pallas kernels, body(): pl.pallas_call(close_kernel, grid=grid, in_specs=[joint_spec, flat_spec,...  15.2 us
    ppermute x16, starting transfers between devices, shifted(): lax.ppermute(block, axis, [((i - distance) % count, i) for i in range(cou...  14.6 us
    all_gather x1, blocking collectives, body(): small = lax.all_gather(small, 'dp', axis=0, tiled=True)  14.5 us
  transfers between devices with their start and end apart: 24, of which 12 were waited for; matrix products, arithmetic and copies ran while one was open for 10% of the time, Pallas kernels for 19%

commit v1 on v0

--- a/solution.py
+++ b/solution.py
@@ -55,7 +55,16 @@
     return ((2 * band + col // WIN) * WIN + col % WIN) * PAD
 
 
-def extract(half, tile_ref, row_ref, col_ref, out_ref):
+def widen(half, row_ref, corner_ref, col_ref, rows_ref, cols_ref):
+    @pl.when(half == 0)
+    def _():
+        own = row_ref.shape[2]
+        rows_ref[:, 0:own, :] = row_ref[0].astype(F32)
+        rows_ref[:, own : own + SHIFT, :] = corner_ref[0].astype(F32)
+        cols_ref[...] = col_ref[0].astype(F32)
+
+
+def extract(half, tile_ref, rows_ref, cols_ref, out_ref):
     _, breadth, height, features = tile_ref.shape
     zero = jnp.zeros((1, features), F32)
     for band in range(BANDS):
@@ -76,11 +85,11 @@
                     out_ref[at : at + count, :] = (
                         tile_ref[0, col + SHIFT, rows, :]
                         if local
-                        else col_ref[0, col + SHIFT - breadth, rows, :]
+                        else cols_ref[col + SHIFT - breadth, rows, :]
                     )
                     for j in range(WIN - count):
-                        out_ref[at + count + j : at + count + j + 1, :] = row_ref[
-                            0, j, col : col + 1, :
+                        out_ref[at + count + j : at + count + j + 1, :] = rows_ref[
+                            j, col : col + 1, :
                         ]
 
 
@@ -139,6 +148,7 @@
     head_size,
     tile_ref,
     row_ref,
+    corner_ref,
     col_ref,
     weight_ref,
     vec_ref,
@@ -150,10 +160,13 @@
     att_ref,
     mid_ref,
     wide_ref,
+    rows_ref,
+    cols_ref,
 ):
     half = pl.program_id(1)
     features = tile_ref.shape[-1]
-    extract(half, tile_ref, row_ref, col_ref, xp_ref)
+    widen(half, row_ref, corner_ref, col_ref, rows_ref, cols_ref)
+    extract(half, tile_ref, rows_ref, cols_ref, xp_ref)
     normed, _ = norm_parts(xp_ref[...])
     hidden = (normed * vec_ref[0:1, :] + vec_ref[1:2, :]).astype(BF)
     hid_ref[...] = hidden
@@ -196,6 +209,7 @@
 def mlp_kernel(
     tile_ref,
     row_ref,
+    corner_ref,
     col_ref,
     mid_ref,
     att_ref,
@@ -209,6 +223,8 @@
     gmid_ref,
     gatt_ref,
     pack_ref,
+    sums_ref,
+    esum_ref,
     cot_ref,
     we_ref,
     ws_ref,
@@ -216,8 +232,8 @@
     gs_ref,
     go_ref,
     out_ref,
-    sums_ref,
-    esum_ref,
+    rows_ref,
+    cols_ref,
 ):
     half = pl.program_id(1)
     step = pl.program_id(0) * pl.num_programs(1) + half
@@ -243,7 +259,8 @@
         sums_ref[...] = jnp.zeros_like(sums_ref)
         esum_ref[...] = jnp.zeros_like(esum_ref)
 
-    extract(half, tile_ref, row_ref, col_ref, cot_ref)
+    widen(half, row_ref, corner_ref, col_ref, rows_ref, cols_ref)
+    extract(half, tile_ref, rows_ref, cols_ref, cot_ref)
     mid = mid_ref[...]
     normed, inverse = norm_parts(mid)
     hidden = (normed * vec_ref[5:6, :] + vec_ref[6:7, :]).astype(BF)
@@ -283,14 +300,8 @@
 
     @pl.when(step == steps - 1)
     def _():
-        even = hidden_units // shards
-        base = 2 * deep + LINES
-        pack_ref[:, 2 * deep : base, :] = jnp.zeros((shards, LINES, hidden_units), BF)
+        base = 2 * deep
         for d in range(shards):
-            pack_ref[d, 2 * deep : base, 0:deep] = sums_ref[:, d * deep : (d + 1) * deep].astype(BF)
-            pack_ref[d, 2 * deep : base, features : features + even] = esum_ref[
-                :, d * even : (d + 1) * even
-            ].astype(BF)
             pack_ref[d, 0:deep, :] = ge_ref[d * deep : (d + 1) * deep, :].astype(BF)
             for j in range(blocks):
                 at = d * deep * blocks + j * deep
@@ -320,6 +331,8 @@
     gatt_ref,
     weight_ref,
     vec_ref,
+    sums_two_ref,
+    esum_ref,
     gact_ref,
     pack_ref,
     acc_ref,
@@ -396,15 +409,20 @@
         )
         for d in range(shards):
             pack_ref[d, 0:deep, :] = acc_ref[d * deep : (d + 1) * deep, :].astype(BF)
-            pack_ref[d, deep : deep + LINES, 4 * lanes + deep :] = jnp.zeros(
-                (LINES, 3 * features - 4 * lanes - deep), BF
-            )
+            pack_ref[d, deep : deep + LINES, :] = jnp.zeros((LINES, 3 * features), BF)
             for j in range(4):
                 pack_ref[d, deep : deep + LINES, j * lanes : (j + 1) * lanes] = table_ref[
                     j * LINES : (j + 1) * LINES, d * lanes : (d + 1) * lanes
                 ].astype(BF)
-            pack_ref[d, deep : deep + LINES, 4 * lanes : 4 * lanes + deep] = lines[
-                :, d * deep : (d + 1) * deep
+            own = slice(d * deep, (d + 1) * deep)
+            at = features
+            pack_ref[d, deep : deep + LINES, at : at + deep] = lines[:, own].astype(BF)
+            at = features + features // 2
+            pack_ref[d, deep : deep + LINES, at : at + deep] = sums_two_ref[:, own].astype(BF)
+            at = 2 * features
+            even = esum_ref.shape[1] // shards
+            pack_ref[d, deep : deep + LINES, at : at + even] = esum_ref[
+                :, d * even : (d + 1) * even
             ].astype(BF)
 
 
@@ -455,12 +473,62 @@
     return lax.ppermute(block, ("row", "col"), route)
 
 
-def roll_in(values):
-    cols = shifted(values[:, :SHIFT].astype(BF), "col", -1)
-    top = values[:, :, :SHIFT].astype(BF).transpose(0, 2, 1, 3)
-    rows = shifted(top[:, :, SHIFT:], "row", -1)
-    corner = slanted(top[:, :, :SHIFT], -1)
-    return jnp.concatenate([rows, corner], axis=2).astype(F32), cols.astype(F32)
+def edge_kernel(first_ref, second_ref, row_ref, corner_ref, col_ref, flank, top, tidy, small, sems):
+    tiles = (first_ref, second_ref)
+    images, breadth = first_ref.shape[:2]
+    copies = []
+    for t, tile in enumerate(tiles):
+        span = slice(t * images, (t + 1) * images)
+        copies.append(
+            pltpu.make_async_copy(tile.at[:, :, 0:PAD], top.at[span], sems.at[2 * t])
+        )
+        copies.append(
+            pltpu.make_async_copy(tile.at[:, 0:SHIFT], flank.at[span], sems.at[2 * t + 1])
+        )
+    for copy in copies:
+        copy.start()
+    for t in range(2):
+        span = slice(t * images, (t + 1) * images)
+        copies[2 * t].wait()
+        for i in range(t * images, (t + 1) * images):
+            for c in range(breadth):
+                for j in range(SHIFT):
+                    if c < SHIFT:
+                        small[i, j, c : c + 1, :] = top[i, c, j : j + 1, :]
+                    else:
+                        tidy[i, j, c - SHIFT : c - SHIFT + 1, :] = top[i, c, j : j + 1, :]
+        copies[2 * t + 1].wait()
+        col_ref[span] = flank[span].astype(BF)
+    row_ref[...] = tidy[...].astype(BF)
+    corner_ref[...] = small[...].astype(BF)
+
+
+def roll_in(first, second):
+    images, breadth, height, features = first.shape
+    both = 2 * images
+    vmem = pl.BlockSpec(memory_space=pltpu.VMEM)
+    shapes = (
+        (both, SHIFT, breadth - SHIFT, features),
+        (both, SHIFT, SHIFT, features),
+        (both, SHIFT, height, features),
+    )
+    row, corner, col = pl.pallas_call(
+        edge_kernel,
+        in_specs=[pl.BlockSpec(memory_space=pl.ANY)] * 2,
+        out_specs=[vmem] * 3,
+        out_shape=[jax.ShapeDtypeStruct(s, BF) for s in shapes],
+        scratch_shapes=[
+            pltpu.VMEM(shapes[2], F32),
+            pltpu.VMEM((both, breadth, PAD, features), F32),
+            pltpu.VMEM(shapes[0], F32),
+            pltpu.VMEM(shapes[1], F32),
+            pltpu.SemaphoreType.DMA((4,)),
+        ],
+        compiler_params=pltpu.CompilerParams(vmem_limit_bytes=24 * 1024 * 1024),
+        cost_estimate=pl.CostEstimate(flops=0, bytes_accessed=5_000_000, transcendentals=0),
+        name="edge",
+    )(first, second)
+    return shifted(row, "row", -1), slanted(corner, -1), shifted(col, "col", -1)
 
 
 def roll_out(tile, rows, cols):
@@ -577,8 +645,7 @@
     )
 
     tokens, cotangent = tokens.transpose(0, 2, 1, 3), cotangent.transpose(0, 2, 1, 3)
-    tok_row, tok_col = roll_in(tokens)
-    cot_row, cot_col = roll_in(cotangent)
+    halo = roll_in(tokens, cotangent)
 
     paired = position_index.reshape(WIN, WIN, WIN, WIN)
     paired = paired.transpose(1, 0, 3, 2)
@@ -606,6 +673,14 @@
     bias = (position[None, None] + masking[:, :, :, None, :]).reshape(2, 2, WT, wide)
 
     tile_spec = pl.BlockSpec((1, breadth, height, features), lambda i, j: (i, 0, 0, 0))
+
+    def halo_specs(first):
+        sizes = (breadth - SHIFT, SHIFT, height)
+        return [
+            pl.BlockSpec((1, SHIFT, size, features), lambda i, j: (first + i, 0, 0, 0))
+            for size in sizes
+        ]
+
     row_spec = pl.BlockSpec((1, SHIFT, breadth, features), lambda i, j: (i, 0, 0, 0))
     col_spec = pl.BlockSpec((1, SHIFT, height, features), lambda i, j: (i, 0, 0, 0))
     flat_spec = pl.BlockSpec((step_rows, features), lambda i, j: (i * halves + j, 0))
@@ -619,6 +694,10 @@
         dimension_semantics=("arbitrary", "arbitrary"), vmem_limit_bytes=VMEM_LIMIT
     )
     shape = jax.ShapeDtypeStruct
+    halo_scratch = [
+        pltpu.VMEM((SHIFT, breadth, features), F32),
+        pltpu.VMEM((SHIFT, height, features), F32),
+    ]
     dense = 2 * total_rows * features * features
 
     xp, hidden_one, qkv, probs, attended, middle = pl.pallas_call(
@@ -626,8 +705,7 @@
         grid=grid,
         in_specs=[
             tile_spec,
-            row_spec,
-            col_spec,
+            *halo_specs(0),
             whole((features, 4 * features)),
             whole((8, features)),
             whole((2, 2, WT, wide)),
@@ -648,22 +726,21 @@
             shape((total_rows, features), BF),
             shape((total_rows, features), F32),
         ],
-        scratch_shapes=[pltpu.VMEM((step_rows, features), F32)],
+        scratch_shapes=[pltpu.VMEM((step_rows, features), F32), *halo_scratch],
         compiler_params=params,
         cost_estimate=pl.CostEstimate(
             flops=6 * dense, bytes_accessed=40_000_000, transcendentals=windows * WT * wide
         ),
         name="attend",
-    )(tokens, tok_row, tok_col, weight_one, vec, bias)
-
-    packed_rows = 2 * deep + deep // blocks + LINES
-    result, res_row, res_col, gmid, gatt, pack_two = pl.pallas_call(
+    )(tokens, *halo, weight_one, vec, bias)
+
+    packed_rows = 2 * deep + deep // blocks
+    result, res_row, res_col, gmid, gatt, pack_two, sums_two, esum = pl.pallas_call(
         mlp_kernel,
         grid=grid,
         in_specs=[
             tile_spec,
-            row_spec,
-            col_spec,
+            *halo_specs(images),
             flat_spec,
             flat_spec,
             whole((features, 4 * features)),
@@ -678,6 +755,8 @@
             flat_spec,
             window_spec(features),
             whole((shards, packed_rows, hidden_units)),
+            whole((LINES, features)),
+            whole((LINES, hidden_units)),
         ],
         out_shape=[
             shape(tokens.shape, F32),
@@ -686,6 +765,8 @@
             shape((total_rows, features), F32),
             shape((windows, WT, features), BF),
             shape((shards, packed_rows, hidden_units), BF),
+            shape((LINES, features), F32),
+            shape((LINES, hidden_units), F32),
         ],
         scratch_shapes=[
             pltpu.VMEM((step_rows, features), F32),
@@ -695,8 +776,7 @@
             pltpu.VMEM((features, hidden_units), F32),
             pltpu.VMEM((features, features), F32),
             pltpu.VMEM((step_rows, features), F32),
-            pltpu.VMEM((LINES, features), F32),
-            pltpu.VMEM((LINES, hidden_units), F32),
+            *halo_scratch,
         ],
         compiler_params=params,
         cost_estimate=pl.CostEstimate(
@@ -707,8 +787,7 @@
         name="mlp",
     )(
         cotangent,
-        cot_row,
-        cot_col,
+        *halo,
         middle,
         attended,
         weight_one,
@@ -730,6 +809,8 @@
             window_spec(features),
             whole((features, 4 * features)),
             whole((8, features)),
+            whole((LINES, features)),
+            whole((LINES, hidden_units)),
         ],
         out_specs=[joint_spec, whole((shards, deep + LINES, 3 * features))],
         out_shape=[
@@ -747,7 +828,7 @@
             flops=18 * dense, bytes_accessed=50_000_000, transcendentals=0
         ),
         name="back",
-    )(hidden_one, qkv, probs, gatt, weight_one, vec)
+    )(hidden_one, qkv, probs, gatt, weight_one, vec, sums_two, esum)
 
     pack_one = lax.psum_scatter(pack_one, "dp", scatter_dimension=0, tiled=True)[0]
 
@@ -777,21 +858,25 @@
     grad_tokens = roll_out(gtok, gtok_row, gtok_col)
 
     pack_two = over_tiles(pack_two)
+    pack_one, pack_two, final, grad_tokens = lax.optimization_barrier(
+        (pack_one, pack_two, final, grad_tokens)
+    )
     pack_one = over_tiles(pack_one)
     grad_expand = pack_two[:deep]
     grad_shrink = jnp.concatenate(
         [pack_two[deep : 2 * deep, j * features : (j + 1) * features] for j in range(blocks)],
         axis=0,
     )
-    base = 2 * deep + LINES
+    base = 2 * deep
     grad_output = jnp.concatenate(
         [pack_two[base:, j * features : (j + 1) * features] for j in range(blocks)], axis=0
     )
-    lines_two = pack_two[2 * deep : base, :deep]
-    grad_expand_bias = pack_two[2 * deep, features : features + blocks * deep]
     grad_joint = pack_one[:deep]
     lanes = table_heads * QL
-    lines_one = pack_one[deep:, 4 * lanes : 4 * lanes + deep]
+    lines_one = pack_one[deep:, features : features + deep]
+    at = features + features // 2
+    lines_two = pack_one[deep:, at : at + deep]
+    grad_expand_bias = pack_one[deep, 2 * features : 2 * features + blocks * deep]
     gtable = jnp.concatenate(
         [pack_one[deep:, j * lanes : (j + 1) * lanes] for j in range(4)], axis=0
     )[:WT]

time: 340 us -> 282 us (0.83)
  waiting for transfers between devices: 75.8 us -> 25.7 us
  other arithmetic: 24 us -> 14.9 us
  local copies, waits for them, and re-layouts: 12.3 us -> 17.1 us
  starting transfers between devices: 24.7 us -> 20.5 us
    reduce_scatter x1, waiting for transfers between devices: 35.6 us -> 0.02 us  [body(): lax.psum_scatter(pack_one, 'dp', scatter_dimension=0, tiled=True)[0]]
    ppermute x16 -> x14, waiting for transfers between devices: 24.3 us -> 15.9 us  [shifted(): lax.ppermute(block, axis, [((i - distance) % count, i) for i in range(cou...]
    reduce_scatter x1, waiting for transfers between devices: 13.1 us -> 5.73 us  [body(): lax.psum_scatter(pack_two, 'dp', scatter_dimension=0, tiled=True)[0]]
    another operation x5 -> x3, other arithmetic: 8.4 us -> 3.06 us
    unnamed x32 -> x40, local copies, waits for them, and re-layouts: 0.76 us -> 5.5 us
    convert_element_type x4 -> x0, other arithmetic: 4.5 us -> none  [the longest x2 4.29 us: roll_in(): cols.astype(F32)]
    ppermute x4 -> x3, starting transfers between devices: 9.88 us -> 6.73 us  [slanted(): return lax.ppermute(block, ('row', 'col'), route)]
    ppermute x16 -> x14, starting transfers between devices: 14.6 us -> 13.6 us  [shifted(): lax.ppermute(block, axis, [((i - distance) % count, i) for i in range(cou...]
  transfers between devices with their start and end apart: 24 -> 21, of which waited for: 12 -> 10; matrix products, arithmetic and copies ran while one was open for 10% -> 8% of each run, Pallas kernels for 19% -> 40%
where the time goes in v1:
time: 282 us; the launch traced here: 281 us
  Pallas kernels  169 us (60%)
  waiting for transfers between devices  25.7 us (9%)
  starting transfers between devices  20.5 us (7%)
  local copies, waits for them, and re-layouts  17.1 us (6%)
  blocking collectives  15 us (5%)
  other arithmetic  14.9 us (5%)
  between operations  14.4 us (5%)
  matrix products  4.41 us (2%)
    pallas_call x1, Pallas kernels, body(): pl.pallas_call(mlp_kernel, grid=grid, in_specs=[tile_spec, *halo_specs(im...  57.4 us
    pallas_call x1, Pallas kernels, body(): pl.pallas_call(functools.partial(back_kernel, head_size), grid=grid, in_s...  48 us
    pallas_call x1, Pallas kernels, body(): pl.pallas_call(functools.partial(attend_kernel, head_size), grid=grid, in...  43.9 us
    ppermute x14, waiting for transfers between devices, shifted(): lax.ppermute(block, axis, [((i - distance) % count, i) for i in range(cou...  15.9 us
    all_gather x1, blocking collectives, body(): small = lax.all_gather(small, 'dp', axis=0, tiled=True)  15 us
    pallas_call x1, Pallas kernels, body(): pl.pallas_call(close_kernel, grid=grid, in_specs=[joint_spec, flat_spec,...  15 us
    ppermute x14, starting transfers between devices, shifted(): lax.ppermute(block, axis, [((i - distance) % count, i) for i in range(cou...  13.6 us
    ppermute x3, starting transfers between devices, slanted(): return lax.ppermute(block, ('row', 'col'), route)  6.73 us
  transfers between devices with their start and end apart: 21, of which 10 were waited for; matrix products, arithmetic and copies ran while one was open for 8% of the time, Pallas kernels for 40%

profile of v1, /device:TPU:0, one launch (start us, length us, event | category | flops | bytes accessed | tf_op | source)
XLA Modules:
  0.0 281.2 jit_solution(15754928646534285303)
XLA Ops:
  7.2 1.0 convert.27
  8.2 1.0 convert.26
  9.2 0.7 pad_maximum_fusion.4
  10.0 1.1 convert.29
  11.2 0.8 pad_maximum_fusion.1
  12.1 2.4 copy-done
  14.5 2.4 copy-done.1
  17.6 4.0 %collective-permute-start.1 = (bf16[6,3,3,512]{3,2,1,0:T(4,128)(2,1)S(1)}, bf16[6,3,3,512]{3,2,1,0:T(4,128)(2,1)}, u32[]{:S(2)}, u32[]{:S(2)}) collective-permute-start(bf16[6,3,3,512]{3,2,1,0:T(4,128)(2,1)S(1)} %get-tuple-element.43), channel_id=1, source_target_pairs={{3,0},{2,1},{1,2},{0,3},{7,4},{6,5},{5,6},{4,7},{11,8},{10,9},{9,1... | collective-permute-start | bytes 165896 | tf_op jit(solution)/shard_map/ppermute | solution.py:473
  23.0 15.0 %all-gather.1 = bf16[8,1,1152]{2,1,0:T(2,128)(2,1)S(1)} all-gather(bf16[1,1,1152]{2,1,0:T(2,128)(2,1)S(1)} %reshape.175), channel_id=2, replica_groups=mesh['dp'=8,'row'=2,'col'=2] {'dp'}, dimensions={0}, use_global_device_ids=true | all-gather | bytes 20736 | tf_op jit(solution)/shard_map/all_gather | solution.py:630
  39.5 2.6 fusion.6
  42.5 1.4 add.136
  44.0 2.2 broadcast_add_fusion.bias_ref
  47.6 43.9 %attend.1 = (f32[2688,512]{1,0:T(8,128)}, bf16[2688,512]{1,0:T(8,128)(2,1)}, bf16[48,56,1536]{2,1,0:T(8,128)(2,1)}, bf16[48,56,1024]{2,1,0:T(8,128)(2,1)}, bf16[...) custom-call(f32[3,14,56,512]{3,2,1,0:T(8,128)} %bitcast.53, bf16[6,3,11,512]{3,2,1,0:T(8,128)(2,1)} %collective-permute-done.row_ref, ...), custom_call_target="tpu_custom_call" | custom-call | flops 8455716864 | bytes 40000000 | tf_op jit(solution)/shard_map/attend/pallas_call | solution.py:703
  91.5 57.4 %mlp.1 = (f32[3,14,56,512]{3,2,1,0:T(8,128)}, f32[3,3,14,512]{3,2,1,0:T(8,128)}, f32[3,3,56,512]{3,2,1,0:T(8,128)}, f32[2688,512]{1,0:T(8,128)}, bf16[48,56,512]...) custom-call(f32[3,14,56,512]{3,2,1,0:T(8,128)} %bitcast.55, ...), custom_call_target="tpu_custom_call" | custom-call | flops 36641439744 | bytes 50000000 | tf_op jit(solution)/shard_map/mlp/pallas_call | solution.py:738
  148.9 48.0 %back.1 = (bf16[2688,1536]{1,0:T(8,128)(2,1)}, bf16[8,80,1536]{2,1,0:T(8,128)(2,1)}) custom-call(bf16[2688,512]{1,0:T(8,128)(2,1)} %get-tuple-element.45.hid_ref, bf16[48,56,1536]{2,1,0:T(8,128)(2,1)} %get-tuple-element.46.qkv_ref, bf16[48,56,1024]{2,1,0:T(8,128)(2,1)} %get-tuple-element.47.prob_ref, bf16[48,56,512]{2,1,0:T(8,128)(2,1)} %get-tuple-element.50.gatt_ref, ...), custom_call_target="tpu_custom_call" | custom-call | flops 25367150592 | bytes 50000000 | tf_op jit(solution)/shard_map/back/pallas_call | solution.py:802
  197.7 1.5 collective-permute-start.9
  199.2 5.7 %reduce-scatter.5.cloned.1.call-done = bf16[1,144,2048]{2,1,0:T(8,128)(2,1)} async-done(((bf16[8,144,2048]{2,1,0:T(8,128)(2,1)}), bf16[1,144,2048]{2,1,0:T(8,128)(2,1)}) %reduce-scatter.5.cloned.1.call-update) | async-done | bytes 589840 | tf_op jit(solution)/shard_map/reduce_scatter | solution.py:799
  204.9 1.9 fusion.12
  206.8 1.6 collective-permute-start.3
  208.4 1.4 collective-permute-start.5
  209.8 15.0 %close.1 = (f32[3,14,56,512]{3,2,1,0:T(8,128)}, f32[3,3,14,512]{3,2,1,0:T(8,128)}, f32[3,3,56,512]{3,2,1,0:T(8,128)}) custom-call(bf16[2688,1536]{1,0:T(8,128)(2,1)} %get-tuple-element.58.gact_ref, f32[2688,512]{1,0:T(8,128)} %get-tuple-element.59.xp_ref, f32[2688,512]{1,0:T(8,128)} %get-tuple-element.60.gmid_ref, ...), custom_call_target="tpu_custom_call" | custom-call | flops 8455716864 | bytes 30000000 | tf_op jit(solution)/shard_map/close/pallas_call | solution.py:835
  224.8 1.3 convert_element_type.168
  226.7 1.6 collective-permute-start.10
  228.4 1.2 add_convert_fusion.1
  230.0 0.9 slice.179
  230.9 1.5 collective-permute-start.8
  232.4 0.8 eq.65
  233.2 2.9 %collective-permute-done.8 = bf16[3,3,3,512]{3,2,1,0:T(4,128)(2,1)S(1)} collective-permute-done((bf16[3,3,3,512]{3,2,1,0:T(4,128)(2,1)S(1)}, bf16[3,3,3,512]{3,2,1,0:T(4,128)(2,1)S(1)}, u32[]{:S(2)}, u32[]{:S(2)}) %collective-permute-start.8) | collective-permute-done | bytes 27680 | tf_op jit(solution)/shard_map/ppermute | solution.py:473
  236.1 1.3 collective-permute-start.11
  237.4 1.9 collective-permute-start.12
  239.3 1.0 maximum_convert_fusion.row_ref
  240.3 1.1 collective-permute-done.11
  241.9 1.4 collective-permute-done.12
  243.3 2.1 patch.2
  245.5 7.4 %collective-permute-done.10.col_ref = bf16[3,3,56,512]{3,2,1,0:T(8,128)(2,1)S(1)} collective-permute-done((bf16[3,3,56,512]{3,2,1,0:T(8,128)(2,1)S(1)}, bf16[3,3,56,512]{3,2,1,0:T(8,128)(2,1)S(1)}, u32[]{:S(2)}, u32[]{:S(2)}) %collective-permute-start.10) | collective-permute-done | bytes 516128 | tf_op jit(solution)/shard_map/ppermute | solution.py:463
  252.9 2.1 patch.3
  255.0 1.0 collective-permute-done.4
  256.4 1.0 fusion.15
  257.9 0.8 collective-permute-start.13
  258.8 0.8 slice.163
  260.3 2.0 collective-permute-done.15
  262.3 1.8 collective-permute-done.13
  264.1 1.0 add_convert_fusion.2
  265.7 0.8 pad_maximum_fusion.2
  266.5 1.5 collective-permute-start.14
  268.0 2.1 collective-permute-done.16
  271.9 0.8 pad_maximum_fusion.3
  272.9 1.8 fusion.3
  (130 shorter events, 11.9 us)
Async XLA Ops:
  7.2 4.0 %copy-start.4 = (f32[64,2048]{1,0:T(8,128)S(1)}, f32[64,2048]{1,0:T(8,128)}, u32[]{:S(2)}) copy-start(f32[64,2048]{1,0:T(8,128)} %param.29) | copy-start | bytes 1572868
  7.2 40.4 %all-gather.5.cloned.1.call-start = ((), (), s32[]{:S(2)}) async-start(), calls=%async_computation.2 | async-start | bytes 2359296 | tf_op jit(solution)/shard_map/all_gather | solution.py:637
  10.0 81.5 %all-gather.7.cloned.1.call-start = ((), (), s32[]{:S(2)}) async-start(), calls=%async_computation.3 | async-start | bytes 4718592 | tf_op jit(solution)/shard_map/all_gather | solution.py:643
  12.1 192.8 %reduce-scatter.5.cloned.1.call-start = ((), (), s32[]{:S(2)}) async-start(), calls=%async_computation.5 | async-start | bytes 5308416 | tf_op jit(solution)/shard_map/reduce_scatter | solution.py:799
  12.1 2.4 copy-start
  14.5 2.4 copy-start.1
  16.9 5.4 %copy-start.10 = (f32[64]{0:T(128)S(1)}, f32[64]{0:T(128)}, u32[]{:S(2)}) copy-start(f32[64]{0:T(128)} %param.19) | copy-start | bytes 772
  16.9 5.4 %copy-start.11 = (f32[64]{0:T(128)S(1)}, f32[64]{0:T(128)}, u32[]{:S(2)}) copy-start(f32[64]{0:T(128)} %param.20) | copy-start | bytes 772
  16.9 5.4 %copy-start.12 = (f32[64]{0:T(128)S(1)}, f32[64]{0:T(128)}, u32[]{:S(2)}) copy-start(f32[64]{0:T(128)} %param.22) | copy-start | bytes 772
  16.9 5.5 %copy-start.13 = (f32[64]{0:T(128)S(1)}, f32[64]{0:T(128)}, u32[]{:S(2)}) copy-start(f32[64]{0:T(128)} %param.23) | copy-start | bytes 772
  16.9 5.5 %copy-start.14 = (f32[64]{0:T(128)S(1)}, f32[64]{0:T(128)}, u32[]{:S(2)}) copy-start(f32[64]{0:T(128)} %param.26) | copy-start | bytes 772
  16.9 5.5 %copy-start.15 = (f32[64]{0:T(128)S(1)}, f32[64]{0:T(128)}, u32[]{:S(2)}) copy-start(f32[64]{0:T(128)} %param.27) | copy-start | bytes 772
  16.9 5.5 %copy-start.16 = (f32[64]{0:T(128)S(1)}, f32[64]{0:T(128)}, u32[]{:S(2)}) copy-start(f32[64]{0:T(128)} %param.28) | copy-start | bytes 772
  16.9 5.5 %copy-start.9 = (f32[256]{0:T(256)S(1)}, f32[256]{0:T(256)}, u32[]{:S(2)}) copy-start(f32[256]{0:T(256)} %param.30) | copy-start | bytes 3076
  16.9 5.5 %copy-start.17 = (f32[64]{0:T(128)S(1)}, f32[64]{0:T(128)}, u32[]{:S(2)}) copy-start(f32[64]{0:T(128)} %param.32) | copy-start | bytes 772
  16.9 5.5 %copy-start.8 = (f32[2,169]{1,0:T(2,128)S(1)}, f32[2,169]{1,0:T(2,128)}, u32[]{:S(2)}) copy-start(f32[2,169]{1,0:T(2,128)} %param.24) | copy-start | bytes 4060
  16.9 21.2 %copy-start.7 = (s32[49,49]{1,0:T(8,128)S(1)}, s32[49,49]{1,0:T(8,128)}, u32[]{:S(2)}) copy-start(s32[49,49]{1,0:T(8,128)} %param.18) | copy-start | bytes 28816
  17.6 29.9 %collective-permute-start.1 = (bf16[6,3,3,512]{3,2,1,0:T(4,128)(2,1)S(1)}, bf16[6,3,3,512]{3,2,1,0:T(4,128)(2,1)}, u32[]{:S(2)}, u32[]{:S(2)}) collective-permute-start(bf16[6,3,3,512]{3,2,1,0:T(4,128)(2,1)S(1)} %get-tuple-element.43), channel_id=1, source_target_pairs={{3,0},{2,1},{1,2},{0,3},{7,4},{6,5},{5,6},{4,7},{11,8},{10,9},{9,1... | collective-permute-start | bytes 165896 | tf_op jit(solution)/shard_map/ppermute | solution.py:473
  21.6 25.9 %collective-permute-start = (bf16[6,3,11,512]{3,2,1,0:T(8,128)(2,1)S(1)}, bf16[6,3,11,512]{3,2,1,0:T(8,128)(2,1)}, u32[]{:S(2)}, u32[]{:S(2)}) collective-permute-start(bf16[6,3,11,512]{3,2,1,0:T(8,128)(2,1)S(1)} %get-tuple-element.42), channel_id=1, source_target_pairs={{2,0},{0,2},{3,1},{1,3},{6,4},{4,6},{7,5},{5,7},{10,8},{8,10},{11,... | collective-permute-start | bytes 608264 | tf_op jit(solution)/shard_map/ppermute | solution.py:463
  22.2 25.4 %collective-permute-start.2 = (bf16[6,3,56,512]{3,2,1,0:T(8,128)(2,1)S(1)}, bf16[6,3,56,512]{3,2,1,0:T(8,128)(2,1)}, u32[]{:S(2)}, u32[]{:S(2)}) collective-permute-start(bf16[6,3,56,512]{3,2,1,0:T(8,128)(2,1)S(1)} %get-tuple-element.44), channel_id=1, source_target_pairs={{1,0},{0,1},{3,2},{2,3},{5,4},{4,5},{7,6},{6,7},{9,8},{8,9},{11,10... | collective-permute-start | bytes 3096584 | tf_op jit(solution)/shard_map/ppermute | solution.py:463
  148.9 107.5 %reduce-scatter.3.cloned.1.call-start = ((), (), s32[]{:S(2)}) async-start(), calls=%async_computation.4 | async-start | bytes 2211840 | tf_op jit(solution)/shard_map/reduce_scatter | solution.py:833
  148.9 48.1 %copy-start.6 = (f32[3,3,14,512]{3,2,1,0:T(8,128)S(1)}, f32[3,3,14,512]{3,2,1,0:T(8,128)}, u32[]{:S(2)}) copy-start(f32[3,3,14,512]{3,2,1,0:T(8,128)} %get-tuple-element.57) | copy-start | bytes 774148
  197.7 39.7 %collective-permute-start.9 = (bf16[3,3,11,512]{3,2,1,0:T(8,128)(2,1)}, bf16[3,3,11,512]{3,2,1,0:T(8,128)(2,1)}, u32[]{:S(2)}, u32[]{:S(2)}) collective-permute-start(bf16[3,3,11,512]{3,2,1,0:T(8,128)(2,1)} %bitcast.51), channel_id=1, source_target_pairs={{2,0},{0,2},{3,1},{1,3},{6,4},{4,6},{7,5},{5,7},{10,8},{8,10},{11,... | collective-permute-start | bytes 304136 | tf_op jit(solution)/shard_map/ppermute | solution.py:463
  206.8 21.5 %collective-permute-start.3 = (bf16[144,1024]{1,0:T(8,128)(2,1)}, bf16[144,1024]{1,0:T(8,128)(2,1)S(1)}, u32[]{:S(2)}, u32[]{:S(2)}) collective-permute-start(bf16[144,1024]{1,0:T(8,128)(2,1)} %get-tuple-element.78), channel_id=1, source_target_pairs={{2,0},{0,2},{3,1},{1,3},{6,4},{4,6},{7,5},{5,7},{10,8},{8,10},{11,... | collective-permute-start | bytes 884744 | tf_op jit(solution)/shard_map/ppermute | solution.py:463
  208.4 20.0 %collective-permute-start.5 = (bf16[144,1024]{1,0:T(8,128)(2,1)}, bf16[144,1024]{1,0:T(8,128)(2,1)}, u32[]{:S(2)}, u32[]{:S(2)}) collective-permute-start(bf16[144,1024]{1,0:T(8,128)(2,1)} %get-tuple-element.79), channel_id=1, source_target_pairs={{1,0},{0,1},{3,2},{2,3},{5,4},{4,5},{7,6},{6,7},{9,8},{8,9},{11,10... | collective-permute-start | bytes 884744 | tf_op jit(solution)/shard_map/ppermute | solution.py:463
  209.8 16.4 %copy-start.3 = (f32[3,3,56,512]{3,2,1,0:T(8,128)S(1)}, f32[3,3,56,512]{3,2,1,0:T(8,128)}, u32[]{:S(2)}) copy-start(f32[3,3,56,512]{3,2,1,0:T(8,128)} %get-tuple-element.56) | copy-start | bytes 3096580
  209.8 18.5 %copy-start.2 = (bf16[1,144,2048]{2,1,0:T(8,128)(2,1)S(1)}, bf16[1,144,2048]{2,1,0:T(8,128)(2,1)}, u32[]{:S(2)}) copy-start(bf16[1,144,2048]{2,1,0:T(8,128)(2,1)} %reduce-scatter.5.cloned.1.call-done) | copy-start | bytes 1769476
  224.8 8.4 %copy-start.5 = (f32[3,3,14,512]{3,2,1,0:T(8,128)S(1)}, f32[3,3,14,512]{3,2,1,0:T(8,128)}, u32[]{:S(2)}) copy-start(f32[3,3,14,512]{3,2,1,0:T(8,128)} %get-tuple-element.63) | copy-start | bytes 774148
  226.2 17.1 %collective-permute-start.7 = (bf16[3,3,56,512]{3,2,1,0:T(8,128)(2,1)S(1)}, bf16[3,3,56,512]{3,2,1,0:T(8,128)(2,1)S(1)}, u32[]{:S(2)}, u32[]{:S(2)}) collective-permute-start(bf16[3,3,56,512]{3,2,1,0:T(8,128)(2,1)S(1)} %convert_element_type.165), channel_id=1, source_target_pairs={{1,0},{0,1},{3,2},{2,3},{5,4},{4,5},{7,6},{6,7},{9,8},{8,9},{11,10... | collective-permute-start | bytes 1548296 | tf_op jit(solution)/shard_map/ppermute | solution.py:463
  226.7 26.2 %collective-permute-start.10 = (bf16[3,3,56,512]{3,2,1,0:T(8,128)(2,1)S(1)}, bf16[3,3,56,512]{3,2,1,0:T(8,128)(2,1)S(1)}, u32[]{:S(2)}, u32[]{:S(2)}) collective-permute-start(bf16[3,3,56,512]{3,2,1,0:T(8,128)(2,1)S(1)} %convert_element_type.168), channel_id=1, source_target_pairs={{1,0},{0,1},{3,2},{2,3},{5,4},{4,5},{7,6},{6,7},{9,8},{8,9},{11,10... | collective-permute-start | bytes 1548296 | tf_op jit(solution)/shard_map/ppermute | solution.py:463
  229.5 26.6 %collective-permute-start.4 = (bf16[144,1024]{1,0:T(8,128)(2,1)S(1)}, bf16[144,1024]{1,0:T(8,128)(2,1)S(1)}, u32[]{:S(2)}, u32[]{:S(2)}) collective-permute-start(bf16[144,1024]{1,0:T(8,128)(2,1)S(1)} %get-tuple-element.76), channel_id=1, source_target_pairs={{1,0},{0,1},{3,2},{2,3},{5,4},{4,5},{7,6},{6,7},{9,8},{8,9},{11,10... | collective-permute-start | bytes 884744 | tf_op jit(solution)/shard_map/ppermute | solution.py:463
  230.9 5.2 %collective-permute-start.8 = (bf16[3,3,3,512]{3,2,1,0:T(4,128)(2,1)S(1)}, bf16[3,3,3,512]{3,2,1,0:T(4,128)(2,1)S(1)}, u32[]{:S(2)}, u32[]{:S(2)}) collective-permute-start(bf16[3,3,3,512]{3,2,1,0:T(4,128)(2,1)S(1)} %slice.179), channel_id=1, source_target_pairs={{3,0},{2,1},{1,2},{0,3},{7,4},{6,5},{5,6},{4,7},{11,8},{10,9},{9,1... | collective-permute-start | bytes 82952 | tf_op jit(solution)/shard_map/ppermute | solution.py:473
  236.1 5.2 %collective-permute-start.11 = (bf16[3,3,3,512]{3,2,1,0:T(4,128)(2,1)S(1)}, bf16[3,3,3,512]{3,2,1,0:T(4,128)(2,1)S(1)}, u32[]{:S(2)}, u32[]{:S(2)}) collective-permute-start(bf16[3,3,3,512]{3,2,1,0:T(4,128)(2,1)S(1)} %slice.181), channel_id=1, source_target_pairs={{3,0},{2,1},{1,2},{0,3},{7,4},{6,5},{5,6},{4,7},{11,8},{10,9},{9,1... | collective-permute-start | bytes 82952 | tf_op jit(solution)/shard_map/ppermute | solution.py:473
  237.4 5.9 %collective-permute-start.12 = (bf16[3,3,11,512]{3,2,1,0:T(8,128)(2,1)S(1)}, bf16[3,3,11,512]{3,2,1,0:T(8,128)(2,1)S(1)}, u32[]{:S(2)}, u32[]{:S(2)}) collective-permute-start(bf16[3,3,11,512]{3,2,1,0:T(8,128)(2,1)S(1)} %bitcast.64), channel_id=1, source_target_pairs={{2,0},{0,2},{3,1},{1,3},{6,4},{4,6},{7,5},{5,7},{10,8},{8,10},{11,... | collective-permute-start | bytes 304136 | tf_op jit(solution)/shard_map/ppermute | solution.py:463
  241.4 14.8 %collective-permute-start.6 = (bf16[144,1024]{1,0:T(8,128)(2,1)S(1)}, bf16[144,1024]{1,0:T(8,128)(2,1)S(1)}, u32[]{:S(2)}, u32[]{:S(2)}) collective-permute-start(bf16[144,1024]{1,0:T(8,128)(2,1)S(1)} %get-tuple-element.77), channel_id=1, source_target_pairs={{2,0},{0,2},{3,1},{1,3},{6,4},{4,6},{7,5},{5,7},{10,8},{8,10},{11,... | collective-permute-start | bytes 884744 | tf_op jit(solution)/shard_map/ppermute | solution.py:463
  257.4 4.9 %collective-permute-start.15 = (bf16[80,768]{1,0:T(8,128)(2,1)S(1)}, bf16[80,768]{1,0:T(8,128)(2,1)S(1)}, u32[]{:S(2)}, u32[]{:S(2)}) collective-permute-start(bf16[80,768]{1,0:T(8,128)(2,1)S(1)} %get-tuple-element.98), channel_id=1, source_target_pairs={{1,0},{0,1},{3,2},{2,3},{5,4},{4,5},{7,6},{6,7},{9,8},{8,9},{11,10... | collective-permute-start | bytes 368648 | tf_op jit(solution)/shard_map/ppermute | solution.py:463
  257.9 6.2 %collective-permute-start.13 = (bf16[80,768]{1,0:T(8,128)(2,1)S(1)}, bf16[80,768]{1,0:T(8,128)(2,1)S(1)}, u32[]{:S(2)}, u32[]{:S(2)}) collective-permute-start(bf16[80,768]{1,0:T(8,128)(2,1)S(1)} %get-tuple-element.99), channel_id=1, source_target_pairs={{2,0},{0,2},{3,1},{1,3},{6,4},{4,6},{7,5},{5,7},{10,8},{8,10},{11,... | collective-permute-start | bytes 368648 | tf_op jit(solution)/shard_map/ppermute | solution.py:463
  265.2 4.9 %collective-permute-start.16 = (bf16[80,768]{1,0:T(8,128)(2,1)S(1)}, bf16[80,768]{1,0:T(8,128)(2,1)S(1)}, u32[]{:S(2)}, u32[]{:S(2)}) collective-permute-start(bf16[80,768]{1,0:T(8,128)(2,1)S(1)} %get-tuple-element.96), channel_id=1, source_target_pairs={{2,0},{0,2},{3,1},{1,3},{6,4},{4,6},{7,5},{5,7},{10,8},{8,10},{11,... | collective-permute-start | bytes 368648 | tf_op jit(solution)/shard_map/ppermute | solution.py:463
  266.5 4.9 %collective-permute-start.14 = (bf16[80,768]{1,0:T(8,128)(2,1)S(1)}, bf16[80,768]{1,0:T(8,128)(2,1)S(1)}, u32[]{:S(2)}, u32[]{:S(2)}) collective-permute-start(bf16[80,768]{1,0:T(8,128)(2,1)S(1)} %get-tuple-element.97), channel_id=1, source_target_pairs={{1,0},{0,1},{3,2},{2,3},{5,4},{4,5},{7,6},{6,7},{9,8},{8,9},{11,10... | collective-permute-start | bytes 368648 | tf_op jit(solution)/shard_map/ppermute | solution.py:463
Sparse Core Ops, SparseCore 0:
  10.2 32.1 all-gather.4
  44.5 46.2 all-gather.6
  149.0 55.8 reduce-scatter.4
  207.1 34.4 reduce-scatter.2

commit v2 on v1

--- a/solution.py
+++ b/solution.py
@@ -183,23 +183,39 @@
 
     group = 256
     span = group // head_size * QL
-    for w in range(2 * BANDS):
-        kind = w % 2
+    items = [(w, g) for w in range(2 * BANDS) for g in range(features // group)]
+
+    def scores(item):
+        w, g = item
+        q = qkv_ref[w, :, g * group : (g + 1) * group]
+        k = qkv_ref[w, :, features + g * group : features + (g + 1) * group]
+        return nt(k, spread(q, head_size, group))
+
+    def soften(item, raw):
+        w, g = item
         edge = jnp.where(half == 0, 0, 1) if w // 2 == BANDS - 1 else 0
-        for g in range(features // group):
-            q = qkv_ref[w, :, g * group : (g + 1) * group]
-            k = qkv_ref[w, :, features + g * group : features + (g + 1) * group]
-            raw = nt(k, spread(q, head_size, group))
-            score = raw * scale + bias_ref[edge, kind, :, g * span : (g + 1) * span]
-            highest = jnp.max(score, axis=0, keepdims=True)
-            grown = jnp.exp(score - highest)
-            total = jnp.sum(grown, axis=0, keepdims=True)
-            probs = (grown * (1.0 / total)).astype(BF)
-            prob_ref[w, :, g * span : (g + 1) * span] = probs
-            v = qkv_ref[w, :, 2 * features + g * group : 2 * features + (g + 1) * group]
-            wide_ref[w * WT : (w + 1) * WT, g * group : (g + 1) * group] = per_query(
-                probs, v, head_size
-            )
+        score = raw * scale + bias_ref[edge, w % 2, :, g * span : (g + 1) * span]
+        highest = jnp.max(score, axis=0, keepdims=True)
+        grown = jnp.exp(score - highest)
+        total = jnp.sum(grown, axis=0, keepdims=True)
+        prob_ref[w, :, g * span : (g + 1) * span] = (grown * (1.0 / total)).astype(BF)
+
+    def mix(item):
+        w, g = item
+        probs = prob_ref[w, :, g * span : (g + 1) * span]
+        v = qkv_ref[w, :, 2 * features + g * group : 2 * features + (g + 1) * group]
+        wide_ref[w * WT : (w + 1) * WT, g * group : (g + 1) * group] = per_query(
+            probs, v, head_size
+        )
+
+    raws = {}
+    for t in range(len(items) + 2):
+        if t < len(items):
+            raws[t] = scores(items[t])
+        if 1 <= t <= len(items):
+            soften(items[t - 1], raws.pop(t - 1))
+        if t >= 2:
+            mix(items[t - 2])
     attended = wide_ref[...].astype(BF)
     att_ref[...] = attended
     branch = nn(attended, weight_ref[:, 3 * features :]) + vec_ref[4:5, :]
@@ -339,6 +355,7 @@
     wide_ref,
     sums_ref,
     table_ref,
+    graw_ref,
 ):
     half = pl.program_id(1)
     step = pl.program_id(0) * pl.num_programs(1) + half
@@ -354,27 +371,47 @@
 
     group = 256
     span = group // head_size * QL
-    for w in range(2 * BANDS):
-        rows = slice(w * WT, (w + 1) * WT)
-        for g in range(features // group):
-            feats = slice(g * group, (g + 1) * group)
-            lanes = slice(g * span, (g + 1) * span)
-            q = qkv_ref[w, :, g * group : (g + 1) * group]
-            k = qkv_ref[w, :, features + g * group : features + (g + 1) * group]
-            v = qkv_ref[w, :, 2 * features + g * group : 2 * features + (g + 1) * group]
-            up = spread(gatt_ref[w, :, feats], head_size, group)
-            low = prob_ref[w, :, lanes]
-            probs = low.astype(F32)
-            gprobs = nt(v, up)
-            mean = jnp.sum(probs * gprobs, axis=0, keepdims=True)
-            gscore = probs * (gprobs - mean)
-            table_ref[0:WT, lanes] += gscore
-            graw = (gscore * scale).astype(BF)
-            wide_ref[rows, g * group : (g + 1) * group] = per_query(graw, k, head_size)
-            wide_ref[rows, features + g * group : features + (g + 1) * group] = nn(
-                graw, spread(q, head_size, group)
-            )
-            wide_ref[rows, 2 * features + g * group : 2 * features + (g + 1) * group] = nn(low, up)
+    items = [(w, g) for w in range(2 * BANDS) for g in range(features // group)]
+
+    def piece(item, part):
+        w, g = item
+        at = part * features + g * group
+        return qkv_ref[w, :, at : at + group]
+
+    def store(item, part, value):
+        w, g = item
+        at = part * features + g * group
+        wide_ref[w * WT : (w + 1) * WT, at : at + group] = value
+
+    def ascend(item):
+        w, g = item
+        lanes = slice(g * span, (g + 1) * span)
+        up = spread(gatt_ref[w, :, g * group : (g + 1) * group], head_size, group)
+        store(item, 2, nn(prob_ref[w, :, lanes], up))
+        return nt(piece(item, 2), up)
+
+    def soften(item, slot, gprobs):
+        w, g = item
+        lanes = slice(g * span, (g + 1) * span)
+        probs = prob_ref[w, :, lanes].astype(F32)
+        mean = jnp.sum(probs * gprobs, axis=0, keepdims=True)
+        gscore = probs * (gprobs - mean)
+        table_ref[0:WT, lanes] += gscore
+        graw_ref[slot] = (gscore * scale).astype(BF)
+
+    def descend(item, slot):
+        graw = graw_ref[slot]
+        store(item, 0, per_query(graw, piece(item, 1), head_size))
+        store(item, 1, nn(graw, spread(piece(item, 0), head_size, group)))
+
+    raws = {}
+    for t in range(len(items) + 2):
+        if t < len(items):
+            raws[t] = ascend(items[t])
+        if 1 <= t <= len(items):
+            soften(items[t - 1], (t - 1) % 4, raws.pop(t - 1))
+        if t >= 2:
+            descend(items[t - 2], (t - 2) % 4)
     gjoint = wide_ref[...]
     sums_ref[...] += jnp.sum(gjoint, axis=0, keepdims=True)
     gjoint = gjoint.astype(BF)
@@ -514,7 +551,7 @@
     )
     row, corner, col = pl.pallas_call(
         edge_kernel,
-        in_specs=[pl.BlockSpec(memory_space=pl.ANY)] * 2,
+        in_specs=[pl.BlockSpec(memory_space=pltpu.HBM)] * 2,
         out_specs=[vmem] * 3,
         out_shape=[jax.ShapeDtypeStruct(s, BF) for s in shapes],
         scratch_shapes=[
@@ -822,6 +859,7 @@
             pltpu.VMEM((step_rows, 3 * features), F32),
             pltpu.VMEM((1, 3 * features), F32),
             pltpu.VMEM((4 * LINES, wide), F32),
+            pltpu.VMEM((4, WT, 256 // head_size * QL), BF),
         ],
         compiler_params=params,
         cost_estimate=pl.CostEstimate(

time: 282 us -> 279 us (0.989)
  Pallas kernels: 169 us -> 134 us
  waiting for transfers between devices: 25.7 us -> 58.7 us
    pallas_call x1, Pallas kernels: 48 us -> 29.8 us  [body(): pl.pallas_call(functools.partial(back_kernel, head_size), grid=grid, in_s...]
    pallas_call x1, Pallas kernels: 43.9 us -> 26.8 us  [body(): pl.pallas_call(functools.partial(attend_kernel, head_size), grid=grid, in...]
    all_gather x1, waiting for transfers between devices: 0.02 us -> 16.4 us  [body(): lax.all_gather(jnp.concatenate([expand_weight, thick], axis=0).astype(BF)...]
    reduce_scatter x1, waiting for transfers between devices: 5.73 us -> 21.8 us  [body(): lax.psum_scatter(pack_two, 'dp', scatter_dimension=0, tiled=True)[0]]
  transfers between devices with their start and end apart: 21 -> 21, of which waited for: 10 -> 11; matrix products, arithmetic and copies ran while one was open for 8% -> 8% of each run, Pallas kernels for 40% -> 27%
where the time goes in v2:
time: 279 us; the launch traced here: 278 us
  Pallas kernels  134 us (48%)
  waiting for transfers between devices  58.7 us (21%)
  starting transfers between devices  20 us (7%)
  local copies, waits for them, and re-layouts  17.1 us (6%)
  blocking collectives  15 us (5%)
  other arithmetic  14.9 us (5%)
  between operations  14.4 us (5%)
  matrix products  4.41 us (2%)
    pallas_call x1, Pallas kernels, body(): pl.pallas_call(mlp_kernel, grid=grid, in_specs=[tile_spec, *halo_specs(im...  57.4 us
    pallas_call x1, Pallas kernels, body(): pl.pallas_call(functools.partial(back_kernel, head_size), grid=grid, in_s...  29.8 us
    pallas_call x1, Pallas kernels, body(): pl.pallas_call(functools.partial(attend_kernel, head_size), grid=grid, in...  26.8 us
    reduce_scatter x1, waiting for transfers between devices, body(): lax.psum_scatter(pack_two, 'dp', scatter_dimension=0, tiled=True)[0]  21.8 us
    all_gather x1, waiting for transfers between devices, body(): lax.all_gather(jnp.concatenate([expand_weight, thick], axis=0).astype(BF)...  16.4 us
    ppermute x14, waiting for transfers between devices, shifted(): lax.ppermute(block, axis, [((i - distance) % count, i) for i in range(cou...  16.2 us
    all_gather x1, blocking collectives, body(): small = lax.all_gather(small, 'dp', axis=0, tiled=True)  15 us
    pallas_call x1, Pallas kernels, body(): pl.pallas_call(close_kernel, grid=grid, in_specs=[joint_spec, flat_spec,...  15 us
  transfers between devices with their start and end apart: 21, of which 11 were waited for; matrix products, arithmetic and copies ran while one was open for 8% of the time, Pallas kernels for 27%

profile of v2, /device:TPU:0, one launch (start us, length us, event | category | flops | bytes accessed | tf_op | source)
XLA Modules:
  0.0 278.5 jit_solution(14683464488789481741)
XLA Ops:
  7.2 1.0 convert.27
  8.2 1.0 convert.26
  9.2 0.7 pad_maximum_fusion.4
  10.0 1.1 convert.29
  11.2 0.8 pad_maximum_fusion.1
  12.1 2.4 copy-done
  14.5 2.4 copy-done.1
  17.6 4.0 %collective-permute-start.1 = (bf16[6,3,3,512]{3,2,1,0:T(4,128)(2,1)S(1)}, bf16[6,3,3,512]{3,2,1,0:T(4,128)(2,1)}, u32[]{:S(2)}, u32[]{:S(2)}) collective-permute-start(bf16[6,3,3,512]{3,2,1,0:T(4,128)(2,1)S(1)} %get-tuple-element.43), channel_id=1, source_target_pairs={{3,0},{2,1},{1,2},{0,3},{7,4},{6,5},{5,6},{4,7},{11,8},{10,9},{9,1... | collective-permute-start | bytes 165896 | tf_op jit(solution)/shard_map/ppermute | solution.py:510
  23.0 15.0 %all-gather.1 = bf16[8,1,1152]{2,1,0:T(2,128)(2,1)S(1)} all-gather(bf16[1,1,1152]{2,1,0:T(2,128)(2,1)S(1)} %reshape.175), channel_id=2, replica_groups=mesh['dp'=8,'row'=2,'col'=2] {'dp'}, dimensions={0}, use_global_device_ids=true | all-gather | bytes 20736 | tf_op jit(solution)/shard_map/all_gather | solution.py:667
  39.5 2.6 fusion.6
  42.5 1.4 add.136
  44.0 2.2 broadcast_add_fusion.bias_ref
  47.6 26.8 %attend.1 = (f32[2688,512]{1,0:T(8,128)}, bf16[2688,512]{1,0:T(8,128)(2,1)}, bf16[48,56,1536]{2,1,0:T(8,128)(2,1)}, bf16[48,56,1024]{2,1,0:T(8,128)(2,1)}, bf16[...) custom-call(f32[3,14,56,512]{3,2,1,0:T(8,128)} %bitcast.53, bf16[6,3,11,512]{3,2,1,0:T(8,128)(2,1)} %collective-permute-done.row_ref, ...), custom_call_target="tpu_custom_call" | custom-call | flops 8455716864 | bytes 40000000 | tf_op jit(solution)/shard_map/attend/pallas_call | solution.py:740
  74.4 16.4 %all-gather.7.cloned.1.call-done.packed_ref = bf16[8,128,2048]{2,1,0:T(8,128)(2,1)} async-done(((bf16[1,128,2048]{2,1,0:T(8,128)(2,1)}), bf16[8,128,2048]{2,1,0:T(8,128)(2,1)}) %all-gather.7.cloned.1.call-update) | async-done | bytes 4194320 | tf_op jit(solution)/shard_map/all_gather | solution.py:680
  90.8 57.4 %mlp.1 = (f32[3,14,56,512]{3,2,1,0:T(8,128)}, f32[3,3,14,512]{3,2,1,0:T(8,128)}, f32[3,3,56,512]{3,2,1,0:T(8,128)}, f32[2688,512]{1,0:T(8,128)}, bf16[48,56,512]...) custom-call(f32[3,14,56,512]{3,2,1,0:T(8,128)} %bitcast.55, ...), custom_call_target="tpu_custom_call" | custom-call | flops 36641439744 | bytes 50000000 | tf_op jit(solution)/shard_map/mlp/pallas_call | solution.py:775
  148.3 29.8 %back.1 = (bf16[2688,1536]{1,0:T(8,128)(2,1)}, bf16[8,80,1536]{2,1,0:T(8,128)(2,1)}) custom-call(bf16[2688,512]{1,0:T(8,128)(2,1)} %get-tuple-element.45.hid_ref, bf16[48,56,1536]{2,1,0:T(8,128)(2,1)} %get-tuple-element.46.qkv_ref, bf16[48,56,1024]{2,1,0:T(8,128)(2,1)} %get-tuple-element.47.prob_ref, bf16[48,56,512]{2,1,0:T(8,128)(2,1)} %get-tuple-element.50.gatt_ref, ...), custom_call_target="tpu_custom_call" | custom-call | flops 25367150592 | bytes 50000000 | tf_op jit(solution)/shard_map/back/pallas_call | solution.py:839
  178.8 1.5 collective-permute-start.9
  180.3 21.8 %reduce-scatter.5.cloned.1.call-done = bf16[1,144,2048]{2,1,0:T(8,128)(2,1)} async-done(((bf16[8,144,2048]{2,1,0:T(8,128)(2,1)}), bf16[1,144,2048]{2,1,0:T(8,128)(2,1)}) %reduce-scatter.5.cloned.1.call-update) | async-done | bytes 589840 | tf_op jit(solution)/shard_map/reduce_scatter | solution.py:836
  202.1 1.9 fusion.12
  204.0 1.5 collective-permute-start.3
  205.5 1.5 collective-permute-start.5
  207.0 15.0 %close.1 = (f32[3,14,56,512]{3,2,1,0:T(8,128)}, f32[3,3,14,512]{3,2,1,0:T(8,128)}, f32[3,3,56,512]{3,2,1,0:T(8,128)}) custom-call(bf16[2688,1536]{1,0:T(8,128)(2,1)} %get-tuple-element.58.gact_ref, f32[2688,512]{1,0:T(8,128)} %get-tuple-element.59.xp_ref, f32[2688,512]{1,0:T(8,128)} %get-tuple-element.60.gmid_ref, ...), custom_call_target="tpu_custom_call" | custom-call | flops 8455716864 | bytes 30000000 | tf_op jit(solution)/shard_map/close/pallas_call | solution.py:873
  222.0 1.3 convert_element_type.168
  223.8 1.7 collective-permute-start.10
  225.5 1.2 add_convert_fusion.1
  227.1 0.9 slice.179
  228.0 1.5 collective-permute-start.8
  229.5 0.8 eq.65
  230.4 2.9 %collective-permute-done.8 = bf16[3,3,3,512]{3,2,1,0:T(4,128)(2,1)S(1)} collective-permute-done((bf16[3,3,3,512]{3,2,1,0:T(4,128)(2,1)S(1)}, bf16[3,3,3,512]{3,2,1,0:T(4,128)(2,1)S(1)}, u32[]{:S(2)}, u32[]{:S(2)}) %collective-permute-start.8) | collective-permute-done | bytes 27680 | tf_op jit(solution)/shard_map/ppermute | solution.py:510
  233.3 1.2 collective-permute-start.11
  234.6 1.9 collective-permute-start.12
  236.5 1.0 maximum_convert_fusion.row_ref
  237.4 1.1 collective-permute-done.11
  238.9 1.6 collective-permute-done.12
  240.6 2.1 patch.2
  242.7 7.4 %collective-permute-done.10.col_ref = bf16[3,3,56,512]{3,2,1,0:T(8,128)(2,1)S(1)} collective-permute-done((bf16[3,3,56,512]{3,2,1,0:T(8,128)(2,1)S(1)}, bf16[3,3,56,512]{3,2,1,0:T(8,128)(2,1)S(1)}, u32[]{:S(2)}, u32[]{:S(2)}) %collective-permute-start.10) | collective-permute-done | bytes 516128 | tf_op jit(solution)/shard_map/ppermute | solution.py:500
  250.1 2.1 patch.3
  252.2 1.0 collective-permute-done.4
  253.6 1.0 fusion.15
  255.8 0.8 slice.163
  257.3 2.2 collective-permute-done.15
  259.5 1.7 collective-permute-done.13
  261.3 1.0 add_convert_fusion.2
  262.9 0.8 pad_maximum_fusion.2
  263.7 1.5 collective-permute-start.14
  265.2 2.0 collective-permute-done.16
  269.1 0.8 pad_maximum_fusion.3
  270.1 1.8 fusion.3
  (130 shorter events, 12.4 us)
Async XLA Ops:
  7.2 4.0 %copy-start.4 = (f32[64,2048]{1,0:T(8,128)S(1)}, f32[64,2048]{1,0:T(8,128)}, u32[]{:S(2)}) copy-start(f32[64,2048]{1,0:T(8,128)} %param.29) | copy-start | bytes 1572868
  7.2 40.4 %all-gather.5.cloned.1.call-start = ((), (), s32[]{:S(2)}) async-start(), calls=%async_computation.2 | async-start | bytes 2359296 | tf_op jit(solution)/shard_map/all_gather | solution.py:674
  10.0 80.9 %all-gather.7.cloned.1.call-start = ((), (), s32[]{:S(2)}) async-start(), calls=%async_computation.3 | async-start | bytes 4718592 | tf_op jit(solution)/shard_map/all_gather | solution.py:680
  12.1 190.0 %reduce-scatter.5.cloned.1.call-start = ((), (), s32[]{:S(2)}) async-start(), calls=%async_computation.5 | async-start | bytes 5308416 | tf_op jit(solution)/shard_map/reduce_scatter | solution.py:836
  12.1 2.4 copy-start
  14.5 2.4 copy-start.1
  16.9 5.4 %copy-start.10 = (f32[64]{0:T(128)S(1)}, f32[64]{0:T(128)}, u32[]{:S(2)}) copy-start(f32[64]{0:T(128)} %param.19) | copy-start | bytes 772
  16.9 5.4 %copy-start.11 = (f32[64]{0:T(128)S(1)}, f32[64]{0:T(128)}, u32[]{:S(2)}) copy-start(f32[64]{0:T(128)} %param.20) | copy-start | bytes 772
  16.9 5.4 %copy-start.12 = (f32[64]{0:T(128)S(1)}, f32[64]{0:T(128)}, u32[]{:S(2)}) copy-start(f32[64]{0:T(128)} %param.22) | copy-start | bytes 772
  16.9 5.5 %copy-start.13 = (f32[64]{0:T(128)S(1)}, f32[64]{0:T(128)}, u32[]{:S(2)}) copy-start(f32[64]{0:T(128)} %param.23) | copy-start | bytes 772
  16.9 5.5 %copy-start.14 = (f32[64]{0:T(128)S(1)}, f32[64]{0:T(128)}, u32[]{:S(2)}) copy-start(f32[64]{0:T(128)} %param.26) | copy-start | bytes 772
  16.9 5.5 %copy-start.15 = (f32[64]{0:T(128)S(1)}, f32[64]{0:T(128)}, u32[]{:S(2)}) copy-start(f32[64]{0:T(128)} %param.27) | copy-start | bytes 772
  16.9 5.5 %copy-start.16 = (f32[64]{0:T(128)S(1)}, f32[64]{0:T(128)}, u32[]{:S(2)}) copy-start(f32[64]{0:T(128)} %param.28) | copy-start | bytes 772
  16.9 5.5 %copy-start.9 = (f32[256]{0:T(256)S(1)}, f32[256]{0:T(256)}, u32[]{:S(2)}) copy-start(f32[256]{0:T(256)} %param.30) | copy-start | bytes 3076
  16.9 5.5 %copy-start.17 = (f32[64]{0:T(128)S(1)}, f32[64]{0:T(128)}, u32[]{:S(2)}) copy-start(f32[64]{0:T(128)} %param.32) | copy-start | bytes 772
  16.9 5.5 %copy-start.8 = (f32[2,169]{1,0:T(2,128)S(1)}, f32[2,169]{1,0:T(2,128)}, u32[]{:S(2)}) copy-start(f32[2,169]{1,0:T(2,128)} %param.24) | copy-start | bytes 4060
  16.9 21.2 %copy-start.7 = (s32[49,49]{1,0:T(8,128)S(1)}, s32[49,49]{1,0:T(8,128)}, u32[]{:S(2)}) copy-start(s32[49,49]{1,0:T(8,128)} %param.18) | copy-start | bytes 28816
  17.6 29.9 %collective-permute-start.1 = (bf16[6,3,3,512]{3,2,1,0:T(4,128)(2,1)S(1)}, bf16[6,3,3,512]{3,2,1,0:T(4,128)(2,1)}, u32[]{:S(2)}, u32[]{:S(2)}) collective-permute-start(bf16[6,3,3,512]{3,2,1,0:T(4,128)(2,1)S(1)} %get-tuple-element.43), channel_id=1, source_target_pairs={{3,0},{2,1},{1,2},{0,3},{7,4},{6,5},{5,6},{4,7},{11,8},{10,9},{9,1... | collective-permute-start | bytes 165896 | tf_op jit(solution)/shard_map/ppermute | solution.py:510
  21.6 25.9 %collective-permute-start = (bf16[6,3,11,512]{3,2,1,0:T(8,128)(2,1)S(1)}, bf16[6,3,11,512]{3,2,1,0:T(8,128)(2,1)}, u32[]{:S(2)}, u32[]{:S(2)}) collective-permute-start(bf16[6,3,11,512]{3,2,1,0:T(8,128)(2,1)S(1)} %get-tuple-element.42), channel_id=1, source_target_pairs={{2,0},{0,2},{3,1},{1,3},{6,4},{4,6},{7,5},{5,7},{10,8},{8,10},{11,... | collective-permute-start | bytes 608264 | tf_op jit(solution)/shard_map/ppermute | solution.py:500
  22.2 25.4 %collective-permute-start.2 = (bf16[6,3,56,512]{3,2,1,0:T(8,128)(2,1)S(1)}, bf16[6,3,56,512]{3,2,1,0:T(8,128)(2,1)}, u32[]{:S(2)}, u32[]{:S(2)}) collective-permute-start(bf16[6,3,56,512]{3,2,1,0:T(8,128)(2,1)S(1)} %get-tuple-element.44), channel_id=1, source_target_pairs={{1,0},{0,1},{3,2},{2,3},{5,4},{4,5},{7,6},{6,7},{9,8},{8,9},{11,10... | collective-permute-start | bytes 3096584 | tf_op jit(solution)/shard_map/ppermute | solution.py:500
  148.2 105.3 %reduce-scatter.3.cloned.1.call-start = ((), (), s32[]{:S(2)}) async-start(), calls=%async_computation.4 | async-start | bytes 2211840 | tf_op jit(solution)/shard_map/reduce_scatter | solution.py:871
  148.3 29.8 %copy-start.6 = (f32[3,3,14,512]{3,2,1,0:T(8,128)S(1)}, f32[3,3,14,512]{3,2,1,0:T(8,128)}, u32[]{:S(2)}) copy-start(f32[3,3,14,512]{3,2,1,0:T(8,128)} %get-tuple-element.57) | copy-start | bytes 774148
  178.8 55.8 %collective-permute-start.9 = (bf16[3,3,11,512]{3,2,1,0:T(8,128)(2,1)}, bf16[3,3,11,512]{3,2,1,0:T(8,128)(2,1)}, u32[]{:S(2)}, u32[]{:S(2)}) collective-permute-start(bf16[3,3,11,512]{3,2,1,0:T(8,128)(2,1)} %bitcast.51), channel_id=1, source_target_pairs={{2,0},{0,2},{3,1},{1,3},{6,4},{4,6},{7,5},{5,7},{10,8},{8,10},{11,... | collective-permute-start | bytes 304136 | tf_op jit(solution)/shard_map/ppermute | solution.py:500
  204.0 21.5 %collective-permute-start.3 = (bf16[144,1024]{1,0:T(8,128)(2,1)}, bf16[144,1024]{1,0:T(8,128)(2,1)S(1)}, u32[]{:S(2)}, u32[]{:S(2)}) collective-permute-start(bf16[144,1024]{1,0:T(8,128)(2,1)} %get-tuple-element.78), channel_id=1, source_target_pairs={{2,0},{0,2},{3,1},{1,3},{6,4},{4,6},{7,5},{5,7},{10,8},{8,10},{11,... | collective-permute-start | bytes 884744 | tf_op jit(solution)/shard_map/ppermute | solution.py:500
  205.5 20.0 %collective-permute-start.5 = (bf16[144,1024]{1,0:T(8,128)(2,1)}, bf16[144,1024]{1,0:T(8,128)(2,1)}, u32[]{:S(2)}, u32[]{:S(2)}) collective-permute-start(bf16[144,1024]{1,0:T(8,128)(2,1)} %get-tuple-element.79), channel_id=1, source_target_pairs={{1,0},{0,1},{3,2},{2,3},{5,4},{4,5},{7,6},{6,7},{9,8},{8,9},{11,10... | collective-permute-start | bytes 884744 | tf_op jit(solution)/shard_map/ppermute | solution.py:500
  207.0 16.4 %copy-start.3 = (f32[3,3,56,512]{3,2,1,0:T(8,128)S(1)}, f32[3,3,56,512]{3,2,1,0:T(8,128)}, u32[]{:S(2)}) copy-start(f32[3,3,56,512]{3,2,1,0:T(8,128)} %get-tuple-element.56) | copy-start | bytes 3096580
  207.0 18.5 %copy-start.2 = (bf16[1,144,2048]{2,1,0:T(8,128)(2,1)S(1)}, bf16[1,144,2048]{2,1,0:T(8,128)(2,1)}, u32[]{:S(2)}) copy-start(bf16[1,144,2048]{2,1,0:T(8,128)(2,1)} %reduce-scatter.5.cloned.1.call-done) | copy-start | bytes 1769476
  222.0 8.4 %copy-start.5 = (f32[3,3,14,512]{3,2,1,0:T(8,128)S(1)}, f32[3,3,14,512]{3,2,1,0:T(8,128)}, u32[]{:S(2)}) copy-start(f32[3,3,14,512]{3,2,1,0:T(8,128)} %get-tuple-element.63) | copy-start | bytes 774148
  223.4 17.2 %collective-permute-start.7 = (bf16[3,3,56,512]{3,2,1,0:T(8,128)(2,1)S(1)}, bf16[3,3,56,512]{3,2,1,0:T(8,128)(2,1)S(1)}, u32[]{:S(2)}, u32[]{:S(2)}) collective-permute-start(bf16[3,3,56,512]{3,2,1,0:T(8,128)(2,1)S(1)} %convert_element_type.165), channel_id=1, source_target_pairs={{1,0},{0,1},{3,2},{2,3},{5,4},{4,5},{7,6},{6,7},{9,8},{8,9},{11,10... | collective-permute-start | bytes 1548296 | tf_op jit(solution)/shard_map/ppermute | solution.py:500
  223.8 26.3 %collective-permute-start.10 = (bf16[3,3,56,512]{3,2,1,0:T(8,128)(2,1)S(1)}, bf16[3,3,56,512]{3,2,1,0:T(8,128)(2,1)S(1)}, u32[]{:S(2)}, u32[]{:S(2)}) collective-permute-start(bf16[3,3,56,512]{3,2,1,0:T(8,128)(2,1)S(1)} %convert_element_type.168), channel_id=1, source_target_pairs={{1,0},{0,1},{3,2},{2,3},{5,4},{4,5},{7,6},{6,7},{9,8},{8,9},{11,10... | collective-permute-start | bytes 1548296 | tf_op jit(solution)/shard_map/ppermute | solution.py:500
  226.7 26.6 %collective-permute-start.4 = (bf16[144,1024]{1,0:T(8,128)(2,1)S(1)}, bf16[144,1024]{1,0:T(8,128)(2,1)S(1)}, u32[]{:S(2)}, u32[]{:S(2)}) collective-permute-start(bf16[144,1024]{1,0:T(8,128)(2,1)S(1)} %get-tuple-element.76), channel_id=1, source_target_pairs={{1,0},{0,1},{3,2},{2,3},{5,4},{4,5},{7,6},{6,7},{9,8},{8,9},{11,10... | collective-permute-start | bytes 884744 | tf_op jit(solution)/shard_map/ppermute | solution.py:500
  228.0 5.3 %collective-permute-start.8 = (bf16[3,3,3,512]{3,2,1,0:T(4,128)(2,1)S(1)}, bf16[3,3,3,512]{3,2,1,0:T(4,128)(2,1)S(1)}, u32[]{:S(2)}, u32[]{:S(2)}) collective-permute-start(bf16[3,3,3,512]{3,2,1,0:T(4,128)(2,1)S(1)} %slice.179), channel_id=1, source_target_pairs={{3,0},{2,1},{1,2},{0,3},{7,4},{6,5},{5,6},{4,7},{11,8},{10,9},{9,1... | collective-permute-start | bytes 82952 | tf_op jit(solution)/shard_map/ppermute | solution.py:510
  233.3 5.3 %collective-permute-start.11 = (bf16[3,3,3,512]{3,2,1,0:T(4,128)(2,1)S(1)}, bf16[3,3,3,512]{3,2,1,0:T(4,128)(2,1)S(1)}, u32[]{:S(2)}, u32[]{:S(2)}) collective-permute-start(bf16[3,3,3,512]{3,2,1,0:T(4,128)(2,1)S(1)} %slice.181), channel_id=1, source_target_pairs={{3,0},{2,1},{1,2},{0,3},{7,4},{6,5},{5,6},{4,7},{11,8},{10,9},{9,1... | collective-permute-start | bytes 82952 | tf_op jit(solution)/shard_map/ppermute | solution.py:510
  234.6 6.0 %collective-permute-start.12 = (bf16[3,3,11,512]{3,2,1,0:T(8,128)(2,1)S(1)}, bf16[3,3,11,512]{3,2,1,0:T(8,128)(2,1)S(1)}, u32[]{:S(2)}, u32[]{:S(2)}) collective-permute-start(bf16[3,3,11,512]{3,2,1,0:T(8,128)(2,1)S(1)} %bitcast.64), channel_id=1, source_target_pairs={{2,0},{0,2},{3,1},{1,3},{6,4},{4,6},{7,5},{5,7},{10,8},{8,10},{11,... | collective-permute-start | bytes 304136 | tf_op jit(solution)/shard_map/ppermute | solution.py:500
  238.6 14.8 %collective-permute-start.6 = (bf16[144,1024]{1,0:T(8,128)(2,1)S(1)}, bf16[144,1024]{1,0:T(8,128)(2,1)S(1)}, u32[]{:S(2)}, u32[]{:S(2)}) collective-permute-start(bf16[144,1024]{1,0:T(8,128)(2,1)S(1)} %get-tuple-element.77), channel_id=1, source_target_pairs={{2,0},{0,2},{3,1},{1,3},{6,4},{4,6},{7,5},{5,7},{10,8},{8,10},{11,... | collective-permute-start | bytes 884744 | tf_op jit(solution)/shard_map/ppermute | solution.py:500
  254.6 4.9 %collective-permute-start.15 = (bf16[80,768]{1,0:T(8,128)(2,1)S(1)}, bf16[80,768]{1,0:T(8,128)(2,1)S(1)}, u32[]{:S(2)}, u32[]{:S(2)}) collective-permute-start(bf16[80,768]{1,0:T(8,128)(2,1)S(1)} %get-tuple-element.98), channel_id=1, source_target_pairs={{1,0},{0,1},{3,2},{2,3},{5,4},{4,5},{7,6},{6,7},{9,8},{8,9},{11,10... | collective-permute-start | bytes 368648 | tf_op jit(solution)/shard_map/ppermute | solution.py:500
  255.1 6.1 %collective-permute-start.13 = (bf16[80,768]{1,0:T(8,128)(2,1)S(1)}, bf16[80,768]{1,0:T(8,128)(2,1)S(1)}, u32[]{:S(2)}, u32[]{:S(2)}) collective-permute-start(bf16[80,768]{1,0:T(8,128)(2,1)S(1)} %get-tuple-element.99), channel_id=1, source_target_pairs={{2,0},{0,2},{3,1},{1,3},{6,4},{4,6},{7,5},{5,7},{10,8},{8,10},{11,... | collective-permute-start | bytes 368648 | tf_op jit(solution)/shard_map/ppermute | solution.py:500
  262.3 4.9 %collective-permute-start.16 = (bf16[80,768]{1,0:T(8,128)(2,1)S(1)}, bf16[80,768]{1,0:T(8,128)(2,1)S(1)}, u32[]{:S(2)}, u32[]{:S(2)}) collective-permute-start(bf16[80,768]{1,0:T(8,128)(2,1)S(1)} %get-tuple-element.96), channel_id=1, source_target_pairs={{2,0},{0,2},{3,1},{1,3},{6,4},{4,6},{7,5},{5,7},{10,8},{8,10},{11,... | collective-permute-start | bytes 368648 | tf_op jit(solution)/shard_map/ppermute | solution.py:500
  263.7 4.9 %collective-permute-start.14 = (bf16[80,768]{1,0:T(8,128)(2,1)S(1)}, bf16[80,768]{1,0:T(8,128)(2,1)S(1)}, u32[]{:S(2)}, u32[]{:S(2)}) collective-permute-start(bf16[80,768]{1,0:T(8,128)(2,1)S(1)} %get-tuple-element.97), channel_id=1, source_target_pairs={{1,0},{0,1},{3,2},{2,3},{5,4},{4,5},{7,6},{6,7},{9,8},{8,9},{11,10... | collective-permute-start | bytes 368648 | tf_op jit(solution)/shard_map/ppermute | solution.py:500
Sparse Core Ops, SparseCore 0:
  10.2 32.1 all-gather.4
  44.5 46.2 all-gather.6
  148.4 53.7 reduce-scatter.4
  204.3 34.3 reduce-scatter.2

commit v3 on v2

--- a/solution.py
+++ b/solution.py
@@ -219,7 +219,17 @@
     attended = wide_ref[...].astype(BF)
     att_ref[...] = attended
     branch = nn(attended, weight_ref[:, 3 * features :]) + vec_ref[4:5, :]
-    mid_ref[...] = xp_ref[...] + branch
+    wide_ref[...] = xp_ref[...] + branch
+    _, breadth, height, _ = tile_ref.shape
+    for place in range(height // (BANDS * WIN)):
+
+        @pl.when(half == place)
+        def _():
+            for col in range(breadth):
+                for band in range(BANDS):
+                    at = row_of(band, col)
+                    to = col * height + (place * BANDS + band) * WIN
+                    mid_ref[to : to + WIN, :] = wide_ref[at : at + WIN, :]
 
 
 def mlp_kernel(
@@ -228,8 +238,6 @@
     corner_ref,
     col_ref,
     mid_ref,
-    att_ref,
-    weight_ref,
     packed_ref,
     vec_ref,
     ebias_ref,
@@ -237,7 +245,6 @@
     resrow_ref,
     rescol_ref,
     gmid_ref,
-    gatt_ref,
     pack_ref,
     sums_ref,
     esum_ref,
@@ -246,19 +253,25 @@
     ws_ref,
     ge_ref,
     gs_ref,
-    go_ref,
     out_ref,
     rows_ref,
     cols_ref,
+    low_ref,
+    hid_ref,
+    act_ref,
+    gbef_ref,
 ):
-    half = pl.program_id(1)
-    step = pl.program_id(0) * pl.num_programs(1) + half
-    steps = pl.num_programs(0) * pl.num_programs(1)
-    features = tile_ref.shape[-1]
+    step = pl.program_id(0)
+    steps = pl.num_programs(0)
+    _, breadth, height, features = tile_ref.shape
     hidden_units = we_ref.shape[1]
     shards = pack_ref.shape[0]
     deep = features // shards
     blocks = hidden_units // features
+    total = breadth * height
+    even = total // 256 * 256
+    rest = total - even
+    inner = height - SHIFT
 
     @pl.when(step == 0)
     def _():
@@ -271,18 +284,28 @@
                 ]
         ge_ref[...] = jnp.zeros_like(ge_ref)
         gs_ref[...] = jnp.zeros_like(gs_ref)
-        go_ref[...] = jnp.zeros_like(go_ref)
         sums_ref[...] = jnp.zeros_like(sums_ref)
         esum_ref[...] = jnp.zeros_like(esum_ref)
 
-    widen(half, row_ref, corner_ref, col_ref, rows_ref, cols_ref)
-    extract(half, tile_ref, rows_ref, cols_ref, cot_ref)
+    widen(0, row_ref, corner_ref, col_ref, rows_ref, cols_ref)
+    for col in range(breadth):
+        at = col * height
+        cot_ref[at : at + inner, :] = (
+            tile_ref[0, col + SHIFT, SHIFT:, :]
+            if col < breadth - SHIFT
+            else cols_ref[col + SHIFT - breadth, SHIFT:, :]
+        )
+        for j in range(SHIFT):
+            cot_ref[at + inner + j : at + inner + j + 1, :] = rows_ref[j, col : col + 1, :]
     mid = mid_ref[...]
     normed, inverse = norm_parts(mid)
     hidden = (normed * vec_ref[5:6, :] + vec_ref[6:7, :]).astype(BF)
-    hidden_t = hidden.T
     low = cot_ref[...].astype(BF)
-    low_t = low.T
+    hidden_t = hidden[:even].T
+    low_t = low[:even].T
+    kept = pl.ds(pl.multiple_of(step * rest, rest), rest)
+    low_ref[kept, :] = low[even:]
+    hid_ref[kept, :] = hidden[even:]
     out = mid + vec_ref[7:8, :]
     ghid = None
     chunk = features
@@ -298,25 +321,38 @@
         gbefore = gbefore.astype(BF)
         back = nt(gbefore, we_ref[:, cols])
         ghid = back if ghid is None else ghid + back
-        gs_ref[:, cols] += nn(low_t, active)
-        ge_ref[:, cols] += nn(hidden_t, gbefore)
+        gs_ref[:, cols] += nn(low_t, active[:even])
+        ge_ref[:, cols] += nn(hidden_t, gbefore[:even])
+        act_ref[kept, cols] = active[even:]
+        gbef_ref[kept, cols] = gbefore[even:]
     out_ref[...] = out
-    deposit(half, out_ref, res_ref, resrow_ref, rescol_ref)
+    for col in range(breadth):
+        at = col * height
+        if col < breadth - SHIFT:
+            res_ref[0, col + SHIFT, SHIFT:, :] = out_ref[at : at + inner, :]
+        else:
+            rescol_ref[0, col + SHIFT - breadth, SHIFT:, :] = out_ref[at : at + inner, :]
+        for j in range(SHIFT):
+            resrow_ref[0, j, col : col + 1, :] = out_ref[at + inner + j : at + inner + j + 1, :]
     cot = cot_ref[...]
     gmid = cot + norm_back(ghid, normed, inverse, vec_ref[5:6, :])
-    gmid_ref[...] = gmid
-    gbranch = gmid.astype(BF)
-    go_ref[...] += nn(att_ref[...].T, gbranch)
-    gatt = nt(gbranch, weight_ref[:, 3 * features :])
-    gatt_ref[...] = gatt.reshape(2 * BANDS, WT, features).astype(BF)
     sums_ref[0:1, :] += jnp.sum(gmid, axis=0, keepdims=True)
     sums_ref[1:2, :] += jnp.sum(ghid * normed, axis=0, keepdims=True)
     sums_ref[2:3, :] += jnp.sum(ghid, axis=0, keepdims=True)
     sums_ref[3:4, :] += jnp.sum(cot, axis=0, keepdims=True)
+    out_ref[...] = gmid
+    zero = jnp.zeros((PAD - WIN, features), F32)
+    for band in range(height // WIN):
+        for col in range(breadth):
+            at = row_of(band, col)
+            src = col * height + band * WIN
+            gmid_ref[at : at + WIN, :] = out_ref[src : src + WIN, :]
+            gmid_ref[at + WIN : at + PAD, :] = zero
 
     @pl.when(step == steps - 1)
     def _():
-        base = 2 * deep
+        ge_ref[...] += nn(hid_ref[...].T, gbef_ref[...])
+        gs_ref[...] += nn(low_ref[...].T, act_ref[...])
         for d in range(shards):
             pack_ref[d, 0:deep, :] = ge_ref[d * deep : (d + 1) * deep, :].astype(BF)
             for j in range(blocks):
@@ -333,10 +369,6 @@
                     pack_ref[d, deep : 2 * deep, j * features : (j + 1) * features] = (
                         gs_ref[:, at : at + deep].T.astype(BF)
                     )
-                thin = deep // blocks
-                pack_ref[d, base : base + thin, j * features : (j + 1) * features] = go_ref[
-                    d * deep + j * thin : d * deep + (j + 1) * thin, :
-                ].astype(BF)
 
 
 def back_kernel(
@@ -344,7 +376,8 @@
     hid_ref,
     qkv_ref,
     prob_ref,
-    gatt_ref,
+    att_ref,
+    gmid_ref,
     weight_ref,
     vec_ref,
     sums_two_ref,
@@ -356,6 +389,8 @@
     sums_ref,
     table_ref,
     graw_ref,
+    gatt_ref,
+    go_ref,
 ):
     half = pl.program_id(1)
     step = pl.program_id(0) * pl.num_programs(1) + half
@@ -368,6 +403,12 @@
         acc_ref[...] = jnp.zeros_like(acc_ref)
         sums_ref[...] = jnp.zeros_like(sums_ref)
         table_ref[...] = jnp.zeros_like(table_ref)
+        go_ref[...] = jnp.zeros_like(go_ref)
+
+    gbranch = gmid_ref[...].astype(BF)
+    gatt = nt(gbranch, weight_ref[:, 3 * features :])
+    gatt_ref[...] = gatt.reshape(2 * BANDS, WT, features).astype(BF)
+    go_ref[...] += nn(att_ref[...].T, gbranch)
 
     group = 256
     span = group // head_size * QL
@@ -445,13 +486,14 @@
             axis=0,
         )
         for d in range(shards):
-            pack_ref[d, 0:deep, :] = acc_ref[d * deep : (d + 1) * deep, :].astype(BF)
-            pack_ref[d, deep : deep + LINES, :] = jnp.zeros((LINES, 3 * features), BF)
+            own = slice(d * deep, (d + 1) * deep)
+            pack_ref[d, 0:deep, : 3 * features] = acc_ref[own, :].astype(BF)
+            pack_ref[d, 0:deep, 3 * features :] = go_ref[own, :].astype(BF)
+            pack_ref[d, deep : deep + LINES, :] = jnp.zeros((LINES, 4 * features), BF)
             for j in range(4):
                 pack_ref[d, deep : deep + LINES, j * lanes : (j + 1) * lanes] = table_ref[
                     j * LINES : (j + 1) * LINES, d * lanes : (d + 1) * lanes
                 ].astype(BF)
-            own = slice(d * deep, (d + 1) * deep)
             at = features
             pack_ref[d, deep : deep + LINES, at : at + deep] = lines[:, own].astype(BF)
             at = features + features // 2
@@ -724,6 +766,10 @@
 
     joint_spec = pl.BlockSpec((step_rows, 3 * features), lambda i, j: (i * halves + j, 0))
 
+    area = height * breadth
+    image_spec = pl.BlockSpec((area, features), lambda i, j: (i, 0))
+    padded_spec = pl.BlockSpec((halves * step_rows, features), lambda i, j: (i, 0))
+
     def window_spec(last):
         return pl.BlockSpec((2 * BANDS, WT, last), lambda i, j: (i * halves + j, 0, 0))
 
@@ -753,7 +799,7 @@
             window_spec(3 * features),
             window_spec(wide),
             flat_spec,
-            flat_spec,
+            image_spec,
         ],
         out_shape=[
             shape((total_rows, features), F32),
@@ -761,7 +807,7 @@
             shape((windows, WT, 3 * features), BF),
             shape((windows, WT, wide), BF),
             shape((total_rows, features), BF),
-            shape((total_rows, features), F32),
+            shape((images * area, features), F32),
         ],
         scratch_shapes=[pltpu.VMEM((step_rows, features), F32), *halo_scratch],
         compiler_params=params,
@@ -771,16 +817,14 @@
         name="attend",
     )(tokens, *halo, weight_one, vec, bias)
 
-    packed_rows = 2 * deep + deep // blocks
-    result, res_row, res_col, gmid, gatt, pack_two, sums_two, esum = pl.pallas_call(
+    rest = images * (area % 256)
+    result, res_row, res_col, gmid, pack_two, sums_two, esum = pl.pallas_call(
         mlp_kernel,
-        grid=grid,
+        grid=(images, 1),
         in_specs=[
             tile_spec,
             *halo_specs(images),
-            flat_spec,
-            flat_spec,
-            whole((features, 4 * features)),
+            image_spec,
             whole((shards, 2 * deep, hidden_units)),
             whole((8, features)),
             whole((1, hidden_units)),
@@ -789,9 +833,8 @@
             tile_spec,
             row_spec,
             col_spec,
-            flat_spec,
-            window_spec(features),
-            whole((shards, packed_rows, hidden_units)),
+            padded_spec,
+            whole((shards, 2 * deep, hidden_units)),
             whole((LINES, features)),
             whole((LINES, hidden_units)),
         ],
@@ -800,24 +843,26 @@
             shape((images, SHIFT, breadth, features), F32),
             shape((images, SHIFT, height, features), F32),
             shape((total_rows, features), F32),
-            shape((windows, WT, features), BF),
-            shape((shards, packed_rows, hidden_units), BF),
+            shape((shards, 2 * deep, hidden_units), BF),
             shape((LINES, features), F32),
             shape((LINES, hidden_units), F32),
         ],
         scratch_shapes=[
-            pltpu.VMEM((step_rows, features), F32),
+            pltpu.VMEM((area, features), F32),
             pltpu.VMEM((features, hidden_units), BF),
             pltpu.VMEM((hidden_units, features), BF),
             pltpu.VMEM((features, hidden_units), F32),
             pltpu.VMEM((features, hidden_units), F32),
-            pltpu.VMEM((features, features), F32),
-            pltpu.VMEM((step_rows, features), F32),
+            pltpu.VMEM((area, features), F32),
             *halo_scratch,
+            pltpu.VMEM((rest, features), BF),
+            pltpu.VMEM((rest, features), BF),
+            pltpu.VMEM((rest, hidden_units), BF),
+            pltpu.VMEM((rest, hidden_units), BF),
         ],
         compiler_params=params,
         cost_estimate=pl.CostEstimate(
-            flops=26 * dense,
+            flops=24 * dense,
             bytes_accessed=50_000_000,
             transcendentals=total_rows * hidden_units,
         ),
@@ -826,8 +871,6 @@
         cotangent,
         *halo,
         middle,
-        attended,
-        weight_one,
         weight_two,
         vec,
         ebias,
@@ -843,16 +886,17 @@
             flat_spec,
             window_spec(3 * features),
             window_spec(wide),
-            window_spec(features),
+            flat_spec,
+            flat_spec,
             whole((features, 4 * features)),
             whole((8, features)),
             whole((LINES, features)),
             whole((LINES, hidden_units)),
         ],
-        out_specs=[joint_spec, whole((shards, deep + LINES, 3 * features))],
+        out_specs=[joint_spec, whole((shards, deep + LINES, 4 * features))],
         out_shape=[
             shape((total_rows, 3 * features), BF),
-            shape((shards, deep + LINES, 3 * features), BF),
+            shape((shards, deep + LINES, 4 * features), BF),
         ],
         scratch_shapes=[
             pltpu.VMEM((features, 3 * features), F32),
@@ -860,13 +904,15 @@
             pltpu.VMEM((1, 3 * features), F32),
             pltpu.VMEM((4 * LINES, wide), F32),
             pltpu.VMEM((4, WT, 256 // head_size * QL), BF),
+            pltpu.VMEM((2 * BANDS, WT, features), BF),
+            pltpu.VMEM((features, features), F32),
         ],
         compiler_params=params,
         cost_estimate=pl.CostEstimate(
             flops=18 * dense, bytes_accessed=50_000_000, transcendentals=0
         ),
         name="back",
-    )(hidden_one, qkv, probs, gatt, weight_one, vec, sums_two, esum)
+    )(hidden_one, qkv, probs, attended, gmid, weight_one, vec, sums_two, esum)
 
     pack_one = lax.psum_scatter(pack_one, "dp", scatter_dimension=0, tiled=True)[0]
 
@@ -905,11 +951,8 @@
         [pack_two[deep : 2 * deep, j * features : (j + 1) * features] for j in range(blocks)],
         axis=0,
     )
-    base = 2 * deep
-    grad_output = jnp.concatenate(
-        [pack_two[base:, j * features : (j + 1) * features] for j in range(blocks)], axis=0
-    )
-    grad_joint = pack_one[:deep]
+    grad_output = pack_one[:deep, 3 * features :]
+    grad_joint = pack_one[:deep, : 3 * features]
     lanes = table_heads * QL
     lines_one = pack_one[deep:, features : features + deep]
     at = features + features // 2

time: 279 us -> 261 us (0.935)
  Pallas kernels: 134 us -> 127 us
  waiting for transfers between devices: 58.7 us -> 53.9 us
  local copies, waits for them, and re-layouts: 17.1 us -> 14.2 us
    pallas_call x1, Pallas kernels: 57.4 us -> 44.8 us  [body(): pl.pallas_call(mlp_kernel, grid=(images, 1), in_specs=[tile_spec, *halo_s...]
    reduce_scatter x1, waiting for transfers between devices: 21.8 us -> 12.6 us  [body(): lax.psum_scatter(pack_two, 'dp', scatter_dimension=0, tiled=True)[0]]
    ppermute x14, waiting for transfers between devices: 16.2 us -> 24.3 us  [shifted(): lax.ppermute(block, axis, [((i - distance) % count, i) for i in range(cou...]
    pallas_call x1, Pallas kernels: 29.8 us -> 33.1 us  [body(): pl.pallas_call(functools.partial(back_kernel, head_size), grid=grid, in_s...]
  transfers between devices with their start and end apart: 21 -> 21, of which waited for: 11 -> 12; matrix products, arithmetic and copies ran while one was open for 8% -> 7% of each run, Pallas kernels for 27% -> 31%
where the time goes in v3:
time: 261 us; the launch traced here: 260 us
  Pallas kernels  127 us (49%)
  waiting for transfers between devices  53.9 us (21%)
  starting transfers between devices  20.3 us (8%)
  blocking collectives  15 us (6%)
  between operations  14.4 us (6%)
  local copies, waits for them, and re-layouts  14.2 us (5%)
  other arithmetic  12.8 us (5%)
  matrix products  3.41 us (1%)
    pallas_call x1, Pallas kernels, body(): pl.pallas_call(mlp_kernel, grid=(images, 1), in_specs=[tile_spec, *halo_s...  44.8 us
    pallas_call x1, Pallas kernels, body(): pl.pallas_call(functools.partial(back_kernel, head_size), grid=grid, in_s...  33.1 us
    pallas_call x1, Pallas kernels, body(): pl.pallas_call(functools.partial(attend_kernel, head_size), grid=grid, in...  28.7 us
    ppermute x14, waiting for transfers between devices, shifted(): lax.ppermute(block, axis, [((i - distance) % count, i) for i in range(cou...  24.3 us
    all_gather x1, blocking collectives, body(): small = lax.all_gather(small, 'dp', axis=0, tiled=True)  15 us
    pallas_call x1, Pallas kernels, body(): pl.pallas_call(close_kernel, grid=grid, in_specs=[joint_spec, flat_spec,...  15 us
    all_gather x1, waiting for transfers between devices, body(): lax.all_gather(jnp.concatenate([expand_weight, thick], axis=0).astype(BF)...  14.9 us
    reduce_scatter x1, waiting for transfers between devices, body(): lax.psum_scatter(pack_two, 'dp', scatter_dimension=0, tiled=True)[0]  12.6 us
  transfers between devices with their start and end apart: 21, of which 12 were waited for; matrix products, arithmetic and copies ran while one was open for 7% of the time, Pallas kernels for 31%

profile of v3, /device:TPU:0, one launch (start us, length us, event | category | flops | bytes accessed | tf_op | source)
XLA Modules:
  0.0 260.5 jit_solution(16513904602337596517)
XLA Ops:
  7.2 0.9 convert.27
  8.1 1.0 convert.26
  9.2 0.7 pad_maximum_fusion.4
  10.0 1.1 convert.29
  11.1 1.1 convert_bitcast_fusion
  12.2 0.8 pad_maximum_fusion.1
  13.1 2.4 copy-done
  15.5 2.4 copy-done.1
  17.9 0.7 edge.1
  18.6 4.0 %collective-permute-start.1 = (bf16[6,3,3,512]{3,2,1,0:T(4,128)(2,1)S(1)}, bf16[6,3,3,512]{3,2,1,0:T(4,128)(2,1)}, u32[]{:S(2)}, u32[]{:S(2)}) collective-permute-start(bf16[6,3,3,512]{3,2,1,0:T(4,128)(2,1)S(1)} %get-tuple-element.42), channel_id=1, source_target_pairs={{3,0},{2,1},{1,2},{0,3},{7,4},{6,5},{5,6},{4,7},{11,8},{10,9},{9,1... | collective-permute-start | bytes 165896 | tf_op jit(solution)/shard_map/ppermute | solution.py:552
  23.9 15.0 %all-gather.1 = bf16[8,1,1152]{2,1,0:T(2,128)(2,1)S(1)} all-gather(bf16[1,1,1152]{2,1,0:T(2,128)(2,1)S(1)} %reshape.175), channel_id=2, replica_groups=mesh['dp'=8,'row'=2,'col'=2] {'dp'}, dimensions={0}, use_global_device_ids=true | all-gather | bytes 20736 | tf_op jit(solution)/shard_map/all_gather | solution.py:709
  39.8 1.6 fusion.6
  41.9 1.4 add.136
  43.3 2.2 broadcast_add_fusion.bias_ref
  46.2 0.7 reshape.171.vec_ref
  47.3 28.7 %attend.1 = (f32[2688,512]{1,0:T(8,128)}, bf16[2688,512]{1,0:T(8,128)(2,1)}, bf16[48,56,1536]{2,1,0:T(8,128)(2,1)}, bf16[48,56,1024]{2,1,0:T(8,128)(2,1)}, bf16[...) custom-call(f32[3,14,56,512]{3,2,1,0:T(8,128)} %bitcast.53, bf16[6,3,11,512]{3,2,1,0:T(8,128)(2,1)} %collective-permute-done.row_ref, ...), custom_call_target="tpu_custom_call" | custom-call | flops 8455716864 | bytes 40000000 | tf_op jit(solution)/shard_map/attend/pallas_call | solution.py:786
  76.0 14.9 %all-gather.7.cloned.1.call-done.packed_ref = bf16[8,128,2048]{2,1,0:T(8,128)(2,1)} async-done(((bf16[1,128,2048]{2,1,0:T(8,128)(2,1)}), bf16[8,128,2048]{2,1,0:T(8,128)(2,1)}) %all-gather.7.cloned.1.call-update) | async-done | bytes 4194320 | tf_op jit(solution)/shard_map/all_gather | solution.py:722
  90.9 44.8 %mlp.1 = (f32[3,14,56,512]{3,2,1,0:T(8,128)}, f32[3,3,14,512]{3,2,1,0:T(8,128)}, f32[3,3,56,512]{3,2,1,0:T(8,128)}, f32[2688,512]{1,0:T(8,128)}, bf16[8,128,2048...) custom-call(f32[3,14,56,512]{3,2,1,0:T(8,128)} %bitcast.55, ...), custom_call_target="tpu_custom_call" | custom-call | flops 33822867456 | bytes 50000000 | tf_op jit(solution)/shard_map/mlp/pallas_call | solution.py:821
  135.8 33.1 %back.1 = (bf16[2688,1536]{1,0:T(8,128)(2,1)}, bf16[8,80,2048]{2,1,0:T(8,128)(2,1)}) custom-call(bf16[2688,512]{1,0:T(8,128)(2,1)} %get-tuple-element.44.hid_ref, bf16[48,56,1536]{2,1,0:T(8,128)(2,1)} %get-tuple-element.45.qkv_ref, bf16[48,56,1024]{2,1,0:T(8,128)(2,1)} %get-tuple-element.46.prob_ref, bf16[2688,512]{1,0:T(8,128)(2,1)} %get-tuple-element.47.att_ref, ...), custom_call_target="tpu_custom_call" | custom-call | flops 25367150592 | bytes 50000000 | tf_op jit(solution)/shard_map/back/pallas_call | solution.py:882
  169.0 2.5 collective-permute-start.8
  172.0 12.6 %reduce-scatter.5.cloned.1.call-done = bf16[1,128,2048]{2,1,0:T(8,128)(2,1)} async-done(((bf16[8,128,2048]{2,1,0:T(8,128)(2,1)}), bf16[1,128,2048]{2,1,0:T(8,128)(2,1)}) %reduce-scatter.5.cloned.1.call-update) | async-done | bytes 524304 | tf_op jit(solution)/shard_map/reduce_scatter | solution.py:879
  184.6 1.1 fusion.11
  185.7 1.5 collective-permute-start.3
  187.2 1.5 collective-permute-start.5
  188.7 15.0 %close.1 = (f32[3,14,56,512]{3,2,1,0:T(8,128)}, f32[3,3,14,512]{3,2,1,0:T(8,128)}, f32[3,3,56,512]{3,2,1,0:T(8,128)}) custom-call(bf16[2688,1536]{1,0:T(8,128)(2,1)} %get-tuple-element.57.gact_ref, f32[2688,512]{1,0:T(8,128)} %get-tuple-element.58.xp_ref, f32[2688,512]{1,0:T(8,128)} %get-tuple-element.49.gmid_ref, ...), custom_call_target="tpu_custom_call" | custom-call | flops 8455716864 | bytes 30000000 | tf_op jit(solution)/shard_map/close/pallas_call | solution.py:919
  203.7 1.3 convert_element_type.168
  205.5 1.7 collective-permute-start.10
  207.9 1.5 collective-permute-start.11
  209.4 1.7 collective-permute-start.12
  211.1 2.0 collective-permute-done.11
  213.8 2.3 collective-permute-done.12
  216.1 4.1 %collective-permute-done.7.col_ref = bf16[3,3,56,512]{3,2,1,0:T(8,128)(2,1)S(1)} collective-permute-done((bf16[3,3,56,512]{3,2,1,0:T(8,128)(2,1)S(1)}, bf16[3,3,56,512]{3,2,1,0:T(8,128)(2,1)S(1)}, u32[]{:S(2)}, u32[]{:S(2)}) %collective-permute-start.7) | collective-permute-done | bytes 516128 | tf_op jit(solution)/shard_map/ppermute | solution.py:542
  220.2 2.1 patch.2
  222.3 8.4 %collective-permute-done.10.col_ref = bf16[3,3,56,512]{3,2,1,0:T(8,128)(2,1)S(1)} collective-permute-done((bf16[3,3,56,512]{3,2,1,0:T(8,128)(2,1)S(1)}, bf16[3,3,56,512]{3,2,1,0:T(8,128)(2,1)S(1)}, u32[]{:S(2)}, u32[]{:S(2)}) %collective-permute-start.10) | collective-permute-done | bytes 516128 | tf_op jit(solution)/shard_map/ppermute | solution.py:542
  230.7 2.1 patch.3
  232.8 0.7 collective-permute-done.4
  233.8 1.0 fusion.13
  235.4 0.7 collective-permute-start.13
  236.2 4.0 %collective-permute-done.15 = bf16[80,1024]{1,0:T(8,128)(2,1)S(1)} collective-permute-done((bf16[80,1024]{1,0:T(8,128)(2,1)S(1)}, bf16[80,1024]{1,0:T(8,128)(2,1)S(1)}, u32[]{:S(2)}, u32[]{:S(2)}) %collective-permute-start.15) | collective-permute-done | bytes 163872 | tf_op jit(solution)/shard_map/ppermute | solution.py:542
  240.2 1.6 collective-permute-done.13
  241.8 1.1 add_convert_fusion.2
  243.6 0.8 slice.151
  244.4 0.8 pad_maximum_fusion.2
  245.3 1.2 collective-permute-start.14
  246.5 1.8 collective-permute-done.16
  249.6 1.0 collective-permute-done.14
  251.2 0.8 pad_maximum_fusion.3
  252.2 1.8 fusion.3
  (126 shorter events, 9.9 us)
Async XLA Ops:
  7.2 40.1 %all-gather.5.cloned.1.call-start = ((), (), s32[]{:S(2)}) async-start(), calls=%async_computation.2 | async-start | bytes 2359296 | tf_op jit(solution)/shard_map/all_gather | solution.py:716
  9.9 81.0 %all-gather.7.cloned.1.call-start = ((), (), s32[]{:S(2)}) async-start(), calls=%async_computation.3 | async-start | bytes 4718592 | tf_op jit(solution)/shard_map/all_gather | solution.py:722
  13.0 171.5 %reduce-scatter.5.cloned.1.call-start = ((), (), s32[]{:S(2)}) async-start(), calls=%async_computation.5 | async-start | bytes 4718592 | tf_op jit(solution)/shard_map/reduce_scatter | solution.py:879
  13.1 2.4 copy-start
  15.5 2.4 copy-start.1
  17.8 5.4 %copy-start.9 = (f32[64]{0:T(128)S(1)}, f32[64]{0:T(128)}, u32[]{:S(2)}) copy-start(f32[64]{0:T(128)} %param.19) | copy-start | bytes 772
  17.8 5.4 %copy-start.10 = (f32[64]{0:T(128)S(1)}, f32[64]{0:T(128)}, u32[]{:S(2)}) copy-start(f32[64]{0:T(128)} %param.20) | copy-start | bytes 772
  17.8 5.4 %copy-start.11 = (f32[64]{0:T(128)S(1)}, f32[64]{0:T(128)}, u32[]{:S(2)}) copy-start(f32[64]{0:T(128)} %param.22) | copy-start | bytes 772
  17.8 5.5 %copy-start.12 = (f32[64]{0:T(128)S(1)}, f32[64]{0:T(128)}, u32[]{:S(2)}) copy-start(f32[64]{0:T(128)} %param.23) | copy-start | bytes 772
  17.8 5.5 %copy-start.13 = (f32[64]{0:T(128)S(1)}, f32[64]{0:T(128)}, u32[]{:S(2)}) copy-start(f32[64]{0:T(128)} %param.26) | copy-start | bytes 772
  17.8 5.5 %copy-start.14 = (f32[64]{0:T(128)S(1)}, f32[64]{0:T(128)}, u32[]{:S(2)}) copy-start(f32[64]{0:T(128)} %param.27) | copy-start | bytes 772
  17.9 5.5 %copy-start.15 = (f32[64]{0:T(128)S(1)}, f32[64]{0:T(128)}, u32[]{:S(2)}) copy-start(f32[64]{0:T(128)} %param.28) | copy-start | bytes 772
  17.9 5.5 %copy-start.8 = (f32[256]{0:T(256)S(1)}, f32[256]{0:T(256)}, u32[]{:S(2)}) copy-start(f32[256]{0:T(256)} %param.30) | copy-start | bytes 3076
  17.9 5.5 %copy-start.16 = (f32[64]{0:T(128)S(1)}, f32[64]{0:T(128)}, u32[]{:S(2)}) copy-start(f32[64]{0:T(128)} %param.32) | copy-start | bytes 772
  17.9 5.5 %copy-start.7 = (f32[2,169]{1,0:T(2,128)S(1)}, f32[2,169]{1,0:T(2,128)}, u32[]{:S(2)}) copy-start(f32[2,169]{1,0:T(2,128)} %param.24) | copy-start | bytes 4060
  17.9 21.2 %copy-start.6 = (s32[49,49]{1,0:T(8,128)S(1)}, s32[49,49]{1,0:T(8,128)}, u32[]{:S(2)}) copy-start(s32[49,49]{1,0:T(8,128)} %param.18) | copy-start | bytes 28816
  18.6 28.3 %collective-permute-start.1 = (bf16[6,3,3,512]{3,2,1,0:T(4,128)(2,1)S(1)}, bf16[6,3,3,512]{3,2,1,0:T(4,128)(2,1)}, u32[]{:S(2)}, u32[]{:S(2)}) collective-permute-start(bf16[6,3,3,512]{3,2,1,0:T(4,128)(2,1)S(1)} %get-tuple-element.42), channel_id=1, source_target_pairs={{3,0},{2,1},{1,2},{0,3},{7,4},{6,5},{5,6},{4,7},{11,8},{10,9},{9,1... | collective-permute-start | bytes 165896 | tf_op jit(solution)/shard_map/ppermute | solution.py:552
  22.6 24.3 %collective-permute-start = (bf16[6,3,11,512]{3,2,1,0:T(8,128)(2,1)S(1)}, bf16[6,3,11,512]{3,2,1,0:T(8,128)(2,1)}, u32[]{:S(2)}, u32[]{:S(2)}) collective-permute-start(bf16[6,3,11,512]{3,2,1,0:T(8,128)(2,1)S(1)} %get-tuple-element.41), channel_id=1, source_target_pairs={{2,0},{0,2},{3,1},{1,3},{6,4},{4,6},{7,5},{5,7},{10,8},{8,10},{11,... | collective-permute-start | bytes 608264 | tf_op jit(solution)/shard_map/ppermute | solution.py:542
  23.1 24.2 %collective-permute-start.2 = (bf16[6,3,56,512]{3,2,1,0:T(8,128)(2,1)S(1)}, bf16[6,3,56,512]{3,2,1,0:T(8,128)(2,1)}, u32[]{:S(2)}, u32[]{:S(2)}) collective-permute-start(bf16[6,3,56,512]{3,2,1,0:T(8,128)(2,1)S(1)} %get-tuple-element.43), channel_id=1, source_target_pairs={{1,0},{0,1},{3,2},{2,3},{5,4},{4,5},{7,6},{6,7},{9,8},{8,9},{11,10... | collective-permute-start | bytes 3096584 | tf_op jit(solution)/shard_map/ppermute | solution.py:542
  135.7 98.1 %reduce-scatter.3.cloned.1.call-start = ((), (), s32[]{:S(2)}) async-start(), calls=%async_computation.4 | async-start | bytes 2949120 | tf_op jit(solution)/shard_map/reduce_scatter | solution.py:917
  135.7 33.2 %copy-start.4 = (f32[3,3,14,512]{3,2,1,0:T(8,128)S(1)}, f32[3,3,14,512]{3,2,1,0:T(8,128)}, u32[]{:S(2)}) copy-start(f32[3,3,14,512]{3,2,1,0:T(8,128)} %get-tuple-element.56) | copy-start | bytes 774148
  169.0 38.9 %collective-permute-start.8 = (bf16[3,3,3,512]{3,2,1,0:T(4,128)(2,1)S(1)}, bf16[3,3,3,512]{3,2,1,0:T(4,128)(2,1)S(1)}, u32[]{:S(2)}, u32[]{:S(2)}) collective-permute-start(bf16[3,3,3,512]{3,2,1,0:T(4,128)(2,1)S(1)} %slice.167), channel_id=1, source_target_pairs={{3,0},{2,1},{1,2},{0,3},{7,4},{6,5},{5,6},{4,7},{11,8},{10,9},{9,1... | collective-permute-start | bytes 82952 | tf_op jit(solution)/shard_map/ppermute | solution.py:552
  171.5 37.9 %collective-permute-start.9 = (bf16[3,3,11,512]{3,2,1,0:T(8,128)(2,1)S(1)}, bf16[3,3,11,512]{3,2,1,0:T(8,128)(2,1)S(1)}, u32[]{:S(2)}, u32[]{:S(2)}) collective-permute-start(bf16[3,3,11,512]{3,2,1,0:T(8,128)(2,1)S(1)} %bitcast.64), channel_id=1, source_target_pairs={{2,0},{0,2},{3,1},{1,3},{6,4},{4,6},{7,5},{5,7},{10,8},{8,10},{11,... | collective-permute-start | bytes 304136 | tf_op jit(solution)/shard_map/ppermute | solution.py:542
  185.7 19.9 %collective-permute-start.3 = (bf16[128,1024]{1,0:T(8,128)(2,1)S(1)}, bf16[128,1024]{1,0:T(8,128)(2,1)S(1)}, u32[]{:S(2)}, u32[]{:S(2)}) collective-permute-start(bf16[128,1024]{1,0:T(8,128)(2,1)S(1)} %get-tuple-element.72), channel_id=1, source_target_pairs={{2,0},{0,2},{3,1},{1,3},{6,4},{4,6},{7,5},{5,7},{10,8},{8,10},{11,... | collective-permute-start | bytes 786440 | tf_op jit(solution)/shard_map/ppermute | solution.py:542
  187.2 20.0 %collective-permute-start.5 = (bf16[128,1024]{1,0:T(8,128)(2,1)S(1)}, bf16[128,1024]{1,0:T(8,128)(2,1)S(1)}, u32[]{:S(2)}, u32[]{:S(2)}) collective-permute-start(bf16[128,1024]{1,0:T(8,128)(2,1)S(1)} %get-tuple-element.73), channel_id=1, source_target_pairs={{1,0},{0,1},{3,2},{2,3},{5,4},{4,5},{7,6},{6,7},{9,8},{8,9},{11,10... | collective-permute-start | bytes 786440 | tf_op jit(solution)/shard_map/ppermute | solution.py:542
  188.7 16.4 %copy-start.3 = (f32[3,3,56,512]{3,2,1,0:T(8,128)S(1)}, f32[3,3,56,512]{3,2,1,0:T(8,128)}, u32[]{:S(2)}) copy-start(f32[3,3,56,512]{3,2,1,0:T(8,128)} %get-tuple-element.55) | copy-start | bytes 3096580
  188.7 18.5 %copy-start.2 = (bf16[1,128,2048]{2,1,0:T(8,128)(2,1)S(1)}, bf16[1,128,2048]{2,1,0:T(8,128)(2,1)}, u32[]{:S(2)}) copy-start(bf16[1,128,2048]{2,1,0:T(8,128)(2,1)} %reduce-scatter.5.cloned.1.call-done) | copy-start | bytes 1572868
  203.7 4.1 %copy-start.5 = (f32[3,3,14,512]{3,2,1,0:T(8,128)S(1)}, f32[3,3,14,512]{3,2,1,0:T(8,128)}, u32[]{:S(2)}) copy-start(f32[3,3,14,512]{3,2,1,0:T(8,128)} %get-tuple-element.61) | copy-start | bytes 774148
  205.1 15.1 %collective-permute-start.7 = (bf16[3,3,56,512]{3,2,1,0:T(8,128)(2,1)S(1)}, bf16[3,3,56,512]{3,2,1,0:T(8,128)(2,1)S(1)}, u32[]{:S(2)}, u32[]{:S(2)}) collective-permute-start(bf16[3,3,56,512]{3,2,1,0:T(8,128)(2,1)S(1)} %convert_element_type.165), channel_id=1, source_target_pairs={{1,0},{0,1},{3,2},{2,3},{5,4},{4,5},{7,6},{6,7},{9,8},{8,9},{11,10... | collective-permute-start | bytes 1548296 | tf_op jit(solution)/shard_map/ppermute | solution.py:542
  205.5 25.2 %collective-permute-start.10 = (bf16[3,3,56,512]{3,2,1,0:T(8,128)(2,1)S(1)}, bf16[3,3,56,512]{3,2,1,0:T(8,128)(2,1)S(1)}, u32[]{:S(2)}, u32[]{:S(2)}) collective-permute-start(bf16[3,3,56,512]{3,2,1,0:T(8,128)(2,1)S(1)} %convert_element_type.168), channel_id=1, source_target_pairs={{1,0},{0,1},{3,2},{2,3},{5,4},{4,5},{7,6},{6,7},{9,8},{8,9},{11,10... | collective-permute-start | bytes 1548296 | tf_op jit(solution)/shard_map/ppermute | solution.py:542
  207.4 26.1 %collective-permute-start.4 = (bf16[128,1024]{1,0:T(8,128)(2,1)S(1)}, bf16[128,1024]{1,0:T(8,128)(2,1)S(1)}, u32[]{:S(2)}, u32[]{:S(2)}) collective-permute-start(bf16[128,1024]{1,0:T(8,128)(2,1)S(1)} %get-tuple-element.70), channel_id=1, source_target_pairs={{1,0},{0,1},{3,2},{2,3},{5,4},{4,5},{7,6},{6,7},{9,8},{8,9},{11,10... | collective-permute-start | bytes 786440 | tf_op jit(solution)/shard_map/ppermute | solution.py:542
  207.9 5.3 %collective-permute-start.11 = (bf16[3,3,3,512]{3,2,1,0:T(4,128)(2,1)S(1)}, bf16[3,3,3,512]{3,2,1,0:T(4,128)(2,1)S(1)}, u32[]{:S(2)}, u32[]{:S(2)}) collective-permute-start(bf16[3,3,3,512]{3,2,1,0:T(4,128)(2,1)S(1)} %slice.169), channel_id=1, source_target_pairs={{3,0},{2,1},{1,2},{0,3},{7,4},{6,5},{5,6},{4,7},{11,8},{10,9},{9,1... | collective-permute-start | bytes 82952 | tf_op jit(solution)/shard_map/ppermute | solution.py:552
  209.4 6.6 %collective-permute-start.12 = (bf16[3,3,11,512]{3,2,1,0:T(8,128)(2,1)S(1)}, bf16[3,3,11,512]{3,2,1,0:T(8,128)(2,1)S(1)}, u32[]{:S(2)}, u32[]{:S(2)}) collective-permute-start(bf16[3,3,11,512]{3,2,1,0:T(8,128)(2,1)S(1)} %bitcast.65), channel_id=1, source_target_pairs={{2,0},{0,2},{3,1},{1,3},{6,4},{4,6},{7,5},{5,7},{10,8},{8,10},{11,... | collective-permute-start | bytes 304136 | tf_op jit(solution)/shard_map/ppermute | solution.py:542
  213.2 20.4 %collective-permute-start.6 = (bf16[128,1024]{1,0:T(8,128)(2,1)S(1)}, bf16[128,1024]{1,0:T(8,128)(2,1)S(1)}, u32[]{:S(2)}, u32[]{:S(2)}) collective-permute-start(bf16[128,1024]{1,0:T(8,128)(2,1)S(1)} %get-tuple-element.71), channel_id=1, source_target_pairs={{2,0},{0,2},{3,1},{1,3},{6,4},{4,6},{7,5},{5,7},{10,8},{8,10},{11,... | collective-permute-start | bytes 786440 | tf_op jit(solution)/shard_map/ppermute | solution.py:542
  234.8 5.4 %collective-permute-start.15 = (bf16[80,1024]{1,0:T(8,128)(2,1)S(1)}, bf16[80,1024]{1,0:T(8,128)(2,1)S(1)}, u32[]{:S(2)}, u32[]{:S(2)}) collective-permute-start(bf16[80,1024]{1,0:T(8,128)(2,1)S(1)} %get-tuple-element.88), channel_id=1, source_target_pairs={{1,0},{0,1},{3,2},{2,3},{5,4},{4,5},{7,6},{6,7},{9,8},{8,9},{11,10... | collective-permute-start | bytes 491528 | tf_op jit(solution)/shard_map/ppermute | solution.py:542
  235.4 6.4 %collective-permute-start.13 = (bf16[80,1024]{1,0:T(8,128)(2,1)S(1)}, bf16[80,1024]{1,0:T(8,128)(2,1)S(1)}, u32[]{:S(2)}, u32[]{:S(2)}) collective-permute-start(bf16[80,1024]{1,0:T(8,128)(2,1)S(1)} %get-tuple-element.89), channel_id=1, source_target_pairs={{2,0},{0,2},{3,1},{1,3},{6,4},{4,6},{7,5},{5,7},{10,8},{8,10},{11,... | collective-permute-start | bytes 491528 | tf_op jit(solution)/shard_map/ppermute | solution.py:542
  242.9 5.4 %collective-permute-start.16 = (bf16[80,1024]{1,0:T(8,128)(2,1)S(1)}, bf16[80,1024]{1,0:T(8,128)(2,1)S(1)}, u32[]{:S(2)}, u32[]{:S(2)}) collective-permute-start(bf16[80,1024]{1,0:T(8,128)(2,1)S(1)} %get-tuple-element.86), channel_id=1, source_target_pairs={{2,0},{0,2},{3,1},{1,3},{6,4},{4,6},{7,5},{5,7},{10,8},{8,10},{11,... | collective-permute-start | bytes 491528 | tf_op jit(solution)/shard_map/ppermute | solution.py:542
  245.3 5.3 %collective-permute-start.14 = (bf16[80,1024]{1,0:T(8,128)(2,1)S(1)}, bf16[80,1024]{1,0:T(8,128)(2,1)S(1)}, u32[]{:S(2)}, u32[]{:S(2)}) collective-permute-start(bf16[80,1024]{1,0:T(8,128)(2,1)S(1)} %get-tuple-element.87), channel_id=1, source_target_pairs={{1,0},{0,1},{3,2},{2,3},{5,4},{4,5},{7,6},{6,7},{9,8},{8,9},{11,10... | collective-permute-start | bytes 491528 | tf_op jit(solution)/shard_map/ppermute | solution.py:542
Sparse Core Ops, SparseCore 0:
  10.2 32.1 all-gather.4
  44.6 46.2 all-gather.6
  135.8 48.7 reduce-scatter.4
  186.7 36.3 reduce-scatter.2

commit v4 on v3

--- a/solution.py
+++ b/solution.py
@@ -20,7 +20,7 @@
 BF = jnp.bfloat16
 F32 = jnp.float32
 BANDS = 4
-LINES = 16
+LINES = 8
 VMEM_LIMIT = 60 * 1024 * 1024
 
 
@@ -490,15 +490,15 @@
             pack_ref[d, 0:deep, : 3 * features] = acc_ref[own, :].astype(BF)
             pack_ref[d, 0:deep, 3 * features :] = go_ref[own, :].astype(BF)
             pack_ref[d, deep : deep + LINES, :] = jnp.zeros((LINES, 4 * features), BF)
-            for j in range(4):
+            for j in range(QL // LINES):
                 pack_ref[d, deep : deep + LINES, j * lanes : (j + 1) * lanes] = table_ref[
                     j * LINES : (j + 1) * LINES, d * lanes : (d + 1) * lanes
                 ].astype(BF)
-            at = features
+            at = 2 * features
             pack_ref[d, deep : deep + LINES, at : at + deep] = lines[:, own].astype(BF)
-            at = features + features // 2
+            at = 2 * features + features // 2
             pack_ref[d, deep : deep + LINES, at : at + deep] = sums_two_ref[:, own].astype(BF)
-            at = 2 * features
+            at = 3 * features
             even = esum_ref.shape[1] // shards
             pack_ref[d, deep : deep + LINES, at : at + even] = esum_ref[
                 :, d * even : (d + 1) * even
@@ -902,7 +902,7 @@
             pltpu.VMEM((features, 3 * features), F32),
             pltpu.VMEM((step_rows, 3 * features), F32),
             pltpu.VMEM((1, 3 * features), F32),
-            pltpu.VMEM((4 * LINES, wide), F32),
+            pltpu.VMEM((QL, wide), F32),
             pltpu.VMEM((4, WT, 256 // head_size * QL), BF),
             pltpu.VMEM((2 * BANDS, WT, features), BF),
             pltpu.VMEM((features, features), F32),
@@ -954,12 +954,12 @@
     grad_output = pack_one[:deep, 3 * features :]
     grad_joint = pack_one[:deep, : 3 * features]
     lanes = table_heads * QL
-    lines_one = pack_one[deep:, features : features + deep]
-    at = features + features // 2
+    lines_one = pack_one[deep:, 2 * features : 2 * features + deep]
+    at = 2 * features + features // 2
     lines_two = pack_one[deep:, at : at + deep]
-    grad_expand_bias = pack_one[deep, 2 * features : 2 * features + blocks * deep]
+    grad_expand_bias = pack_one[deep, 3 * features : 3 * features + blocks * deep]
     gtable = jnp.concatenate(
-        [pack_one[deep:, j * lanes : (j + 1) * lanes] for j in range(4)], axis=0
+        [pack_one[deep:, j * lanes : (j + 1) * lanes] for j in range(QL // LINES)], axis=0
     )[:WT]
     gtable = gtable.reshape(WT, table_heads, QL).transpose(1, 0, 2).reshape(table_heads, WT * QL)
     grad_position = lax.dot_general(

time: 261 us -> 261 us (level)
    unnamed x38 -> x44, local copies, waits for them, and re-layouts: 5.49 us -> 5.51 us
where the time goes in v4:
time: 261 us; the launch traced here: 260 us
  Pallas kernels  126 us (48%)
  waiting for transfers between devices  53.4 us (20%)
  starting transfers between devices  20.5 us (8%)
  blocking collectives  15 us (6%)
  between operations  14.4 us (6%)
  local copies, waits for them, and re-layouts  14.2 us (5%)
  other arithmetic  12.7 us (5%)
  matrix products  3.41 us (1%)
    pallas_call x1, Pallas kernels, body(): pl.pallas_call(mlp_kernel, grid=(images, 1), in_specs=[tile_spec, *halo_s...  44.8 us
    pallas_call x1, Pallas kernels, body(): pl.pallas_call(functools.partial(back_kernel, head_size), grid=grid, in_s...  33.1 us
    pallas_call x1, Pallas kernels, body(): pl.pallas_call(functools.partial(attend_kernel, head_size), grid=grid, in...  28.7 us
    ppermute x14, waiting for transfers between devices, shifted(): lax.ppermute(block, axis, [((i - distance) % count, i) for i in range(cou...  23.7 us
    all_gather x1, blocking collectives, body(): small = lax.all_gather(small, 'dp', axis=0, tiled=True)  15 us
    pallas_call x1, Pallas kernels, body(): pl.pallas_call(close_kernel, grid=grid, in_specs=[joint_spec, flat_spec,...  15 us
    all_gather x1, waiting for transfers between devices, body(): lax.all_gather(jnp.concatenate([expand_weight, thick], axis=0).astype(BF)...  14.9 us
    reduce_scatter x1, waiting for transfers between devices, body(): lax.psum_scatter(pack_two, 'dp', scatter_dimension=0, tiled=True)[0]  12.7 us
  transfers between devices with their start and end apart: 21, of which 12 were waited for; matrix products, arithmetic and copies ran while one was open for 7% of the time, Pallas kernels for 31%

profile of v4, /device:TPU:0, one launch (start us, length us, event | category | flops | bytes accessed | tf_op | source)
XLA Modules:
  0.0 260.0 jit_solution(10673668993224759687)
XLA Ops:
  7.2 0.9 convert.27
  8.1 1.0 convert.26
  9.2 0.7 pad_maximum_fusion.4
  10.0 1.1 convert.29
  11.1 1.1 convert_bitcast_fusion
  12.2 0.8 pad_maximum_fusion.1
  13.1 2.4 copy-done
  15.5 2.4 copy-done.1
  17.9 0.7 edge.1
  18.6 4.0 %collective-permute-start.1 = (bf16[6,3,3,512]{3,2,1,0:T(4,128)(2,1)S(1)}, bf16[6,3,3,512]{3,2,1,0:T(4,128)(2,1)}, u32[]{:S(2)}, u32[]{:S(2)}) collective-permute-start(bf16[6,3,3,512]{3,2,1,0:T(4,128)(2,1)S(1)} %get-tuple-element.42), channel_id=1, source_target_pairs={{3,0},{2,1},{1,2},{0,3},{7,4},{6,5},{5,6},{4,7},{11,8},{10,9},{9,1... | collective-permute-start | bytes 165896 | tf_op jit(solution)/shard_map/ppermute | solution.py:552
  23.9 15.0 %all-gather.1 = bf16[8,1,1152]{2,1,0:T(2,128)(2,1)S(1)} all-gather(bf16[1,1,1152]{2,1,0:T(2,128)(2,1)S(1)} %reshape.175), channel_id=2, replica_groups=mesh['dp'=8,'row'=2,'col'=2] {'dp'}, dimensions={0}, use_global_device_ids=true | all-gather | bytes 20736 | tf_op jit(solution)/shard_map/all_gather | solution.py:709
  39.8 1.6 fusion.6
  41.9 1.4 add.136
  43.3 2.2 broadcast_add_fusion.bias_ref
  46.2 0.7 reshape.171.vec_ref
  47.3 28.7 %attend.1 = (f32[2688,512]{1,0:T(8,128)}, bf16[2688,512]{1,0:T(8,128)(2,1)}, bf16[48,56,1536]{2,1,0:T(8,128)(2,1)}, bf16[48,56,1024]{2,1,0:T(8,128)(2,1)}, bf16[...) custom-call(f32[3,14,56,512]{3,2,1,0:T(8,128)} %bitcast.53, bf16[6,3,11,512]{3,2,1,0:T(8,128)(2,1)} %collective-permute-done.row_ref, ...), custom_call_target="tpu_custom_call" | custom-call | flops 8455716864 | bytes 40000000 | tf_op jit(solution)/shard_map/attend/pallas_call | solution.py:786
  76.0 14.9 %all-gather.7.cloned.1.call-done.packed_ref = bf16[8,128,2048]{2,1,0:T(8,128)(2,1)} async-done(((bf16[1,128,2048]{2,1,0:T(8,128)(2,1)}), bf16[8,128,2048]{2,1,0:T(8,128)(2,1)}) %all-gather.7.cloned.1.call-update) | async-done | bytes 4194320 | tf_op jit(solution)/shard_map/all_gather | solution.py:722
  90.9 44.8 %mlp.1 = (f32[3,14,56,512]{3,2,1,0:T(8,128)}, f32[3,3,14,512]{3,2,1,0:T(8,128)}, f32[3,3,56,512]{3,2,1,0:T(8,128)}, f32[2688,512]{1,0:T(8,128)}, bf16[8,128,2048...) custom-call(f32[3,14,56,512]{3,2,1,0:T(8,128)} %bitcast.55, ...), custom_call_target="tpu_custom_call" | custom-call | flops 33822867456 | bytes 50000000 | tf_op jit(solution)/shard_map/mlp/pallas_call | solution.py:821
  135.8 33.1 %back.1 = (bf16[2688,1536]{1,0:T(8,128)(2,1)}, bf16[8,72,2048]{2,1,0:T(8,128)(2,1)}) custom-call(bf16[2688,512]{1,0:T(8,128)(2,1)} %get-tuple-element.44.hid_ref, bf16[48,56,1536]{2,1,0:T(8,128)(2,1)} %get-tuple-element.45.qkv_ref, bf16[48,56,1024]{2,1,0:T(8,128)(2,1)} %get-tuple-element.46.prob_ref, bf16[2688,512]{1,0:T(8,128)(2,1)} %get-tuple-element.47.att_ref, ...), custom_call_target="tpu_custom_call" | custom-call | flops 25367150592 | bytes 50000000 | tf_op jit(solution)/shard_map/back/pallas_call | solution.py:882
  168.9 2.4 collective-permute-start.8
  171.9 12.7 %reduce-scatter.5.cloned.1.call-done = bf16[1,128,2048]{2,1,0:T(8,128)(2,1)} async-done(((bf16[8,128,2048]{2,1,0:T(8,128)(2,1)}), bf16[1,128,2048]{2,1,0:T(8,128)(2,1)}) %reduce-scatter.5.cloned.1.call-update) | async-done | bytes 524304 | tf_op jit(solution)/shard_map/reduce_scatter | solution.py:879
  184.6 1.1 fusion.11
  185.6 1.5 collective-permute-start.3
  187.2 1.5 collective-permute-start.5
  188.6 15.0 %close.1 = (f32[3,14,56,512]{3,2,1,0:T(8,128)}, f32[3,3,14,512]{3,2,1,0:T(8,128)}, f32[3,3,56,512]{3,2,1,0:T(8,128)}) custom-call(bf16[2688,1536]{1,0:T(8,128)(2,1)} %get-tuple-element.57.gact_ref, f32[2688,512]{1,0:T(8,128)} %get-tuple-element.58.xp_ref, f32[2688,512]{1,0:T(8,128)} %get-tuple-element.49.gmid_ref, ...), custom_call_target="tpu_custom_call" | custom-call | flops 8455716864 | bytes 30000000 | tf_op jit(solution)/shard_map/close/pallas_call | solution.py:919
  203.6 1.3 convert_element_type.168
  205.5 1.7 collective-permute-start.10
  207.8 1.5 collective-permute-start.11
  209.4 1.7 collective-permute-start.12
  211.1 2.1 collective-permute-done.11
  213.7 2.2 collective-permute-done.12
  216.0 4.1 %collective-permute-done.7.col_ref = bf16[3,3,56,512]{3,2,1,0:T(8,128)(2,1)S(1)} collective-permute-done((bf16[3,3,56,512]{3,2,1,0:T(8,128)(2,1)S(1)}, bf16[3,3,56,512]{3,2,1,0:T(8,128)(2,1)S(1)}, u32[]{:S(2)}, u32[]{:S(2)}) %collective-permute-start.7) | collective-permute-done | bytes 516128 | tf_op jit(solution)/shard_map/ppermute | solution.py:542
  220.1 2.1 patch.2
  222.2 8.4 %collective-permute-done.10.col_ref = bf16[3,3,56,512]{3,2,1,0:T(8,128)(2,1)S(1)} collective-permute-done((bf16[3,3,56,512]{3,2,1,0:T(8,128)(2,1)S(1)}, bf16[3,3,56,512]{3,2,1,0:T(8,128)(2,1)S(1)}, u32[]{:S(2)}, u32[]{:S(2)}) %collective-permute-start.10) | collective-permute-done | bytes 516128 | tf_op jit(solution)/shard_map/ppermute | solution.py:542
  230.7 2.1 patch.3
  232.8 0.7 collective-permute-done.4
  233.7 1.0 fusion.12
  235.4 0.7 collective-permute-start.13
  236.1 4.1 %collective-permute-done.15 = bf16[72,1024]{1,0:T(8,128)(2,1)S(1)} collective-permute-done((bf16[72,1024]{1,0:T(8,128)(2,1)S(1)}, bf16[72,1024]{1,0:T(8,128)(2,1)S(1)}, u32[]{:S(2)}, u32[]{:S(2)}) %collective-permute-start.15) | collective-permute-done | bytes 147488 | tf_op jit(solution)/shard_map/ppermute | solution.py:542
  240.5 1.1 add_convert_fusion.2
  241.6 1.5 collective-permute-start.14
  243.1 0.8 slice.159
  244.0 0.8 pad_maximum_fusion.2
  245.3 1.4 collective-permute-done.14
  247.9 2.0 collective-permute-done.16
  250.0 0.8 pad_maximum_fusion.3
  250.8 0.7 slice.190
  251.7 1.8 fusion.3
  (131 shorter events, 9.4 us)
Async XLA Ops:
  7.2 40.1 %all-gather.5.cloned.1.call-start = ((), (), s32[]{:S(2)}) async-start(), calls=%async_computation.2 | async-start | bytes 2359296 | tf_op jit(solution)/shard_map/all_gather | solution.py:716
  9.9 81.0 %all-gather.7.cloned.1.call-start = ((), (), s32[]{:S(2)}) async-start(), calls=%async_computation.3 | async-start | bytes 4718592 | tf_op jit(solution)/shard_map/all_gather | solution.py:722
  13.0 171.5 %reduce-scatter.5.cloned.1.call-start = ((), (), s32[]{:S(2)}) async-start(), calls=%async_computation.5 | async-start | bytes 4718592 | tf_op jit(solution)/shard_map/reduce_scatter | solution.py:879
  13.1 2.4 copy-start
  15.5 2.4 copy-start.1
  17.8 5.4 %copy-start.9 = (f32[64]{0:T(128)S(1)}, f32[64]{0:T(128)}, u32[]{:S(2)}) copy-start(f32[64]{0:T(128)} %param.19) | copy-start | bytes 772
  17.8 5.4 %copy-start.10 = (f32[64]{0:T(128)S(1)}, f32[64]{0:T(128)}, u32[]{:S(2)}) copy-start(f32[64]{0:T(128)} %param.20) | copy-start | bytes 772
  17.8 5.4 %copy-start.11 = (f32[64]{0:T(128)S(1)}, f32[64]{0:T(128)}, u32[]{:S(2)}) copy-start(f32[64]{0:T(128)} %param.22) | copy-start | bytes 772
  17.8 5.5 %copy-start.12 = (f32[64]{0:T(128)S(1)}, f32[64]{0:T(128)}, u32[]{:S(2)}) copy-start(f32[64]{0:T(128)} %param.23) | copy-start | bytes 772
  17.8 5.5 %copy-start.13 = (f32[64]{0:T(128)S(1)}, f32[64]{0:T(128)}, u32[]{:S(2)}) copy-start(f32[64]{0:T(128)} %param.26) | copy-start | bytes 772
  17.8 5.5 %copy-start.14 = (f32[64]{0:T(128)S(1)}, f32[64]{0:T(128)}, u32[]{:S(2)}) copy-start(f32[64]{0:T(128)} %param.27) | copy-start | bytes 772
  17.9 5.5 %copy-start.15 = (f32[64]{0:T(128)S(1)}, f32[64]{0:T(128)}, u32[]{:S(2)}) copy-start(f32[64]{0:T(128)} %param.28) | copy-start | bytes 772
  17.9 5.5 %copy-start.8 = (f32[256]{0:T(256)S(1)}, f32[256]{0:T(256)}, u32[]{:S(2)}) copy-start(f32[256]{0:T(256)} %param.30) | copy-start | bytes 3076
  17.9 5.5 %copy-start.16 = (f32[64]{0:T(128)S(1)}, f32[64]{0:T(128)}, u32[]{:S(2)}) copy-start(f32[64]{0:T(128)} %param.32) | copy-start | bytes 772
  17.9 5.5 %copy-start.7 = (f32[2,169]{1,0:T(2,128)S(1)}, f32[2,169]{1,0:T(2,128)}, u32[]{:S(2)}) copy-start(f32[2,169]{1,0:T(2,128)} %param.24) | copy-start | bytes 4060
  17.9 21.2 %copy-start.6 = (s32[49,49]{1,0:T(8,128)S(1)}, s32[49,49]{1,0:T(8,128)}, u32[]{:S(2)}) copy-start(s32[49,49]{1,0:T(8,128)} %param.18) | copy-start | bytes 28816
  18.6 28.3 %collective-permute-start.1 = (bf16[6,3,3,512]{3,2,1,0:T(4,128)(2,1)S(1)}, bf16[6,3,3,512]{3,2,1,0:T(4,128)(2,1)}, u32[]{:S(2)}, u32[]{:S(2)}) collective-permute-start(bf16[6,3,3,512]{3,2,1,0:T(4,128)(2,1)S(1)} %get-tuple-element.42), channel_id=1, source_target_pairs={{3,0},{2,1},{1,2},{0,3},{7,4},{6,5},{5,6},{4,7},{11,8},{10,9},{9,1... | collective-permute-start | bytes 165896 | tf_op jit(solution)/shard_map/ppermute | solution.py:552
  22.6 24.3 %collective-permute-start = (bf16[6,3,11,512]{3,2,1,0:T(8,128)(2,1)S(1)}, bf16[6,3,11,512]{3,2,1,0:T(8,128)(2,1)}, u32[]{:S(2)}, u32[]{:S(2)}) collective-permute-start(bf16[6,3,11,512]{3,2,1,0:T(8,128)(2,1)S(1)} %get-tuple-element.41), channel_id=1, source_target_pairs={{2,0},{0,2},{3,1},{1,3},{6,4},{4,6},{7,5},{5,7},{10,8},{8,10},{11,... | collective-permute-start | bytes 608264 | tf_op jit(solution)/shard_map/ppermute | solution.py:542
  23.1 24.2 %collective-permute-start.2 = (bf16[6,3,56,512]{3,2,1,0:T(8,128)(2,1)S(1)}, bf16[6,3,56,512]{3,2,1,0:T(8,128)(2,1)}, u32[]{:S(2)}, u32[]{:S(2)}) collective-permute-start(bf16[6,3,56,512]{3,2,1,0:T(8,128)(2,1)S(1)} %get-tuple-element.43), channel_id=1, source_target_pairs={{1,0},{0,1},{3,2},{2,3},{5,4},{4,5},{7,6},{6,7},{9,8},{8,9},{11,10... | collective-permute-start | bytes 3096584 | tf_op jit(solution)/shard_map/ppermute | solution.py:542
  135.7 98.0 %reduce-scatter.3.cloned.1.call-start = ((), (), s32[]{:S(2)}) async-start(), calls=%async_computation.4 | async-start | bytes 2654208 | tf_op jit(solution)/shard_map/reduce_scatter | solution.py:917
  135.7 33.1 %copy-start.4 = (f32[3,3,14,512]{3,2,1,0:T(8,128)S(1)}, f32[3,3,14,512]{3,2,1,0:T(8,128)}, u32[]{:S(2)}) copy-start(f32[3,3,14,512]{3,2,1,0:T(8,128)} %get-tuple-element.56) | copy-start | bytes 774148
  168.9 38.9 %collective-permute-start.8 = (bf16[3,3,3,512]{3,2,1,0:T(4,128)(2,1)S(1)}, bf16[3,3,3,512]{3,2,1,0:T(4,128)(2,1)S(1)}, u32[]{:S(2)}, u32[]{:S(2)}) collective-permute-start(bf16[3,3,3,512]{3,2,1,0:T(4,128)(2,1)S(1)} %slice.175), channel_id=1, source_target_pairs={{3,0},{2,1},{1,2},{0,3},{7,4},{6,5},{5,6},{4,7},{11,8},{10,9},{9,1... | collective-permute-start | bytes 82952 | tf_op jit(solution)/shard_map/ppermute | solution.py:552
  171.3 38.0 %collective-permute-start.9 = (bf16[3,3,11,512]{3,2,1,0:T(8,128)(2,1)S(1)}, bf16[3,3,11,512]{3,2,1,0:T(8,128)(2,1)S(1)}, u32[]{:S(2)}, u32[]{:S(2)}) collective-permute-start(bf16[3,3,11,512]{3,2,1,0:T(8,128)(2,1)S(1)} %bitcast.64), channel_id=1, source_target_pairs={{2,0},{0,2},{3,1},{1,3},{6,4},{4,6},{7,5},{5,7},{10,8},{8,10},{11,... | collective-permute-start | bytes 304136 | tf_op jit(solution)/shard_map/ppermute | solution.py:542
  185.6 19.8 %collective-permute-start.3 = (bf16[128,1024]{1,0:T(8,128)(2,1)S(1)}, bf16[128,1024]{1,0:T(8,128)(2,1)S(1)}, u32[]{:S(2)}, u32[]{:S(2)}) collective-permute-start(bf16[128,1024]{1,0:T(8,128)(2,1)S(1)} %get-tuple-element.72), channel_id=1, source_target_pairs={{2,0},{0,2},{3,1},{1,3},{6,4},{4,6},{7,5},{5,7},{10,8},{8,10},{11,... | collective-permute-start | bytes 786440 | tf_op jit(solution)/shard_map/ppermute | solution.py:542
  187.2 20.0 %collective-permute-start.5 = (bf16[128,1024]{1,0:T(8,128)(2,1)S(1)}, bf16[128,1024]{1,0:T(8,128)(2,1)S(1)}, u32[]{:S(2)}, u32[]{:S(2)}) collective-permute-start(bf16[128,1024]{1,0:T(8,128)(2,1)S(1)} %get-tuple-element.73), channel_id=1, source_target_pairs={{1,0},{0,1},{3,2},{2,3},{5,4},{4,5},{7,6},{6,7},{9,8},{8,9},{11,10... | collective-permute-start | bytes 786440 | tf_op jit(solution)/shard_map/ppermute | solution.py:542
  188.6 16.3 %copy-start.3 = (f32[3,3,56,512]{3,2,1,0:T(8,128)S(1)}, f32[3,3,56,512]{3,2,1,0:T(8,128)}, u32[]{:S(2)}) copy-start(f32[3,3,56,512]{3,2,1,0:T(8,128)} %get-tuple-element.55) | copy-start | bytes 3096580
  188.6 18.5 %copy-start.2 = (bf16[1,128,2048]{2,1,0:T(8,128)(2,1)S(1)}, bf16[1,128,2048]{2,1,0:T(8,128)(2,1)}, u32[]{:S(2)}) copy-start(bf16[1,128,2048]{2,1,0:T(8,128)(2,1)} %reduce-scatter.5.cloned.1.call-done) | copy-start | bytes 1572868
  203.6 4.1 %copy-start.5 = (f32[3,3,14,512]{3,2,1,0:T(8,128)S(1)}, f32[3,3,14,512]{3,2,1,0:T(8,128)}, u32[]{:S(2)}) copy-start(f32[3,3,14,512]{3,2,1,0:T(8,128)} %get-tuple-element.61) | copy-start | bytes 774148
  205.0 15.1 %collective-permute-start.7 = (bf16[3,3,56,512]{3,2,1,0:T(8,128)(2,1)S(1)}, bf16[3,3,56,512]{3,2,1,0:T(8,128)(2,1)S(1)}, u32[]{:S(2)}, u32[]{:S(2)}) collective-permute-start(bf16[3,3,56,512]{3,2,1,0:T(8,128)(2,1)S(1)} %convert_element_type.165), channel_id=1, source_target_pairs={{1,0},{0,1},{3,2},{2,3},{5,4},{4,5},{7,6},{6,7},{9,8},{8,9},{11,10... | collective-permute-start | bytes 1548296 | tf_op jit(solution)/shard_map/ppermute | solution.py:542
  205.5 25.2 %collective-permute-start.10 = (bf16[3,3,56,512]{3,2,1,0:T(8,128)(2,1)S(1)}, bf16[3,3,56,512]{3,2,1,0:T(8,128)(2,1)S(1)}, u32[]{:S(2)}, u32[]{:S(2)}) collective-permute-start(bf16[3,3,56,512]{3,2,1,0:T(8,128)(2,1)S(1)} %convert_element_type.168), channel_id=1, source_target_pairs={{1,0},{0,1},{3,2},{2,3},{5,4},{4,5},{7,6},{6,7},{9,8},{8,9},{11,10... | collective-permute-start | bytes 1548296 | tf_op jit(solution)/shard_map/ppermute | solution.py:542
  207.3 26.1 %collective-permute-start.4 = (bf16[128,1024]{1,0:T(8,128)(2,1)S(1)}, bf16[128,1024]{1,0:T(8,128)(2,1)S(1)}, u32[]{:S(2)}, u32[]{:S(2)}) collective-permute-start(bf16[128,1024]{1,0:T(8,128)(2,1)S(1)} %get-tuple-element.70), channel_id=1, source_target_pairs={{1,0},{0,1},{3,2},{2,3},{5,4},{4,5},{7,6},{6,7},{9,8},{8,9},{11,10... | collective-permute-start | bytes 786440 | tf_op jit(solution)/shard_map/ppermute | solution.py:542
  207.8 5.3 %collective-permute-start.11 = (bf16[3,3,3,512]{3,2,1,0:T(4,128)(2,1)S(1)}, bf16[3,3,3,512]{3,2,1,0:T(4,128)(2,1)S(1)}, u32[]{:S(2)}, u32[]{:S(2)}) collective-permute-start(bf16[3,3,3,512]{3,2,1,0:T(4,128)(2,1)S(1)} %slice.177), channel_id=1, source_target_pairs={{3,0},{2,1},{1,2},{0,3},{7,4},{6,5},{5,6},{4,7},{11,8},{10,9},{9,1... | collective-permute-start | bytes 82952 | tf_op jit(solution)/shard_map/ppermute | solution.py:552
  209.4 6.6 %collective-permute-start.12 = (bf16[3,3,11,512]{3,2,1,0:T(8,128)(2,1)S(1)}, bf16[3,3,11,512]{3,2,1,0:T(8,128)(2,1)S(1)}, u32[]{:S(2)}, u32[]{:S(2)}) collective-permute-start(bf16[3,3,11,512]{3,2,1,0:T(8,128)(2,1)S(1)} %bitcast.65), channel_id=1, source_target_pairs={{2,0},{0,2},{3,1},{1,3},{6,4},{4,6},{7,5},{5,7},{10,8},{8,10},{11,... | collective-permute-start | bytes 304136 | tf_op jit(solution)/shard_map/ppermute | solution.py:542
  213.1 20.4 %collective-permute-start.6 = (bf16[128,1024]{1,0:T(8,128)(2,1)S(1)}, bf16[128,1024]{1,0:T(8,128)(2,1)S(1)}, u32[]{:S(2)}, u32[]{:S(2)}) collective-permute-start(bf16[128,1024]{1,0:T(8,128)(2,1)S(1)} %get-tuple-element.71), channel_id=1, source_target_pairs={{2,0},{0,2},{3,1},{1,3},{6,4},{4,6},{7,5},{5,7},{10,8},{8,10},{11,... | collective-permute-start | bytes 786440 | tf_op jit(solution)/shard_map/ppermute | solution.py:542
  234.7 5.5 %collective-permute-start.15 = (bf16[72,1024]{1,0:T(8,128)(2,1)S(1)}, bf16[72,1024]{1,0:T(8,128)(2,1)S(1)}, u32[]{:S(2)}, u32[]{:S(2)}) collective-permute-start(bf16[72,1024]{1,0:T(8,128)(2,1)S(1)} %get-tuple-element.84), channel_id=1, source_target_pairs={{2,0},{0,2},{3,1},{1,3},{6,4},{4,6},{7,5},{5,7},{10,8},{8,10},{11,... | collective-permute-start | bytes 442376 | tf_op jit(solution)/shard_map/ppermute | solution.py:542
  235.4 5.1 %collective-permute-start.13 = (bf16[72,1024]{1,0:T(8,128)(2,1)S(1)}, bf16[72,1024]{1,0:T(8,128)(2,1)S(1)}, u32[]{:S(2)}, u32[]{:S(2)}) collective-permute-start(bf16[72,1024]{1,0:T(8,128)(2,1)S(1)} %get-tuple-element.85), channel_id=1, source_target_pairs={{1,0},{0,1},{3,2},{2,3},{5,4},{4,5},{7,6},{6,7},{9,8},{8,9},{11,10... | collective-permute-start | bytes 442376 | tf_op jit(solution)/shard_map/ppermute | solution.py:542
  241.6 5.2 %collective-permute-start.14 = (bf16[72,1024]{1,0:T(8,128)(2,1)S(1)}, bf16[72,1024]{1,0:T(8,128)(2,1)S(1)}, u32[]{:S(2)}, u32[]{:S(2)}) collective-permute-start(bf16[72,1024]{1,0:T(8,128)(2,1)S(1)} %get-tuple-element.83), channel_id=1, source_target_pairs={{2,0},{0,2},{3,1},{1,3},{6,4},{4,6},{7,5},{5,7},{10,8},{8,10},{11,... | collective-permute-start | bytes 442376 | tf_op jit(solution)/shard_map/ppermute | solution.py:542
  244.8 5.1 %collective-permute-start.16 = (bf16[72,1024]{1,0:T(8,128)(2,1)S(1)}, bf16[72,1024]{1,0:T(8,128)(2,1)S(1)}, u32[]{:S(2)}, u32[]{:S(2)}) collective-permute-start(bf16[72,1024]{1,0:T(8,128)(2,1)S(1)} %get-tuple-element.82), channel_id=1, source_target_pairs={{1,0},{0,1},{3,2},{2,3},{5,4},{4,5},{7,6},{6,7},{9,8},{8,9},{11,10... | collective-permute-start | bytes 442376 | tf_op jit(solution)/shard_map/ppermute | solution.py:542
Sparse Core Ops, SparseCore 0:
  10.2 32.1 all-gather.4
  44.6 46.2 all-gather.6
  135.8 48.6 reduce-scatter.4
  186.7 35.5 reduce-scatter.2
